TPU v7x, 32 devices: a whole 2x2x4 slice. The times are simulated.
32 devices in a mesh: dp: 4 (over y, core), ctx: 8 (over z, x).
Axes of the slice: x: 2, y: 2, z: 4, core: 2. Of those that a mesh axis runs over, the one named last changes fastest.
Arguments:
- tokens_in: bfloat16 [4, 1024, 1024], P('dp', 'ctx'), may hold values from -6 to 6
- upstream: float32 [4, 1024, 1024], P('dp', 'ctx'), may hold values from -6 to 6
- query_weight: float32 [1024, 768], P(('dp', 'ctx')), may hold values from -0.1875 to 0.1875
- key_weight: float32 [1024, 768], P(('dp', 'ctx')), may hold values from -0.1875 to 0.1875
- value_weight: float32 [1024, 1536], P(('dp', 'ctx')), may hold values from -0.1875 to 0.1875
- gate_weight: float32 [1024, 1536], P(('dp', 'ctx')), may hold values from -0.1875 to 0.1875
- output_weight: float32 [1024, 1536], P(('dp', 'ctx')), may hold values from -0.15625 to 0.15625
- swiglu_gate: float32 [1024, 2816], P(('dp', 'ctx')), may hold values from -0.1875 to 0.1875
- swiglu_up: float32 [1024, 2816], P(('dp', 'ctx')), may hold values from -0.1875 to 0.1875
- swiglu_down: float32 [1024, 2816], P(('dp', 'ctx')), may hold values from -0.109375 to 0.109375
- query_moment: float32 [1024, 768], P(('dp', 'ctx'))
- key_moment: float32 [1024, 768], P(('dp', 'ctx'))
- value_moment: float32 [1024, 1536], P(('dp', 'ctx'))
- gate_moment: float32 [1024, 1536], P(('dp', 'ctx'))
- output_moment: float32 [1024, 1536], P(('dp', 'ctx'))
- swiglu_gate_moment: float32 [1024, 2816], P(('dp', 'ctx'))
- swiglu_up_moment: float32 [1024, 2816], P(('dp', 'ctx'))
- swiglu_down_moment: float32 [1024, 2816], P(('dp', 'ctx'))
- small_params: float32 [26892], replicated, may hold values from -8.5 to 1.5
- small_moment: float32 [26892], replicated, may hold values from -48 to 48
Outputs:
- block_out: float32 [4, 1024, 1024], P('dp', 'ctx')
- input_grad: float32 [4, 1024, 1024], P('dp', 'ctx')
- query_weight_grad: float32 [1024, 768], P(('dp', 'ctx'))
- key_weight_grad: float32 [1024, 768], P(('dp', 'ctx'))
- value_weight_grad: float32 [1024, 1536], P(('dp', 'ctx'))
- gate_weight_grad: float32 [1024, 1536], P(('dp', 'ctx'))
- output_weight_grad: float32 [1024, 1536], P(('dp', 'ctx'))
- swiglu_gate_grad: float32 [1024, 2816], P(('dp', 'ctx'))
- swiglu_up_grad: float32 [1024, 2816], P(('dp', 'ctx'))
- swiglu_down_grad: float32 [1024, 2816], P(('dp', 'ctx'))
- query_weight_new: float32 [1024, 768], P(('dp', 'ctx'))
- key_weight_new: float32 [1024, 768], P(('dp', 'ctx'))
- value_weight_new: float32 [1024, 1536], P(('dp', 'ctx'))
- gate_weight_new: float32 [1024, 1536], P(('dp', 'ctx'))
- output_weight_new: float32 [1024, 1536], P(('dp', 'ctx'))
- swiglu_gate_new: float32 [1024, 2816], P(('dp', 'ctx'))
- swiglu_up_new: float32 [1024, 2816], P(('dp', 'ctx'))
- swiglu_down_new: float32 [1024, 2816], P(('dp', 'ctx'))
- query_moment_new: float32 [1024, 768], P(('dp', 'ctx'))
- key_moment_new: float32 [1024, 768], P(('dp', 'ctx'))
- value_moment_new: float32 [1024, 1536], P(('dp', 'ctx'))
- gate_moment_new: float32 [1024, 1536], P(('dp', 'ctx'))
- output_moment_new: float32 [1024, 1536], P(('dp', 'ctx'))
- swiglu_gate_moment_new: float32 [1024, 2816], P(('dp', 'ctx'))
- swiglu_up_moment_new: float32 [1024, 2816], P(('dp', 'ctx'))
- swiglu_down_moment_new: float32 [1024, 2816], P(('dp', 'ctx'))
- small_grad: float32 [26892], replicated
- small_new: float32 [26892], replicated
- small_moment_new: float32 [26892], replicated
- moment_norms: float32 [8], replicated
All inputs are finite; a program needn't handle non-finite values.
Results may differ from a plain program's by a relative error of at most 0.018.
Values may be sent and summed in bfloat16 or wider, within the bound.
No kernel may reach another device: no remote copies, remote signals or barrier semaphores. Data moves between devices by JAX's collectives and lax.ppermute only.
A program may use at most 320 MiB of HBM per device.

v0:
```python
import math

import jax
import jax.numpy as jnp
from jax import lax
from jax.sharding import PartitionSpec as P

D = 1024
H = 6
DK = 128
DV = 256
CONV = 4
GROUP = 64
NS_STEPS = 3
KD = 768
VD = 1536
QKV = 3072
PADW = 2816


highest_precision = lax.Precision.HIGHEST
eps_norm = 1e-05
eps_unit = 1e-06
eps_muon = 1e-07
moment_rate = 0.95
matrix_rate = 0.3
small_rate = 0.002
poly_one = 3.4445
poly_two = -4.775
poly_three = 2.0315


def passed_along(value, axis, steps):
    count = lax.axis_size(axis)
    first, last = (max(0, -steps), min(count, count - steps))
    return lax.ppermute(value, axis, [(source, source + steps) for source in range(first, last)])


def prefix(array, axis, combine, identity):
    devices, mine = (lax.axis_size(axis), lax.axis_index(axis))
    everything = jax.tree.map(
        lambda part, kind: lax.all_gather(part.astype(kind), axis),
        array,
        (jnp.bfloat16, jnp.bfloat16),
    )
    start = jax.tree.map(
        lambda part, zero: jnp.broadcast_to(jnp.asarray(zero, part.dtype), part.shape),
        array,
        identity,
    )

    def prefix_turn(k, before):
        reached = k < mine
        new = combine(
            before, jax.tree.map(lambda part, own: part[k].astype(own.dtype), everything, array)
        )
        return jax.tree.map(lambda a, b: jnp.where(reached, a, b), new, before)

    return lax.fori_loop(0, devices, prefix_turn, start)


def carried_in(array, axis, combine, identity):
    devices, mine = (lax.axis_size(axis), lax.axis_index(axis))
    everything = jax.tree.map(
        lambda part, kind: lax.all_gather(part.astype(kind), axis),
        array,
        jax.tree.map(lambda a: jnp.bfloat16 if a.dtype == jnp.float32 else a.dtype, array),
    )
    start = jax.tree.map(
        lambda part, zero: jnp.broadcast_to(jnp.asarray(zero, part.dtype), part.shape),
        array,
        identity,
    )

    def carried_turn(k, before):
        at = devices - 1 - k
        reached = at > mine
        new = combine(
            before, jax.tree.map(lambda part, own: part[at].astype(own.dtype), everything, array)
        )
        return jax.tree.map(lambda a, b: jnp.where(reached, a, b), new, before)

    return lax.fori_loop(0, devices, carried_turn, start)


def shortened(array):
    return jax.tree.map(lambda a: a.astype(jnp.bfloat16) if a.dtype == jnp.float32 else a, array)


def matmul(left, right):
    return jnp.dot(left, right, preferred_element_type=jnp.float32)


def times_transposed(left, right):
    return lax.dot_general(
        left, right, (((1,), (1,)), ((), ())), preferred_element_type=jnp.float32
    )


def transposed_times(left, right):
    return lax.dot_general(
        left, right, (((0,), (0,)), ((), ())), preferred_element_type=jnp.float32
    )


def root_norm(values, gain):
    return values * lax.rsqrt(jnp.mean(values * values, axis=-1, keepdims=True) + eps_norm) * gain


def unit_rows(values):
    return values * lax.rsqrt(jnp.sum(values * values, axis=-1, keepdims=True) + eps_unit)


def unpack_small(packed):
    lengths = [D, D, DV, CONV * QKV, H, H, D * 2 * H]
    pieces = []
    offset = 0
    for length in lengths:
        pieces.append(packed[offset : offset + length])
        offset = offset + length
    return (
        pieces[0],
        pieces[1],
        pieces[2],
        pieces[3].reshape(CONV, QKV),
        pieces[4],
        pieces[5],
        pieces[6].reshape(D, 2 * H),
    )


def pack_small(members):
    return jnp.concatenate([member.reshape(-1) for member in members])


def conv_silu(extended, conv_taps):
    kernel_size = conv_taps.shape[0]
    rows_out = extended.shape[0] - kernel_size + 1
    summed = jnp.zeros((rows_out, extended.shape[1]), jnp.float32)
    for offset in range(kernel_size):
        summed = summed + conv_taps[offset] * extended[offset : offset + rows_out]
    return jax.nn.silu(summed)


def mixer_inputs(extended, route_pre, conv_taps, decay_log, decay_bias):
    conv_out = conv_silu(extended, conv_taps)
    rows_now = conv_out.shape[0]
    queries = unit_rows(conv_out[:, :KD].reshape(rows_now, H, DK)) * DK ** (-0.5)
    keys_all = unit_rows(conv_out[:, KD : 2 * KD].reshape(rows_now, H, DK))
    values = conv_out[:, 2 * KD :].reshape(rows_now, H, DV)
    betas = jax.nn.sigmoid(route_pre[:, :H])
    log_decay = -jnp.exp(decay_log) * jax.nn.softplus(route_pre[:, H:] + decay_bias)
    return (queries, keys_all, values, betas, log_decay)


def solve_unit(matrix, target):
    return jax.scipy.linalg.solve_triangular(matrix, target, lower=True, unit_diagonal=True)


def group_terms(queries, keys_all, values, betas, log_decay):
    head_query = jnp.transpose(queries, (1, 0, 2))
    key_head = jnp.transpose(keys_all, (1, 0, 2))
    value_head = jnp.transpose(values, (1, 0, 2))
    beta_head = jnp.transpose(betas)
    cumulative = jnp.cumsum(jnp.transpose(log_decay), axis=1)
    positions = jnp.arange(cumulative.shape[1])
    inclusive = positions[:, None] >= positions[None, :]
    strictly = positions[:, None] > positions[None, :]
    differ = cumulative[:, :, None] - cumulative[:, None, :]
    within = jnp.where(inclusive, jnp.exp(jnp.where(inclusive, differ, 0.0)), 0.0)
    key_key = jnp.einsum("htd,hsd->hts", key_head, key_head, precision=highest_precision)
    lower_part = jnp.where(strictly, beta_head[:, :, None] * within * key_key, 0.0)
    growth_factor = jnp.exp(cumulative)
    system = jnp.eye(cumulative.shape[1], dtype=jnp.float32)[None] + lower_part
    right_keys = (beta_head * growth_factor)[:, :, None] * key_head
    right_values = beta_head[:, :, None] * value_head
    triangular_keys = jax.vmap(solve_unit)(system, right_keys)
    triangular_values = jax.vmap(solve_unit)(system, right_values)
    attend = within * jnp.einsum("htd,hsd->hts", head_query, key_head, precision=highest_precision)
    tail_decay = jnp.exp(cumulative[:, -1:] - cumulative)
    beta_scaled_keys = key_head * tail_decay[:, :, None]
    identity = jnp.eye(DK, dtype=jnp.float32)
    transition = growth_factor[:, -1][:, None, None] * identity[None] - jnp.einsum(
        "hck,hcj->hkj", beta_scaled_keys, triangular_keys, precision=highest_precision
    )
    shifted_state = jnp.einsum(
        "aom,aos->ams", beta_scaled_keys, triangular_values, precision=highest_precision
    )
    return (
        head_query,
        growth_factor,
        attend,
        triangular_keys,
        triangular_values,
        transition,
        shifted_state,
    )


def group_all(queries, keys_all, values, betas, log_decay):
    blocks = queries.shape[0] // GROUP

    def split_blocks(member):
        return member.reshape((blocks, GROUP) + member.shape[1:])

    return jax.vmap(group_terms)(
        split_blocks(queries),
        split_blocks(keys_all),
        split_blocks(values),
        split_blocks(betas),
        split_blocks(log_decay),
    )


def apply_groups(terms, state_in):

    def advance(carry_state, group_term):
        (
            head_query,
            growth_factor,
            attend,
            triangular_keys,
            triangular_values,
            transition,
            shifted_state,
        ) = group_term
        pseudo_value = triangular_values - jnp.einsum(
            "uqb,ubi->uqi", triangular_keys, carry_state, precision=highest_precision
        )
        output_rows = growth_factor[:, :, None] * jnp.einsum(
            "uqb,ubi->uqi", head_query, carry_state, precision=highest_precision
        )
        output_rows = output_rows + jnp.einsum(
            "hts,hsv->htv", attend, pseudo_value, precision=highest_precision
        )
        following = (
            jnp.einsum("hij,hjv->hiv", transition, carry_state, precision=highest_precision)
            + shifted_state
        )
        return (following, output_rows)

    final_state, stacked = lax.scan(advance, state_in, terms)
    output_rows = jnp.transpose(stacked, (0, 2, 1, 3)).reshape(-1, H, DV)
    return (output_rows, final_state)


def gate_outputs(output_rows, gate_pre, head_gain):
    normed = (
        output_rows
        * lax.rsqrt(jnp.mean(output_rows * output_rows, axis=-1, keepdims=True) + eps_norm)
        * head_gain
    )
    gated = normed * jax.nn.silu(gate_pre.reshape(output_rows.shape))
    return gated.reshape(output_rows.shape[0], VD)


def mixer_core(
    extended, route_pre, gate_pre, conv_taps, decay_log, decay_bias, head_gain, state_in
):
    inputs = mixer_inputs(extended, route_pre, conv_taps, decay_log, decay_bias)
    terms = group_all(*inputs)
    output_rows, final_state = apply_groups(terms, state_in)
    return (gate_outputs(output_rows, gate_pre, head_gain), final_state)


def compose_pair(earlier, later):
    trans_early, offset_early = earlier
    trans_late, offset_late = later
    joined_trans = jnp.einsum("hij,hjk->hik", trans_late, trans_early, precision=highest_precision)
    joined_offset = (
        jnp.einsum("hij,hjv->hiv", trans_late, offset_early, precision=highest_precision)
        + offset_late
    )
    return (joined_trans, joined_offset)


def identity_pair():
    return (
        jnp.broadcast_to(jnp.eye(DK, dtype=jnp.float32), (H, DK, DK)),
        jnp.zeros((H, DK, DV), jnp.float32),
    )


def compose_device(terms):

    def step_map(carry_state, pair):
        return (compose_pair(carry_state, pair), None)

    result, unused = lax.scan(step_map, identity_pair(), (terms[5], terms[6]))
    return result


def local(
    tokens_in,
    upstream,
    query_weight,
    key_weight,
    value_weight,
    gate_weight,
    output_weight,
    swiglu_gate,
    swiglu_up,
    swiglu_down,
    query_moment,
    key_moment,
    value_moment,
    gate_moment,
    output_moment,
    swiglu_gate_moment,
    swiglu_up_moment,
    swiglu_down_moment,
    small_params,
    small_moment,
):
    weights_in = (
        query_weight,
        key_weight,
        value_weight,
        gate_weight,
        output_weight,
        swiglu_gate,
        swiglu_up,
        swiglu_down,
    )
    moments_in = (
        query_moment,
        key_moment,
        value_moment,
        gate_moment,
        output_moment,
        swiglu_gate_moment,
        swiglu_up_moment,
        swiglu_down_moment,
    )
    gain_one, gain_two, head_gain, conv_taps, decay_log, decay_bias, route_weight = unpack_small(
        small_params
    )
    route_low = route_weight.astype(jnp.bfloat16)
    rim_rows = CONV - 1
    query_low = query_weight.astype(jnp.bfloat16)
    key_low = key_weight.astype(jnp.bfloat16)
    value_low = value_weight.astype(jnp.bfloat16)
    gate_low = gate_weight.astype(jnp.bfloat16)
    output_low = output_weight.astype(jnp.bfloat16)
    swiglu_gate_low = swiglu_gate.astype(jnp.bfloat16)
    swiglu_up_low = swiglu_up.astype(jnp.bfloat16)
    swiglu_down_low = swiglu_down.astype(jnp.bfloat16)
    gathered = (
        lax.all_gather(query_low, ("dp", "ctx"), axis=0, tiled=True),
        lax.all_gather(key_low, ("dp", "ctx"), axis=0, tiled=True),
        lax.all_gather(value_low, ("dp", "ctx"), axis=0, tiled=True),
        lax.all_gather(gate_low, ("dp", "ctx"), axis=0, tiled=True),
        lax.all_gather(output_low, ("dp", "ctx"), axis=0, tiled=True),
        lax.all_gather(swiglu_gate_low, ("dp", "ctx"), axis=0, tiled=True),
        lax.all_gather(swiglu_up_low, ("dp", "ctx"), axis=0, tiled=True),
        lax.all_gather(swiglu_down_low, ("dp", "ctx"), axis=0, tiled=True),
    )
    (
        query_full,
        key_full,
        value_full,
        gate_full,
        output_full,
        swiglu_gate_full,
        swiglu_up_full,
        swiglu_down_full,
    ) = gathered
    inputs_full = tokens_in[0].astype(jnp.float32)
    normed_one, norm_one_back = jax.vjp(root_norm, inputs_full, gain_one)
    normed_one_low = normed_one.astype(jnp.bfloat16)
    pre_proj = jnp.concatenate(
        [
            matmul(normed_one_low, query_full),
            matmul(normed_one_low, key_full),
            matmul(normed_one_low, value_full),
        ],
        axis=1,
    )
    gate_pre = matmul(normed_one_low, gate_full)
    route_pre = matmul(normed_one_low, route_low)
    prior_rim = passed_along(
        pre_proj[pre_proj.shape[0] - rim_rows :].astype(jnp.bfloat16), "ctx", 1
    ).astype(jnp.float32)
    extended = jnp.concatenate([prior_rim, pre_proj], axis=0)
    terms = group_all(*mixer_inputs(extended, route_pre, conv_taps, decay_log, decay_bias))
    device_trans, device_offset = compose_device(terms)
    prefix_trans, state_in = prefix(
        (device_trans, device_offset), "ctx", compose_pair, identity_pair()
    )
    output_rows, state_out = apply_groups(terms, state_in)
    mixed = gate_outputs(output_rows, gate_pre, head_gain)
    mixed_low = mixed.astype(jnp.bfloat16)
    residual_one = inputs_full + times_transposed(mixed_low, output_full)
    normed_two, norm_two_back = jax.vjp(root_norm, residual_one, gain_two)
    normed_two_low = normed_two.astype(jnp.bfloat16)
    gate_act = matmul(normed_two_low, swiglu_gate_full)
    up_act = matmul(normed_two_low, swiglu_up_full)
    middle = (jax.nn.silu(gate_act) * up_act).astype(jnp.bfloat16)
    block_out = residual_one + times_transposed(middle, swiglu_down_full)
    again = (
        lax.all_gather(query_low, ("dp", "ctx"), axis=0, tiled=True),
        lax.all_gather(key_low, ("dp", "ctx"), axis=0, tiled=True),
        lax.all_gather(value_low, ("dp", "ctx"), axis=0, tiled=True),
        lax.all_gather(gate_low, ("dp", "ctx"), axis=0, tiled=True),
        lax.all_gather(output_low, ("dp", "ctx"), axis=0, tiled=True),
        lax.all_gather(swiglu_gate_low, ("dp", "ctx"), axis=0, tiled=True),
        lax.all_gather(swiglu_up_low, ("dp", "ctx"), axis=0, tiled=True),
        lax.all_gather(swiglu_down_low, ("dp", "ctx"), axis=0, tiled=True),
    )
    (
        query_back,
        key_back,
        value_back,
        gate_back,
        output_back,
        swiglu_gate_back,
        swiglu_up_back,
        swiglu_down_back,
    ) = again
    upstream_full = upstream[0]
    upstream_low = upstream_full.astype(jnp.bfloat16)
    grad_middle = matmul(upstream_low, swiglu_down_back)
    sigma = jax.nn.sigmoid(gate_act)
    grad_gate = (grad_middle * up_act * sigma * (1.0 + gate_act * (1.0 - sigma))).astype(
        jnp.bfloat16
    )
    grad_up = (grad_middle * gate_act * sigma).astype(jnp.bfloat16)
    grad_normed_two = times_transposed(grad_gate, swiglu_gate_back) + times_transposed(
        grad_up, swiglu_up_back
    )
    grad_residual_norm, grad_gain_two = norm_two_back(grad_normed_two)
    grad_residual = upstream_full + grad_residual_norm
    grad_residual_low = grad_residual.astype(jnp.bfloat16)
    grad_mixed = matmul(grad_residual_low, output_back)

    def outputs_from_state(state_now):
        outputs_now, unused_state = apply_groups(terms, state_now)
        return gate_outputs(outputs_now, gate_pre, head_gain)

    unused_mixed, state_back = jax.vjp(outputs_from_state, state_in)
    local_state_grad = state_back(grad_mixed)[0]
    trans_flip = jnp.swapaxes(device_trans, 1, 2)
    suffix_trans, state_out_grad = carried_in(
        (trans_flip, local_state_grad), "ctx", compose_pair, identity_pair()
    )
    primal_out, mixer_back = jax.vjp(
        mixer_core,
        extended,
        route_pre,
        gate_pre,
        conv_taps,
        decay_log,
        decay_bias,
        head_gain,
        state_in,
    )
    mixer_total = mixer_back((grad_mixed, state_out_grad))
    (
        grad_extended,
        grad_route_pre,
        grad_gate_pre,
        grad_conv_taps,
        grad_decay_log,
        grad_decay_bias,
        grad_head_gain,
        unused_grad,
    ) = mixer_total
    back_rim = passed_along(shortened(grad_extended[:rim_rows]), "ctx", -1)
    grad_pre = grad_extended[rim_rows:]
    split_row = grad_pre.shape[0] - rim_rows
    grad_pre = jnp.concatenate([grad_pre[:split_row], grad_pre[split_row:] + back_rim], axis=0)
    grad_pre_low = grad_pre.astype(jnp.bfloat16)
    grad_gate_pre_low = grad_gate_pre.astype(jnp.bfloat16)
    grad_route_low = grad_route_pre.astype(jnp.bfloat16)
    right_parts = (
        grad_pre_low[:, :KD],
        grad_pre_low[:, KD : 2 * KD],
        grad_pre_low[:, 2 * KD :],
        grad_gate_pre_low,
        mixed_low,
        grad_gate,
        grad_up,
        middle,
    )
    column_parts = (
        lax.all_to_all(right_parts[0], "ctx", split_axis=1, concat_axis=0, tiled=True),
        lax.all_to_all(right_parts[1], "ctx", split_axis=1, concat_axis=0, tiled=True),
        lax.all_to_all(right_parts[2], "ctx", split_axis=1, concat_axis=0, tiled=True),
        lax.all_to_all(right_parts[3], "ctx", split_axis=1, concat_axis=0, tiled=True),
        lax.all_to_all(right_parts[4], "ctx", split_axis=1, concat_axis=0, tiled=True),
        lax.all_to_all(right_parts[5], "ctx", split_axis=1, concat_axis=0, tiled=True),
        lax.all_to_all(right_parts[6], "ctx", split_axis=1, concat_axis=0, tiled=True),
        lax.all_to_all(right_parts[7], "ctx", split_axis=1, concat_axis=0, tiled=True),
    )
    left_rows = (
        lax.all_gather(normed_one_low, "ctx", axis=0, tiled=True),
        lax.all_gather(grad_residual_low, "ctx", axis=0, tiled=True),
        lax.all_gather(normed_two_low, "ctx", axis=0, tiled=True),
        lax.all_gather(upstream_low, "ctx", axis=0, tiled=True),
    )
    left_choice = (0, 0, 0, 0, 1, 2, 2, 3)
    column_terms = tuple(
        (
            transposed_times(left_rows[left_choice[position]], column_parts[position])
            for position in range(8)
        )
    )
    summed_terms = (
        lax.psum_scatter(
            column_terms[0].astype(jnp.bfloat16), "dp", scatter_dimension=0, tiled=True
        ).astype(jnp.float32),
        lax.psum_scatter(
            column_terms[1].astype(jnp.bfloat16), "dp", scatter_dimension=0, tiled=True
        ).astype(jnp.float32),
        lax.psum_scatter(
            column_terms[2].astype(jnp.bfloat16), "dp", scatter_dimension=0, tiled=True
        ).astype(jnp.float32),
        lax.psum_scatter(
            column_terms[3].astype(jnp.bfloat16), "dp", scatter_dimension=0, tiled=True
        ).astype(jnp.float32),
        lax.psum_scatter(
            column_terms[4].astype(jnp.bfloat16), "dp", scatter_dimension=0, tiled=True
        ).astype(jnp.float32),
        lax.psum_scatter(
            column_terms[5].astype(jnp.bfloat16), "dp", scatter_dimension=0, tiled=True
        ).astype(jnp.float32),
        lax.psum_scatter(
            column_terms[6].astype(jnp.bfloat16), "dp", scatter_dimension=0, tiled=True
        ).astype(jnp.float32),
        lax.psum_scatter(
            column_terms[7].astype(jnp.bfloat16), "dp", scatter_dimension=0, tiled=True
        ).astype(jnp.float32),
    )
    gradients = jax.tree.map(
        lambda part, own: part.astype(own.dtype),
        lax.all_to_all(shortened(summed_terms), "ctx", split_axis=0, concat_axis=1, tiled=True),
        summed_terms,
    )
    route_weight_grad = transposed_times(normed_one_low, grad_route_low)
    grad_normed_one = times_transposed(grad_pre_low[:, :KD], query_back) + times_transposed(
        grad_pre_low[:, KD : 2 * KD], key_back
    )
    grad_normed_one = grad_normed_one + times_transposed(grad_pre_low[:, 2 * KD :], value_back)
    grad_normed_one = (
        grad_normed_one
        + times_transposed(grad_gate_pre_low, gate_back)
        + times_transposed(grad_route_low, route_low)
    )
    grad_inputs, grad_gain_one = norm_one_back(grad_normed_one)
    input_grad = grad_residual + grad_inputs
    small_local = pack_small(
        (
            grad_gain_one,
            grad_gain_two,
            grad_head_gain,
            grad_conv_taps,
            grad_decay_log,
            grad_decay_bias,
            route_weight_grad,
        )
    )
    moments_new = tuple(
        (moment_rate * moment + gradient for moment, gradient in zip(moments_in, gradients))
    )
    squares_local = jnp.stack([jnp.sum(member * member) for member in moments_new])
    small_grad, squares = lax.psum((small_local, squares_local), ("dp", "ctx"))
    moment_norms = jnp.sqrt(squares)
    start_blocks = []
    for index in range(8):
        scaled = (moments_new[index] / (moment_norms[index] + eps_muon)).astype(jnp.bfloat16)
        start_blocks.append(jnp.pad(scaled, ((0, 0), (0, PADW - scaled.shape[1]))))
    data_count = lax.axis_size("dp")
    per_owner = 8 // data_count
    outgoing = jnp.stack(
        [
            jnp.stack(
                [
                    start_blocks[owner_index + data_count * slot_index]
                    for slot_index in range(per_owner)
                ]
            )
            for owner_index in range(data_count)
        ]
    )
    received = lax.all_to_all(outgoing, "dp", split_axis=0, concat_axis=2, tiled=True)
    iterate = lax.optimization_barrier(received[0])
    for step_index in range(NS_STEPS):
        whole = lax.all_gather(iterate, "ctx", axis=1, tiled=True)
        gram_low = lax.optimization_barrier(
            jnp.einsum("mrc,mkc->mrk", iterate, whole, preferred_element_type=jnp.float32).astype(
                jnp.bfloat16
            )
        )

        def fold_gram(carry_state, piece, start, gram_low=gram_low):
            return jnp.einsum("mrk,mkd->mrd", gram_low, piece, preferred_element_type=jnp.float32)

        squared = fold_gram(
            jnp.zeros(gram_low.shape, jnp.float32),
            lax.all_gather(gram_low, "ctx", axis=1, tiled=True),
            jnp.int32(0),
        )
        polynomial = (poly_two * gram_low.astype(jnp.float32) + poly_three * squared).astype(
            jnp.bfloat16
        )
        iterate = lax.optimization_barrier(
            (
                poly_one * iterate.astype(jnp.float32)
                + jnp.einsum("mrk,mkc->mrc", polynomial, whole, preferred_element_type=jnp.float32)
            ).astype(jnp.bfloat16)
        )
    returned = lax.all_to_all(iterate[None], "dp", split_axis=2, concat_axis=0, tiled=True)
    weights_new = []
    for index in range(8):
        owner_index = index % data_count
        slot_index = index // data_count
        columns_now = weights_in[index].shape[1]
        factor = matrix_rate * math.sqrt(max(1.0, columns_now / D))
        weights_new.append(
            weights_in[index]
            - factor * returned[owner_index, slot_index, :, :columns_now].astype(jnp.float32)
        )
    small_moment_new = moment_rate * small_moment + small_grad
    small_new = small_params - small_rate * small_moment_new
    return (
        block_out[None],
        input_grad[None],
        gradients[0],
        gradients[1],
        gradients[2],
        gradients[3],
        gradients[4],
        gradients[5],
        gradients[6],
        gradients[7],
        weights_new[0],
        weights_new[1],
        weights_new[2],
        weights_new[3],
        weights_new[4],
        weights_new[5],
        weights_new[6],
        weights_new[7],
        moments_new[0],
        moments_new[1],
        moments_new[2],
        moments_new[3],
        moments_new[4],
        moments_new[5],
        moments_new[6],
        moments_new[7],
        small_grad,
        small_new,
        small_moment_new,
        moment_norms,
    )


def solution(mesh):
    in_specs = (
        P("dp", "ctx", None),
        P("dp", "ctx", None),
        P(("dp", "ctx"), None),
        P(("dp", "ctx"), None),
        P(("dp", "ctx"), None),
        P(("dp", "ctx"), None),
        P(("dp", "ctx"), None),
        P(("dp", "ctx"), None),
        P(("dp", "ctx"), None),
        P(("dp", "ctx"), None),
        P(("dp", "ctx"), None),
        P(("dp", "ctx"), None),
        P(("dp", "ctx"), None),
        P(("dp", "ctx"), None),
        P(("dp", "ctx"), None),
        P(("dp", "ctx"), None),
        P(("dp", "ctx"), None),
        P(("dp", "ctx"), None),
        P(),
        P(),
    )
    out_specs = (
        P("dp", "ctx", None),
        P("dp", "ctx", None),
        P(("dp", "ctx"), None),
        P(("dp", "ctx"), None),
        P(("dp", "ctx"), None),
        P(("dp", "ctx"), None),
        P(("dp", "ctx"), None),
        P(("dp", "ctx"), None),
        P(("dp", "ctx"), None),
        P(("dp", "ctx"), None),
        P(("dp", "ctx"), None),
        P(("dp", "ctx"), None),
        P(("dp", "ctx"), None),
        P(("dp", "ctx"), None),
        P(("dp", "ctx"), None),
        P(("dp", "ctx"), None),
        P(("dp", "ctx"), None),
        P(("dp", "ctx"), None),
        P(("dp", "ctx"), None),
        P(("dp", "ctx"), None),
        P(("dp", "ctx"), None),
        P(("dp", "ctx"), None),
        P(("dp", "ctx"), None),
        P(("dp", "ctx"), None),
        P(("dp", "ctx"), None),
        P(("dp", "ctx"), None),
        P(),
        P(),
        P(),
        P(),
    )
    return jax.shard_map(local, mesh=mesh, in_specs=in_specs, out_specs=out_specs, check_vma=False)
```

profile of v0, /device:TPU:8, one launch (start us, length us, event | category | flops | bytes accessed | tf_op | source)
XLA Modules:
  0.0 2247.3 jit_solution(3328272169844483319)
XLA Ops:
  20.4 46.3 %all-gather.29.cloned.1.call-done = bf16[1024,768]{1,0:T(8,128)(2,1)} async-done(((bf16[32,768]{1,0:T(8,128)(2,1)}), bf16[1024,768]{1,0:T(8,128)(2,1)}) %all-gather.29.cloned.1.call-update) | async-done | bytes 1572880 | tf_op jit(solution)/shard_map/all_gather | solution.py:350
  68.5 55.7 %all-gather.27.cloned.1.call-done = bf16[1024,768]{1,0:T(8,128)(2,1)} async-done(((bf16[32,768]{1,0:T(8,128)(2,1)}), bf16[1024,768]{1,0:T(8,128)(2,1)}) %all-gather.27.cloned.1.call-update) | async-done | bytes 1572880 | tf_op jit(solution)/shard_map/all_gather | solution.py:349
  126.0 59.8 %all-gather.31.cloned.1.call-done = bf16[1024,1536]{1,0:T(8,128)(2,1)} async-done(((bf16[32,1536]{1,0:T(8,128)(2,1)}), bf16[1024,1536]{1,0:T(8,128)(2,1)}) %all-gather.31.cloned.1.call-update) | async-done | bytes 3145744 | tf_op jit(solution)/shard_map/all_gather | solution.py:351
  205.3 59.0 %custom-call.22 = f32[2,6,1,64,64]{3,4,2,1,0:T(8,128)S(1)} custom-call(f32[2,6,1,64,64]{4,3,2,1,0:T(8,128)S(1)} %get-tuple-element.1456), custom_call_target="InvertDiagBlocksLowerTriangular" | custom-call | tf_op jit(solution)/shard_map/vmap(vmap(jit(_solve_triangular)))/triangular_solve/custom-call.1 | solution.py:157
  296.8 28.1 %all-gather.63.cloned.1.call-done = bf16[48,128,128]{2,1,0:T(8,128)(2,1)} async-done(((bf16[6,128,128]{2,1,0:T(8,128)(2,1)}), bf16[48,128,128]{2,1,0:T(8,128)(2,1)}) %all-gather.63.cloned.1.call-update) | async-done | bytes 1572880 | tf_op jit(solution)/shard_map/all_gather | solution.py:42
  324.9 61.1 %all-gather.65.cloned.1.call-done = bf16[48,128,256]{2,1,0:T(8,128)(2,1)} async-done(((bf16[6,128,256]{2,1,0:T(8,128)(2,1)}), bf16[48,128,256]{2,1,0:T(8,128)(2,1)}) %all-gather.65.cloned.1.call-update) | async-done | bytes 3145744 | tf_op jit(solution)/shard_map/all_gather | solution.py:42
  386.0 25.1 %while.137 = (s32[]{:T(128)}, f32[6,128,256]{2,1,0:T(8,128)S(1)}, s32[]{:T(128)}, bf16[8,6,128,128]{3,2,1,0:T(8,128)(2,1)}, bf16[8,6,128,256]{3,2,1,0:T(8,128)(2,1)}, /*index=5*/s32[]{:T(128)}, s32[]{:T(128)}) while((s32[]{:T(128)}, f32[6,128,256]{2,1,0:T(8,128)S(1)}, s32[]{:T(128)}, bf16[8,6,128,128]{3,2,1,0:T(8,128)(2,1)}, ...), condition=%wide.region_6.9_spmd.clone, body=%wide.region_5.8_spmd.clone.sunk | while | flops 302972928 | bytes 4524647 | solution.py:59
  412.9 11.3 while.132
  451.4 65.8 %all-gather.37.cloned.1.call-done = bf16[1024,2816]{1,0:T(8,128)(2,1)} async-done(((bf16[32,2816]{1,0:T(8,128)(2,1)}), bf16[1024,2816]{1,0:T(8,128)(2,1)}) %all-gather.37.cloned.1.call-update) | async-done | bytes 5767184 | tf_op jit(solution)/shard_map/all_gather | solution.py:354
  521.9 64.7 %all-gather.39.cloned.1.call-done = bf16[1024,2816]{1,0:T(8,128)(2,1)} async-done(((bf16[32,2816]{1,0:T(8,128)(2,1)}), bf16[1024,2816]{1,0:T(8,128)(2,1)}) %all-gather.39.cloned.1.call-update) | async-done | bytes 5767184 | tf_op jit(solution)/shard_map/all_gather | solution.py:355
  591.4 64.6 %all-gather.41.cloned.1.call-done = bf16[1024,2816]{1,0:T(8,128)(2,1)} async-done(((bf16[32,2816]{1,0:T(8,128)(2,1)}), bf16[1024,2816]{1,0:T(8,128)(2,1)}) %all-gather.41.cloned.1.call-update) | async-done | bytes 5767184 | tf_op jit(solution)/shard_map/all_gather | solution.py:356
  676.9 15.4 while.134
  747.5 21.3 all-to-all-done.14
  796.0 33.7 %all-gather.45.cloned.1.call-done = bf16[1024,1024]{1,0:T(8,128)(2,1)} async-done(((bf16[128,1024]{1,0:T(8,128)(2,1)}), bf16[1024,1024]{1,0:T(8,128)(2,1)}) %all-gather.45.cloned.1.call-update) | async-done | bytes 2097168 | tf_op jit(solution)/shard_map/all_gather | solution.py:497
  833.1 47.3 %all-gather.47.cloned.1.call-done = bf16[1024,1024]{1,0:T(8,128)(2,1)} async-done(((bf16[128,1024]{1,0:T(8,128)(2,1)}), bf16[1024,1024]{1,0:T(8,128)(2,1)}) %all-gather.47.cloned.1.call-update) | async-done | bytes 2097168 | tf_op jit(solution)/shard_map/all_gather | solution.py:498
  909.8 17.6 reduce-scatter.23.cloned.1.call-done
  953.1 10.7 all-to-all-done.12
  977.5 45.2 %all-gather.67.cloned.1.call-done = bf16[48,128,128]{2,1,0:T(8,128)(2,1)} async-done(((bf16[6,128,128]{2,1,0:T(8,128)(2,1)}), bf16[48,128,128]{2,1,0:T(8,128)(2,1)}) %all-gather.67.cloned.1.call-update) | async-done | bytes 1572880 | tf_op jit(solution)/shard_map/all_gather | solution.py:65
  1022.6 61.1 %all-gather.69.cloned.1.call-done = bf16[48,128,256]{2,1,0:T(8,128)(2,1)} async-done(((bf16[6,128,256]{2,1,0:T(8,128)(2,1)}), bf16[48,128,256]{2,1,0:T(8,128)(2,1)}) %all-gather.69.cloned.1.call-update) | async-done | bytes 3145744 | tf_op jit(solution)/shard_map/all_gather | solution.py:65
  1083.7 15.0 while.139
  1104.9 18.8 while.135
  1234.5 13.5 reduce-scatter.11.cloned.1.call-done
  1261.5 10.2 reduce-scatter.13.cloned.1.call-done
  1290.9 40.2 %psum.14 = f32[8]{0:T(128)S(1)} all-reduce(f32[8]{0:T(128)S(1)} %stack.86), channel_id=1, replica_groups=mesh['dp'=4,'ctx'=8] {'dp','ctx'}, use_global_device_ids=true, to_apply=%region_56.60 | all-reduce | flops 8 | bytes 64 | tf_op jit(solution)/shard_map/psum | solution.py:566
  1337.6 22.0 all_to_all.283
  1360.9 159.7 %all-gather.51.cloned.1.call-done = bf16[2,1024,2816]{2,1,0:T(8,128)(2,1)} async-done(((bf16[2,128,2816]{2,1,0:T(8,128)(2,1)}), bf16[2,1024,2816]{2,1,0:T(8,128)(2,1)}) %all-gather.51.cloned.1.call-update) | async-done | bytes 11534352 | tf_op jit(solution)/shard_map/all_gather | solution.py:588
  1529.6 72.6 %all-gather.53.cloned.1.call-done = bf16[2,1024,1024]{2,1,0:T(8,128)(2,1)} async-done(((bf16[2,128,1024]{2,1,0:T(8,128)(2,1)}), bf16[2,1024,1024]{2,1,0:T(8,128)(2,1)}) %all-gather.53.cloned.1.call-update) | async-done | bytes 4194320 | tf_op jit(solution)/shard_map/all_gather | solution.py:600
  1611.6 160.4 %all-gather.55.cloned.1.call-done = bf16[2,1024,2816]{2,1,0:T(8,128)(2,1)} async-done(((bf16[2,128,2816]{2,1,0:T(8,128)(2,1)}), bf16[2,1024,2816]{2,1,0:T(8,128)(2,1)}) %all-gather.55.cloned.1.call-update) | async-done | bytes 11534352 | tf_op jit(solution)/shard_map/all_gather | solution.py:588
  1781.0 72.6 %all-gather.57.cloned.1.call-done = bf16[2,1024,1024]{2,1,0:T(8,128)(2,1)} async-done(((bf16[2,128,1024]{2,1,0:T(8,128)(2,1)}), bf16[2,1024,1024]{2,1,0:T(8,128)(2,1)}) %all-gather.57.cloned.1.call-update) | async-done | bytes 4194320 | tf_op jit(solution)/shard_map/all_gather | solution.py:600
  1863.0 160.4 %all-gather.59.cloned.1.call-done = bf16[2,1024,2816]{2,1,0:T(8,128)(2,1)} async-done(((bf16[2,128,2816]{2,1,0:T(8,128)(2,1)}), bf16[2,1024,2816]{2,1,0:T(8,128)(2,1)}) %all-gather.59.cloned.1.call-update) | async-done | bytes 11534352 | tf_op jit(solution)/shard_map/all_gather | solution.py:588
  2058.4 46.5 %all-gather.61.cloned.1.call-done = bf16[2,1024,1024]{2,1,0:T(8,128)(2,1)} async-done(((bf16[2,128,1024]{2,1,0:T(8,128)(2,1)}), bf16[2,1024,1024]{2,1,0:T(8,128)(2,1)}) %all-gather.61.cloned.1.call-update) | async-done | bytes 4194320 | tf_op jit(solution)/shard_map/all_gather | solution.py:600
  2120.5 114.1 %all-reduce.22.cloned.1.call-done = f32[26892]{0:T(1024)} async-done(((f32[26892]{0:T(1024)}), f32[26892]{0:T(1024)}) %all-reduce.22.cloned.1.call-update) | async-done | bytes 107584 | tf_op jit(solution)/shard_map/psum | solution.py:566
  (1068 shorter events, 633.8 us)
Async XLA Ops:
  7.2 59.5 %all-gather.29.cloned.1.call-start = ((), (), s32[]{:S(2)}) async-start(), calls=%async_computation.27 | async-start | bytes 1622016 | tf_op jit(solution)/shard_map/all_gather | solution.py:350
  8.8 115.4 %all-gather.27.cloned.1.call-start = ((), (), s32[]{:S(2)}) async-start(), calls=%async_computation.26 | async-start | bytes 1622016 | tf_op jit(solution)/shard_map/all_gather | solution.py:349
  10.4 175.4 %all-gather.31.cloned.1.call-start = ((), (), s32[]{:S(2)}) async-start(), calls=%async_computation.28 | async-start | bytes 3244032 | tf_op jit(solution)/shard_map/all_gather | solution.py:351
  12.1 280.0 %all-gather.33.cloned.1.call-start = ((), (), s32[]{:S(2)}) async-start(), calls=%async_computation.29 | async-start | bytes 3244032 | tf_op jit(solution)/shard_map/all_gather | solution.py:352
  13.7 311.1 %all-gather.63.cloned.1.call-start = ((), (), s32[]{:S(2)}) async-start(), calls=%async_computation.53 | async-start | bytes 1769472 | tf_op jit(solution)/shard_map/all_gather | solution.py:42
  280.7 105.2 %all-gather.65.cloned.1.call-start = ((), (), s32[]{:S(2)}) async-start(), calls=%async_computation.54 | async-start | bytes 3538944 | tf_op jit(solution)/shard_map/all_gather | solution.py:42
  282.7 163.5 %all-gather.35.cloned.1.call-start = ((), (), s32[]{:S(2)}) async-start(), calls=%async_computation.30 | async-start | bytes 3244032 | tf_op jit(solution)/shard_map/all_gather | solution.py:353
  283.5 233.7 %all-gather.37.cloned.1.call-start = ((), (), s32[]{:S(2)}) async-start(), calls=%async_computation.31 | async-start | bytes 5947392 | tf_op jit(solution)/shard_map/all_gather | solution.py:354
  285.2 301.4 %all-gather.39.cloned.1.call-start = ((), (), s32[]{:S(2)}) async-start(), calls=%async_computation.32 | async-start | bytes 5947392 | tf_op jit(solution)/shard_map/all_gather | solution.py:355
  287.0 369.0 %all-gather.41.cloned.1.call-start = ((), (), s32[]{:S(2)}) async-start(), calls=%async_computation.33 | async-start | bytes 5947392 | tf_op jit(solution)/shard_map/all_gather | solution.py:356
  288.7 455.8 %all-gather.43.cloned.1.call-start = ((), (), s32[]{:S(2)}) async-start(), calls=%async_computation.34 | async-start | bytes 2359296 | tf_op jit(solution)/shard_map/all_gather | solution.py:496
  289.5 485.1 %all-gather.49.cloned.1.call-start = ((), (), s32[]{:S(2)}) async-start(), calls=%async_computation.44 | async-start | bytes 2359296 | tf_op jit(solution)/shard_map/all_gather | solution.py:499
  290.3 539.4 %all-gather.45.cloned.1.call-start = ((), (), s32[]{:S(2)}) async-start(), calls=%async_computation.39 | async-start | bytes 2359296 | tf_op jit(solution)/shard_map/all_gather | solution.py:497
  670.9 209.5 %all-gather.47.cloned.1.call-start = ((), (), s32[]{:S(2)}) async-start(), calls=%async_computation.41 | async-start | bytes 2359296 | tf_op jit(solution)/shard_map/all_gather | solution.py:498
  744.5 157.6 %reduce-scatter.15.cloned.1.call-start = ((), (), s32[]{:S(2)}) async-start(), calls=%async_computation.38 | async-start | bytes 491520 | tf_op jit(solution)/shard_map/reduce_scatter | solution.py:518
  774.6 152.7 %reduce-scatter.23.cloned.1.call-start = ((), (), s32[]{:S(2)}) async-start(), calls=%async_computation.45 | async-start | bytes 901120 | tf_op jit(solution)/shard_map/reduce_scatter | solution.py:530
  789.3 43.7 %all-to-all-start.10 = ((bf16[128,8,352]{0,2,1:T(8,128)(2,1)}), bf16[128,8,352]{0,2,1:T(8,128)(2,1)S(1)}, u32[]{:S(2)}, u32[]{:S(2)}) async-start(bf16[128,8,352]{0,2,1:T(8,128)(2,1)} %bitcast.134), calls=%async_computation.15 | async-start | bytes 1441792 | tf_op jit(solution)/shard_map/all_to_all | solution.py:491
  796.0 171.5 %reduce-scatter.17.cloned.1.call-start = ((), (), s32[]{:S(2)}) async-start(), calls=%async_computation.40 | async-start | bytes 491520 | tf_op jit(solution)/shard_map/reduce_scatter | solution.py:521
  832.6 143.1 %reduce-scatter.19.cloned.1.call-start = ((), (), s32[]{:S(2)}) async-start(), calls=%async_computation.42 | async-start | bytes 901120 | tf_op jit(solution)/shard_map/reduce_scatter | solution.py:524
  883.8 138.8 %all-gather.67.cloned.1.call-start = ((), (), s32[]{:S(2)}) async-start(), calls=%async_computation.55 | async-start | bytes 1769472 | tf_op jit(solution)/shard_map/all_gather | solution.py:65
  886.9 196.7 %all-gather.69.cloned.1.call-start = ((), (), s32[]{:S(2)}) async-start(), calls=%async_computation.56 | async-start | bytes 3538944 | tf_op jit(solution)/shard_map/all_gather | solution.py:65
  947.8 222.3 %reduce-scatter.21.cloned.1.call-start = ((), (), s32[]{:S(2)}) async-start(), calls=%async_computation.43 | async-start | bytes 901120 | tf_op jit(solution)/shard_map/reduce_scatter | solution.py:527
  969.2 187.1 %all-to-all-start.9 = ((bf16[8,32,192]{2,1,0:T(8,128)(2,1)}), bf16[8,32,192]{2,1,0:T(8,128)(2,1)}, u32[]{:S(2)}, u32[]{:S(2)}) async-start(bf16[8,32,192]{2,1,0:T(8,128)(2,1)} %bitcast.132), calls=%async_computation.14 | async-start | bytes 262144 | tf_op jit(solution)/shard_map/all_to_all | solution.py:536
  1215.8 55.9 %reduce-scatter.13.cloned.1.call-start = ((), (), s32[]{:S(2)}) async-start(), calls=%async_computation.37 | async-start | bytes 491520 | tf_op jit(solution)/shard_map/reduce_scatter | solution.py:515
  1279.4 241.2 %all-gather.51.cloned.1.call-start = ((), (), s32[]{:S(2)}) async-start(), calls=%async_computation.46 | async-start | bytes 12976128 | tf_op jit(solution)/shard_map/all_gather | solution.py:588
  1360.9 241.3 %all-gather.53.cloned.1.call-start = ((), (), s32[]{:S(2)}) async-start(), calls=%async_computation.47 | async-start | bytes 4718592 | tf_op jit(solution)/shard_map/all_gather | solution.py:600
  1529.5 242.5 %all-gather.55.cloned.1.call-start = ((), (), s32[]{:S(2)}) async-start(), calls=%async_computation.48 | async-start | bytes 12976128 | tf_op jit(solution)/shard_map/all_gather | solution.py:588
  1611.6 242.0 %all-gather.57.cloned.1.call-start = ((), (), s32[]{:S(2)}) async-start(), calls=%async_computation.49 | async-start | bytes 4718592 | tf_op jit(solution)/shard_map/all_gather | solution.py:600
  1780.9 242.5 %all-gather.59.cloned.1.call-start = ((), (), s32[]{:S(2)}) async-start(), calls=%async_computation.50 | async-start | bytes 12976128 | tf_op jit(solution)/shard_map/all_gather | solution.py:588
  1862.9 242.0 %all-gather.61.cloned.1.call-start = ((), (), s32[]{:S(2)}) async-start(), calls=%async_computation.51 | async-start | bytes 4718592 | tf_op jit(solution)/shard_map/all_gather | solution.py:600
  2032.3 202.2 %all-reduce.22.cloned.1.call-start = ((), (), s32[]{:S(2)}) async-start(), calls=%async_computation.52 | async-start | bytes 221184 | tf_op jit(solution)/shard_map/psum | solution.py:566
  2115.8 120.4 %all-to-all-start.17 = ((bf16[1,2,128,2816]{3,1,0,2:T(2,128)(2,1)}), bf16[1,2,128,2816]{3,1,0,2:T(2,128)(2,1)S(1)}, u32[]{:S(2)}, u32[]{:S(2)}) async-start(bf16[1,2,128,2816]{3,1,0,2:T(2,128)(2,1)} %copy.482), calls=%async_computation.25 | async-start | bytes 2883584 | tf_op jit(solution)/shard_map/all_to_all | solution.py:612
  (293 other events, 5235.9 us)
Sparse Core Ops, SparseCore 0:
  11.6 55.1 all-gather.28
  70.3 53.9 all-gather.26
  127.8 58.0 all-gather.30
  189.3 59.3 all-gather.32
  280.8 44.0 all-gather.62
  327.5 58.4 all-gather.64
  389.5 56.6 all-gather.34
  449.7 67.3 all-gather.36
  520.6 65.9 all-gather.38
  590.0 65.9 all-gather.40
  658.1 47.5 all-gather.42
  708.3 56.8 all-gather.48
  767.9 61.7 all-gather.44
  832.2 48.1 all-gather.46
  882.7 19.2 reduce-scatter.14
  904.4 22.8 reduce-scatter.22
  929.7 20.7 reduce-scatter.16
  952.8 22.8 reduce-scatter.18
  978.5 44.1 all-gather.66
  1025.2 58.4 all-gather.68
  1086.2 21.4 reduce-scatter.20
  1204.5 20.5 reduce-scatter.8
  1228.1 19.7 reduce-scatter.10
  1250.9 20.8 reduce-scatter.12
  1361.0 159.5 all-gather.50
  1529.7 72.4 all-gather.52
  1611.7 160.2 all-gather.54
  1781.0 72.4 all-gather.56
  1863.0 160.2 all-gather.58
  2032.4 72.4 all-gather.60
  2111.1 123.3 all-reduce.21
where the time goes:
time: 2260 us; the launch traced here: 2250 us
  waiting for transfers between devices  1560 us (69%)
  matrix products  231 us (10%)
  local copies, waits for them, and re-layouts  138 us (6%)
  other arithmetic  130 us (6%)
  starting transfers between devices  105 us (5%)
  blocking collectives  62.2 us (3%)
    all_gather x3, waiting for transfers between devices, local(): whole = lax.all_gather(iterate, 'ctx', axis=1, tiled=True)  481 us
    all_gather x3, waiting for transfers between devices, local(): lax.all_gather(gram_low, 'ctx', axis=1, tiled=True)  192 us
    psum x1, waiting for transfers between devices, local(): small_grad, squares = lax.psum((small_local, squares_local), ('dp', 'ctx'))  114 us
    all_gather x2, waiting for transfers between devices, carried_in(): lax.all_gather(part.astype(kind), axis)  106 us
    all_gather x2, waiting for transfers between devices, prefix(): lax.all_gather(part.astype(kind), axis)  89.1 us
    all_gather x1, waiting for transfers between devices, local(): lax.all_gather(swiglu_gate_low, ('dp', 'ctx'), axis=0, tiled=True)  65.8 us
    all_gather x1, waiting for transfers between devices, local(): lax.all_gather(swiglu_up_low, ('dp', 'ctx'), axis=0, tiled=True)  64.7 us
    all_gather x1, waiting for transfers between devices, local(): lax.all_gather(swiglu_down_low, ('dp', 'ctx'), axis=0, tiled=True)  64.6 us
  transfers between devices with their start and end apart: 50, of which 38 were waited for; matrix products, arithmetic and copies ran while one was open for 18% of the time, Pallas kernels for 0%

commit v1 on v0

v1 whole, which is shorter than its diff:
```python
import math

import jax
import jax.numpy as jnp
from jax import lax
from jax.experimental import pallas as pl
from jax.sharding import PartitionSpec as P

D = 1024
H = 6
DK = 128
DV = 256
CONV = 4
GROUP = 64
NS_STEPS = 3
KD = 768
VD = 1536
QKV = 3072
FF = 2816
BOTH_AXES = ("dp", "ctx")


highest_precision = lax.Precision.HIGHEST
eps_norm = 1e-05
eps_unit = 1e-06
eps_muon = 1e-07
moment_rate = 0.95
matrix_rate = 0.3
small_rate = 0.002
poly_one = 3.4445
poly_two = -4.775
poly_three = 2.0315


def passed_along(value, axis, steps):
    count = lax.axis_size(axis)
    first, last = (max(0, -steps), min(count, count - steps))
    return lax.ppermute(value, axis, [(source, source + steps) for source in range(first, last)])


def shortened(array):
    return jax.tree.map(lambda a: a.astype(jnp.bfloat16) if a.dtype == jnp.float32 else a, array)


def matmul(left, right):
    return jnp.dot(left, right, preferred_element_type=jnp.float32)


def times_transposed(left, right):
    return lax.dot_general(
        left, right, (((1,), (1,)), ((), ())), preferred_element_type=jnp.float32
    )


def transposed_times(left, right):
    return lax.dot_general(
        left, right, (((0,), (0,)), ((), ())), preferred_element_type=jnp.float32
    )


def root_norm(values, gain):
    return values * lax.rsqrt(jnp.mean(values * values, axis=-1, keepdims=True) + eps_norm) * gain


def unit_rows(values):
    return values * lax.rsqrt(jnp.sum(values * values, axis=-1, keepdims=True) + eps_unit)


def unpack_small(packed):
    lengths = [D, D, DV, CONV * QKV, H, H, D * 2 * H]
    pieces = []
    offset = 0
    for length in lengths:
        pieces.append(packed[offset : offset + length])
        offset = offset + length
    return (
        pieces[0],
        pieces[1],
        pieces[2],
        pieces[3].reshape(CONV, QKV),
        pieces[4],
        pieces[5],
        pieces[6].reshape(D, 2 * H),
    )


def pack_small(members):
    return jnp.concatenate([member.reshape(-1) for member in members])


def conv_silu(extended, conv_taps):
    kernel_size = conv_taps.shape[0]
    rows_out = extended.shape[0] - kernel_size + 1
    summed = jnp.zeros((rows_out, extended.shape[1]), jnp.float32)
    for offset in range(kernel_size):
        summed = summed + conv_taps[offset] * extended[offset : offset + rows_out]
    return jax.nn.silu(summed)


def raw_dot(left, right, left_dim, right_dim):
    return lax.dot_general(
        left,
        right,
        (((left_dim,), (right_dim,)), ((), ())),
        precision=highest_precision,
        preferred_element_type=jnp.float32,
    )


@jax.custom_vjp
def mm(left, right):
    return raw_dot(left, right, 1, 0)


@jax.custom_vjp
def mm_nt(left, right):
    return raw_dot(left, right, 1, 1)


@jax.custom_vjp
def mm_tn(left, right):
    return raw_dot(left, right, 0, 0)


def keep_operands(function):
    return lambda left, right: (function(left, right), (left, right))


mm.defvjp(
    keep_operands(mm),
    lambda kept, grad: (raw_dot(grad, kept[1], 1, 1), raw_dot(kept[0], grad, 0, 0)),
)
mm_nt.defvjp(
    keep_operands(mm_nt),
    lambda kept, grad: (raw_dot(grad, kept[1], 1, 0), raw_dot(grad, kept[0], 0, 0)),
)
mm_tn.defvjp(
    keep_operands(mm_tn),
    lambda kept, grad: (raw_dot(kept[1], grad, 1, 1), raw_dot(kept[0], grad, 1, 0)),
)


def position_pair(rows, columns):
    return (
        lax.broadcasted_iota(jnp.int32, (rows, columns), 0),
        lax.broadcasted_iota(jnp.int32, (rows, columns), 1),
    )


def widened(member, columns):
    copies = columns // member.shape[1]
    return member if copies == 1 else jnp.concatenate([member] * copies, axis=1)


def head_masks(rows):
    at, source = position_pair(rows, rows)
    same = at // GROUP == source // GROUP
    return same, same & (at >= source), same & (at > source)


def unit_inverse(lower):
    rows = lower.shape[0]
    at, source = position_pair(rows, rows)

    def step_part(block):
        inside = (at // (2 * block) == source // (2 * block)) & (at // block != source // block)
        return jnp.where(inside, lower, 0.0)

    result = jnp.where(at == source, 1.0, 0.0) - step_part(1)
    block = 2
    while block < GROUP:
        result = result - raw_dot(result, raw_dot(step_part(block), result, 1, 0), 1, 0)
        block = 2 * block
    return result


@jax.custom_vjp
def solved(lower, target, inverse):
    return raw_dot(inverse, target, 1, 0)


def solved_forward(lower, target, inverse):
    result = raw_dot(inverse, target, 1, 0)
    return (result, (inverse, result))


def solved_backward(kept, grad):
    inverse, result = kept
    target_grad = raw_dot(inverse, grad, 0, 0)
    return (-raw_dot(target_grad, result, 1, 1), target_grad, jnp.zeros_like(inverse))


solved.defvjp(solved_forward, solved_backward)


def decay_parts(log_wide):
    rows = log_wide.shape[0]
    at, source = position_pair(rows, rows)
    same, inclusive, strictly = head_masks(rows)
    growth = jnp.exp(mm(inclusive.astype(jnp.float32), log_wide))
    tail = jnp.exp(mm((same & ~inclusive).astype(jnp.float32), log_wide))
    differ = mm(inclusive.astype(jnp.float32), jnp.where(at > source, log_wide, 0.0))
    within = jnp.where(inclusive, jnp.exp(jnp.where(inclusive, differ, 0.0)), 0.0)
    return growth, tail, within


def group_decay(log_wide, group):
    rows = log_wide.shape[0]
    source = lax.broadcasted_iota(jnp.int32, (DK, rows), 1)
    return jnp.exp(mm((source // GROUP == group).astype(jnp.float32), log_wide))


def in_group(member, group):
    row = lax.broadcasted_iota(jnp.int32, member.shape, 0)
    return jnp.where(row // GROUP == group, member, 0.0)


def lower_system(keys, beta_wide, within):
    unused_same, unused_inclusive, strictly = head_masks(keys.shape[0])
    return jnp.where(strictly, beta_wide * within * mm_nt(keys, keys), 0.0)


def solve_targets(keys, values, beta_wide, growth):
    return jnp.concatenate(
        [beta_wide * growth * keys, widened(beta_wide, DV) * values], axis=1
    )


def head_terms(queries, keys, values, beta_wide, log_wide):
    growth, tail, within = decay_parts(log_wide)
    lower = lower_system(keys, beta_wide, within)
    inverse = unit_inverse(lower)
    both = raw_dot(inverse, solve_targets(keys, values, beta_wide, growth), 1, 0)
    solved_keys = both[:, :DK]
    at, source = position_pair(DK, DK + DV)
    state = jnp.where(at == source, 1.0, 0.0)
    offset_rows = jnp.where(
        lax.broadcasted_iota(jnp.int32, both.shape, 1) >= DK, both, 0.0
    )
    decayed_keys = keys * tail
    for group in range(keys.shape[0] // GROUP):
        pseudo = offset_rows - mm(solved_keys, state)
        state = widened(group_decay(log_wide, group), DK + DV) * state + mm_tn(
            in_group(decayed_keys, group), pseudo
        )
    return inverse, both, state


def head_outputs(queries, keys, log_wide, both, gate_pre, head_gain, state):
    growth, tail, within = decay_parts(log_wide)
    attend = within * mm_nt(queries, keys)
    decayed_keys = keys * tail
    solved_keys, solved_values = both[:, :DK], both[:, DK:]
    stacked = jnp.concatenate([queries, solved_keys], axis=0)
    rows = queries.shape[0]
    read = 0.0
    for group in range(rows // GROUP):
        now = mm(stacked, state)
        pseudo_now = solved_values - now[rows:]
        read = read + jnp.concatenate(
            [in_group(now[:rows], group), in_group(now[rows:], group)], axis=0
        )
        state = widened(group_decay(log_wide, group), DV) * state + mm_tn(
            in_group(decayed_keys, group), pseudo_now
        )
    output_rows = widened(growth, DV) * read[:rows] + mm(attend, solved_values - read[rows:])
    normed = (
        output_rows
        * lax.rsqrt(jnp.mean(output_rows * output_rows, axis=-1, keepdims=True) + eps_norm)
        * head_gain
    )
    return normed * (gate_pre * jax.nn.sigmoid(gate_pre)), state


def head_whole(inverse, state, queries, keys, values, beta_wide, log_wide, gate_pre, head_gain):
    growth, tail, within = decay_parts(log_wide)
    lower = lower_system(keys, beta_wide, within)
    both = solved(lower, solve_targets(keys, values, beta_wide, growth), inverse)
    return head_outputs(queries, keys, log_wide, both, gate_pre, head_gain, state)


def unit_rows_scaled(values, factor):
    return values * lax.rsqrt(jnp.sum(values * values, axis=-1, keepdims=True) + eps_unit) * factor


def rate_columns(rates, head):
    lane = lax.broadcasted_iota(jnp.int32, rates.shape, 1)
    beta = jnp.sum(jnp.where(lane == head, rates, 0.0), axis=1, keepdims=True)
    log_decay = jnp.sum(jnp.where(lane == head + H, rates, 0.0), axis=1, keepdims=True)
    wide = (rates.shape[0], DK)
    return jnp.broadcast_to(beta, wide), jnp.broadcast_to(log_decay, wide)


def head_inputs(query_conv, key_conv, rates, head):
    queries = unit_rows_scaled(query_conv, DK ** (-0.5))
    keys = unit_rows_scaled(key_conv, 1.0)
    beta_wide, log_wide = rate_columns(rates, head)
    return queries, keys, beta_wide, log_wide


def terms_kernel(query_ref, key_ref, value_ref, rates_ref, inverse_ref, both_ref, map_ref):
    queries, keys, beta_wide, log_wide = head_inputs(
        query_ref[...], key_ref[...], rates_ref[...], pl.program_id(0)
    )
    inverse, both, state = head_terms(queries, keys, value_ref[...], beta_wide, log_wide)
    inverse_ref[...] = inverse
    both_ref[...] = both
    map_ref[0] = state


def outputs_kernel(
    query_ref, key_ref, rates_ref, both_ref, gate_ref, gain_ref, state_ref, mixed_ref
):
    queries, keys, beta_wide, log_wide = head_inputs(
        query_ref[...], key_ref[...], rates_ref[...], pl.program_id(0)
    )
    mixed, unused = head_outputs(
        queries, keys, log_wide, both_ref[...], gate_ref[...], gain_ref[...], state_ref[0]
    )
    mixed_ref[...] = mixed.astype(mixed_ref.dtype)


def state_kernel(
    query_ref, key_ref, rates_ref, both_ref, gate_ref, gain_ref, state_ref, grad_ref, out_ref
):
    queries, keys, beta_wide, log_wide = head_inputs(
        query_ref[...], key_ref[...], rates_ref[...], pl.program_id(0)
    )

    def from_state(state):
        return head_outputs(
            queries, keys, log_wide, both_ref[...], gate_ref[...], gain_ref[...], state
        )[0]

    unused, back = jax.vjp(from_state, state_ref[0])
    out_ref[0] = back(grad_ref[...])[0]


def backward_kernel(
    inverse_ref,
    state_ref,
    query_ref,
    key_ref,
    value_ref,
    rates_ref,
    gate_ref,
    gain_ref,
    grad_ref,
    state_grad_ref,
    query_out,
    key_out,
    value_out,
    rates_out,
    gate_out,
    gain_out,
):
    inverse, state = inverse_ref[...], state_ref[0]
    head = pl.program_id(0)

    def whole(query_conv, key_conv, values, rates, gate_pre, gain):
        queries, keys, beta_wide, log_wide = head_inputs(query_conv, key_conv, rates, head)
        return head_whole(
            inverse, state, queries, keys, values, beta_wide, log_wide, gate_pre, gain
        )

    unused, back = jax.vjp(
        whole,
        query_ref[...],
        key_ref[...],
        value_ref[...],
        rates_ref[...],
        gate_ref[...],
        gain_ref[...],
    )
    grads = back((grad_ref[...], state_grad_ref[0]))
    query_out[...] = grads[0]
    key_out[...] = grads[1]
    value_out[...] = grads[2]
    gate_out[...] = grads[4].astype(gate_out.dtype)
    gain_out[0] = grads[5]

    @pl.when(head == 0)
    def first_head():
        rates_out[...] = grads[3]

    @pl.when(head > 0)
    def later_head():
        rates_out[...] = rates_out[...] + grads[3]


def columns_of(rows, width, first=0):
    return pl.BlockSpec((rows, width), lambda head: (0, head + first))


def matrix_of(rows, width):
    return pl.BlockSpec((1, rows, width), lambda head: (head, 0, 0))


def fixed_block(rows, width):
    return pl.BlockSpec((rows, width), lambda head: (0, 0))


def per_head(kernel, in_specs, out_specs, out_shapes):
    return pl.pallas_call(
        kernel, grid=(H,), in_specs=in_specs, out_specs=out_specs, out_shape=out_shapes
    )


def shape_of(*dims, kind=jnp.float32):
    return jax.ShapeDtypeStruct(dims, kind)


def run_terms(conv_out, rates):
    rows = conv_out.shape[0]
    return per_head(
        terms_kernel,
        [
            columns_of(rows, DK),
            columns_of(rows, DK, H),
            columns_of(rows, DV, 2 * KD // DV),
            fixed_block(rows, 2 * H),
        ],
        [columns_of(rows, rows), columns_of(rows, DK + DV), matrix_of(DK, DK + DV)],
        [
            shape_of(rows, H * rows),
            shape_of(rows, H * (DK + DV)),
            shape_of(H, DK, DK + DV),
        ],
    )(conv_out, conv_out, conv_out, rates)


def output_specs(rows):
    return [
        columns_of(rows, DK),
        columns_of(rows, DK, H),
        fixed_block(rows, 2 * H),
        columns_of(rows, DK + DV),
        columns_of(rows, DV, QKV // DV),
        fixed_block(1, DV),
        matrix_of(DK, DV),
    ]


def run_outputs(conv_out, rates, both, projected, gain_row, state):
    rows = conv_out.shape[0]
    return per_head(
        outputs_kernel,
        output_specs(rows),
        columns_of(rows, DV),
        shape_of(rows, H * DV, kind=jnp.bfloat16),
    )(conv_out, conv_out, rates, both, projected, gain_row, state)


def run_state(conv_out, rates, both, projected, gain_row, state, grad):
    rows = conv_out.shape[0]
    return per_head(
        state_kernel,
        output_specs(rows) + [columns_of(rows, DV)],
        matrix_of(DK, DV),
        shape_of(H, DK, DV),
    )(conv_out, conv_out, rates, both, projected, gain_row, state, grad)


def run_backward(inverse, state, conv_out, rates, projected, gain_row, grad, state_grad):
    rows = conv_out.shape[0]
    narrow, wide = columns_of(rows, DK), columns_of(rows, DV)
    return per_head(
        backward_kernel,
        [
            columns_of(rows, rows),
            matrix_of(DK, DV),
            narrow,
            columns_of(rows, DK, H),
            columns_of(rows, DV, 2 * KD // DV),
            fixed_block(rows, 2 * H),
            columns_of(rows, DV, QKV // DV),
            fixed_block(1, DV),
            wide,
            matrix_of(DK, DV),
        ],
        [narrow, narrow, wide, fixed_block(rows, 2 * H), wide, matrix_of(1, DV)],
        [
            shape_of(rows, H * DK),
            shape_of(rows, H * DK),
            shape_of(rows, H * DV),
            shape_of(rows, 2 * H),
            shape_of(rows, H * DV, kind=jnp.bfloat16),
            shape_of(H, 1, DV),
        ],
    )(
        inverse,
        state,
        conv_out,
        conv_out,
        conv_out,
        rates,
        projected,
        gain_row,
        grad,
        state_grad,
    )


def rate_parts(route_pre, decay_log, decay_bias):
    betas = jax.nn.sigmoid(route_pre[:, :H])
    log_decay = -jnp.exp(decay_log) * jax.nn.softplus(route_pre[:, H:] + decay_bias)
    return jnp.concatenate([betas, log_decay], axis=1)


def map_times(left, right):
    return jnp.einsum("hij,hjv->hiv", left, right, precision=highest_precision)


def sent_low(value, steps):
    return passed_along(value.astype(jnp.bfloat16), "ctx", steps).astype(jnp.float32)


def window_maps(trans, direction):
    count = lax.axis_size("ctx")
    levels = [trans]
    window = 1
    while 2 * window < count:
        levels.append(map_times(levels[-1], sent_low(levels[-1], direction * window)))
        window = 2 * window
    return levels, sent_low(levels[-1], direction)


def carried_state(levels, near_trans, offset, direction):
    window = 1
    for trans in levels[:-1]:
        offset = offset + map_times(trans, sent_low(offset, direction * window))
        window = 2 * window
    near = sent_low(offset, direction)
    far = sent_low(offset, direction * (window + 1))
    return near + map_times(near_trans, far)


def swap_columns(rows, count):
    split = rows.reshape(rows.shape[0], count, rows.shape[1] // count)
    return jnp.transpose(split, (1, 0, 2))


def summed_rows(terms, columns):
    dp_count, ctx_count = lax.axis_size("dp"), lax.axis_size("ctx")
    parts = lax.all_to_all(
        terms.reshape(dp_count, D // dp_count, columns), "dp", split_axis=0, concat_axis=0, tiled=True
    )
    block = jnp.sum(parts.astype(jnp.float32), axis=0).astype(jnp.bfloat16)
    rows = D // (dp_count * ctx_count)
    return lax.all_to_all(
        block.reshape(ctx_count, rows, columns), "ctx", split_axis=0, concat_axis=0, tiled=True
    )


def joined_columns(blocks):
    count, rows, columns = blocks.shape
    return jnp.transpose(blocks, (1, 0, 2)).reshape(rows, count * columns).astype(jnp.float32)


def summed_everywhere(vector):
    count = lax.axis_size("dp") * lax.axis_size("ctx")
    chunk = -(-vector.shape[0] // (count * 128)) * 128
    padded = jnp.pad(vector, (0, count * chunk - vector.shape[0])).reshape(count, chunk)
    parts = lax.all_to_all(padded, BOTH_AXES, split_axis=0, concat_axis=0, tiled=True)
    total = jnp.broadcast_to(jnp.sum(parts, axis=0)[None], (count, chunk))
    whole = lax.all_to_all(total, BOTH_AXES, split_axis=0, concat_axis=0, tiled=True)
    return whole.reshape(-1)[: vector.shape[0]]


def square_times(left, right):
    return jnp.dot(left, right, preferred_element_type=jnp.float32)


def orthogonal_rows(raw_rows):
    low = jnp.bfloat16
    raw = lax.all_gather(raw_rows, "dp", axis=0, tiled=True)
    gram_raw = times_transposed(raw, raw)
    norm = jnp.sqrt(jnp.trace(gram_raw))
    scale = 1.0 / (norm + eps_muon)
    gram = gram_raw * (scale * scale)
    factors = []
    for step in range(NS_STEPS):
        gram_low = gram.astype(low)
        factor = (poly_two * gram + poly_three * square_times(gram_low, gram_low)).astype(low)
        factors.append(factor)
        if step + 1 < NS_STEPS:
            turned = poly_one * gram + square_times(factor, gram_low)
            gram = poly_one * turned + square_times(turned.astype(low), factor)
    rows = raw_rows.shape[0]
    start = lax.axis_index("dp") * rows
    last = factors[-1]
    at = lax.broadcasted_iota(jnp.int32, (rows, D), 0) + start
    own = at == lax.broadcasted_iota(jnp.int32, (rows, D), 1)
    product = lax.dynamic_slice_in_dim(last, start, rows, axis=0).astype(jnp.float32)
    identity_part = poly_one
    for factor in factors[-2::-1]:
        product_low = product.astype(low)
        mine = lax.dynamic_slice_in_dim(factor, start, rows, axis=0).astype(jnp.float32)
        product = (
            poly_one * product + identity_part * mine + square_times(product_low, factor)
        )
        identity_part = identity_part * poly_one
    mapped = square_times(product.astype(low), raw)
    return ((identity_part * raw_rows.astype(jnp.float32) + mapped) * scale).astype(low)


def local(
    tokens_in,
    upstream,
    query_weight,
    key_weight,
    value_weight,
    gate_weight,
    output_weight,
    swiglu_gate,
    swiglu_up,
    swiglu_down,
    query_moment,
    key_moment,
    value_moment,
    gate_moment,
    output_moment,
    swiglu_gate_moment,
    swiglu_up_moment,
    swiglu_down_moment,
    small_params,
    small_moment,
):
    weights_in = (
        query_weight,
        key_weight,
        value_weight,
        gate_weight,
        output_weight,
        swiglu_gate,
        swiglu_up,
        swiglu_down,
    )
    moments_in = (
        query_moment,
        key_moment,
        value_moment,
        gate_moment,
        output_moment,
        swiglu_gate_moment,
        swiglu_up_moment,
        swiglu_down_moment,
    )
    low = jnp.bfloat16
    ctx_count = lax.axis_size("ctx")
    gain_one, gain_two, head_gain, conv_taps, decay_log, decay_bias, route_weight = unpack_small(
        small_params
    )
    route_low = route_weight.astype(low)
    rim_rows = CONV - 1
    front_rows = jnp.concatenate([member.astype(low) for member in weights_in[:4]], axis=1)
    back_rows = jnp.concatenate([member.astype(low) for member in weights_in[4:]], axis=1)
    front_full = lax.all_gather(front_rows, BOTH_AXES, axis=0, tiled=True)
    front_full, back_rows = lax.optimization_barrier((front_full, back_rows))
    back_full = lax.all_gather(back_rows, BOTH_AXES, axis=0, tiled=True)
    output_full = back_full[:, :VD]
    gate_up_full = back_full[:, VD : VD + 2 * FF]
    down_full = back_full[:, VD + 2 * FF :]

    inputs_full = tokens_in[0].astype(jnp.float32)
    normed_one, norm_one_back = jax.vjp(root_norm, inputs_full, gain_one)
    normed_one_low = normed_one.astype(low)
    projected = matmul(normed_one_low, front_full)
    pre_proj = projected[:, :QKV]
    route_pre = matmul(normed_one_low, route_low)
    prior_rim = passed_along(
        pre_proj[pre_proj.shape[0] - rim_rows :].astype(low), "ctx", 1
    ).astype(jnp.float32)
    extended = jnp.concatenate([prior_rim, pre_proj], axis=0)
    conv_out, conv_back = jax.vjp(conv_silu, extended, conv_taps)
    rates, rates_back = jax.vjp(rate_parts, route_pre, decay_log, decay_bias)
    gain_row = head_gain[None]

    inverse, both, maps = run_terms(conv_out, rates)
    trans, offset = maps[:, :, :DK], maps[:, :, DK:]
    levels, near_trans = window_maps(trans, 1)
    state_in = carried_state(levels, near_trans, offset, 1)
    back_levels, back_near = window_maps(jnp.swapaxes(trans, 1, 2), -1)
    mixed_low = run_outputs(conv_out, rates, both, projected, gain_row, state_in)
    residual_one = inputs_full + times_transposed(mixed_low, output_full)
    normed_two, norm_two_back = jax.vjp(root_norm, residual_one, gain_two)
    normed_two_low = normed_two.astype(low)
    gate_up = matmul(normed_two_low, gate_up_full)
    gate_act, up_act = gate_up[:, :FF], gate_up[:, FF:]
    sigma = jax.nn.sigmoid(gate_act)
    middle = (gate_act * sigma * up_act).astype(low)
    block_out = residual_one + times_transposed(middle, down_full)

    upstream_full = upstream[0]
    upstream_low = upstream_full.astype(low)
    grad_middle = matmul(upstream_low, down_full)
    grad_gate = (grad_middle * up_act * sigma * (1.0 + gate_act * (1.0 - sigma))).astype(low)
    grad_up = (grad_middle * gate_act * sigma).astype(low)
    grad_gate_up = jnp.concatenate([grad_gate, grad_up], axis=1)
    grad_normed_two = times_transposed(grad_gate_up, gate_up_full)
    grad_residual_norm, grad_gain_two = norm_two_back(grad_normed_two)
    grad_residual = upstream_full + grad_residual_norm
    grad_residual_low = grad_residual.astype(low)
    grad_mixed = matmul(grad_residual_low, output_full)

    early_left = jnp.concatenate([normed_one_low, upstream_low], axis=1)
    early_left, unused_full = lax.optimization_barrier((early_left, back_full))
    early_left = lax.all_gather(early_left, "ctx", axis=0, tiled=True)
    late_left = lax.all_gather(
        jnp.concatenate([normed_two_low, grad_residual_low], axis=1), "ctx", axis=0, tiled=True
    )

    state_grad = run_state(conv_out, rates, both, projected, gain_row, state_in, grad_mixed)
    state_out_grad = carried_state(back_levels, back_near, state_grad, -1)
    back_columns = jnp.concatenate(
        [swap_columns(member, ctx_count) for member in (mixed_low, grad_gate_up, middle)], axis=2
    )
    back_columns = lax.all_to_all(back_columns, "ctx", split_axis=0, concat_axis=0, tiled=True)

    query_grad, key_grad, value_grad, rates_grad, grad_gate_pre_low, gain_grads = run_backward(
        inverse, state_in, conv_out, rates, projected, gain_row, grad_mixed, state_out_grad
    )
    grad_conv = jnp.concatenate([query_grad, key_grad, value_grad], axis=1)
    grad_extended, grad_conv_taps = conv_back(grad_conv)
    grad_route_pre, grad_decay_log, grad_decay_bias = rates_back(rates_grad)
    grad_head_gain = jnp.sum(gain_grads, axis=(0, 1))
    back_rim = passed_along(shortened(grad_extended[:rim_rows]), "ctx", -1)
    grad_pre = grad_extended[rim_rows:]
    split_row = grad_pre.shape[0] - rim_rows
    grad_pre = jnp.concatenate([grad_pre[:split_row], grad_pre[split_row:] + back_rim], axis=0)
    grad_front_low = jnp.concatenate([grad_pre.astype(low), grad_gate_pre_low], axis=1)
    grad_route_low = grad_route_pre.astype(low)

    front_columns = lax.all_to_all(
        swap_columns(grad_front_low, ctx_count), "ctx", split_axis=0, concat_axis=0, tiled=True
    )
    count_rows = ctx_count * grad_front_low.shape[0]
    widths = (VD // ctx_count, 2 * FF // ctx_count, FF // ctx_count)
    back_columns = back_columns.reshape(count_rows, sum(widths))
    piece_out = back_columns[:, : widths[0]]
    piece_gate_up = back_columns[:, widths[0] : widths[0] + widths[1]]
    piece_down = back_columns[:, widths[0] + widths[1] :]
    back_terms = jnp.concatenate(
        [
            transposed_times(late_left[:, D:], piece_out).astype(low),
            transposed_times(late_left[:, :D], piece_gate_up).astype(low),
            transposed_times(early_left[:, D:], piece_down).astype(low),
        ],
        axis=1,
    )
    back_blocks = summed_rows(back_terms, sum(widths))
    front_width = grad_front_low.shape[1] // ctx_count
    front_terms = transposed_times(
        early_left[:, :D], front_columns.reshape(count_rows, front_width)
    ).astype(low)
    front_blocks = summed_rows(front_terms, front_width)
    front_grads = joined_columns(front_blocks)
    gate_up_grads = joined_columns(back_blocks[:, :, widths[0] : widths[0] + widths[1]])
    gradients = (
        front_grads[:, :KD],
        front_grads[:, KD : 2 * KD],
        front_grads[:, 2 * KD : QKV],
        front_grads[:, QKV:],
        joined_columns(back_blocks[:, :, : widths[0]]),
        gate_up_grads[:, :FF],
        gate_up_grads[:, FF:],
        joined_columns(back_blocks[:, :, widths[0] + widths[1] :]),
    )

    route_weight_grad = transposed_times(normed_one_low, grad_route_low)
    grad_normed_one = times_transposed(grad_front_low, front_full) + times_transposed(
        grad_route_low, route_low
    )
    grad_inputs, grad_gain_one = norm_one_back(grad_normed_one)
    input_grad = grad_residual + grad_inputs
    small_local = pack_small(
        (
            grad_gain_one,
            grad_gain_two,
            grad_head_gain,
            grad_conv_taps,
            grad_decay_log,
            grad_decay_bias,
            route_weight_grad,
        )
    )
    moments_new = tuple(
        (moment_rate * moment + gradient for moment, gradient in zip(moments_in, gradients))
    )
    squares_local = jnp.stack([jnp.sum(member * member) for member in moments_new])

    repeats = ctx_count // 8
    outgoing = jnp.stack(
        [
            jnp.pad(moments_new[owner // repeats].astype(low), ((0, 0), (0, FF - moments_new[owner // repeats].shape[1])))
            for owner in range(ctx_count)
        ]
    )
    received = lax.all_to_all(outgoing, "ctx", split_axis=0, concat_axis=0, tiled=True)
    ortho = orthogonal_rows(received.reshape(-1, FF))
    returned = lax.all_to_all(
        ortho.reshape(received.shape), "ctx", split_axis=0, concat_axis=0, tiled=True
    )
    weights_new = []
    for index in range(8):
        columns_now = weights_in[index].shape[1]
        factor = matrix_rate * math.sqrt(max(1.0, columns_now / D))
        weights_new.append(
            weights_in[index]
            - factor * returned[index * repeats, :, :columns_now].astype(jnp.float32)
        )
    summed = summed_everywhere(jnp.concatenate([small_local, squares_local]))
    small_grad = summed[: small_local.shape[0]]
    moment_norms = jnp.sqrt(summed[small_local.shape[0] :])
    small_moment_new = moment_rate * small_moment + small_grad
    small_new = small_params - small_rate * small_moment_new
    return (
        block_out[None],
        input_grad[None],
        *gradients,
        *weights_new,
        *moments_new,
        small_grad,
        small_new,
        small_moment_new,
        moment_norms,
    )


def solution(mesh):
    in_specs = (
        P("dp", "ctx", None),
        P("dp", "ctx", None),
        P(("dp", "ctx"), None),
        P(("dp", "ctx"), None),
        P(("dp", "ctx"), None),
        P(("dp", "ctx"), None),
        P(("dp", "ctx"), None),
        P(("dp", "ctx"), None),
        P(("dp", "ctx"), None),
        P(("dp", "ctx"), None),
        P(("dp", "ctx"), None),
        P(("dp", "ctx"), None),
        P(("dp", "ctx"), None),
        P(("dp", "ctx"), None),
        P(("dp", "ctx"), None),
        P(("dp", "ctx"), None),
        P(("dp", "ctx"), None),
        P(("dp", "ctx"), None),
        P(),
        P(),
    )
    out_specs = (
        P("dp", "ctx", None),
        P("dp", "ctx", None),
        P(("dp", "ctx"), None),
        P(("dp", "ctx"), None),
        P(("dp", "ctx"), None),
        P(("dp", "ctx"), None),
        P(("dp", "ctx"), None),
        P(("dp", "ctx"), None),
        P(("dp", "ctx"), None),
        P(("dp", "ctx"), None),
        P(("dp", "ctx"), None),
        P(("dp", "ctx"), None),
        P(("dp", "ctx"), None),
        P(("dp", "ctx"), None),
        P(("dp", "ctx"), None),
        P(("dp", "ctx"), None),
        P(("dp", "ctx"), None),
        P(("dp", "ctx"), None),
        P(("dp", "ctx"), None),
        P(("dp", "ctx"), None),
        P(("dp", "ctx"), None),
        P(("dp", "ctx"), None),
        P(("dp", "ctx"), None),
        P(("dp", "ctx"), None),
        P(("dp", "ctx"), None),
        P(("dp", "ctx"), None),
        P(),
        P(),
        P(),
        P(),
    )
    return jax.shard_map(local, mesh=mesh, in_specs=in_specs, out_specs=out_specs, check_vma=False)
```

time: 2260 us -> 873 us (0.39)
  waiting for transfers between devices: 1560 us -> 401 us
  matrix products: 231 us -> 115 us
  Pallas kernels: 0 us -> 102 us
  local copies, waits for them, and re-layouts: 138 us -> 40.4 us
  other arithmetic: 130 us -> 46 us
  blocking collectives: 62.2 us -> 38.7 us
    all_gather x22 -> x5, waiting for transfers between devices: 1320 us -> 110 us  [the longest x1 80.6 us: local(): front_full = lax.all_gather(front_rows, BOTH_AXES, axis=0, tiled=True)]
    psum x1 -> x0, waiting for transfers between devices: 114 us -> none  [local(): small_grad, squares = lax.psum((small_local, squares_local), ('dp', 'ctx'))]
    all_to_all x17 -> x9, waiting for transfers between devices: 74.8 us -> 188 us  [the longest x1 79.5 us: local(): lax.all_to_all(back_columns, 'ctx', split_axis=0, concat_axis=0, tiled=True)]
    dot_general x88 -> x19, matrix products: 146 us -> 42.8 us  [the longest x9 30.3 us: square_times(): return jnp.dot(left, right, preferred_element_type=jnp.float32)]
    pallas_call x0 -> x4, Pallas kernels: none -> 102 us  [the longest x1 37.8 us: run_backward(): per_head(backward_kernel, [columns_of(rows, rows), matrix_of(DK, DV), nar...]
    ppermute x2 -> x16, waiting for transfers between devices: 2.81 us -> 103 us  [passed_along(): lax.ppermute(value, axis, [(source, source + steps) for source in range(f...]
    another operation x16 -> x3, other arithmetic: 65.9 us -> 2.83 us  [the longest x4 59.1 us: solve_unit(): jax.scipy.linalg.solve_triangular(matrix, target, lower=True, unit_diagon...]
    all_to_all x17 -> x9, starting transfers between devices: 95.2 us -> 46.8 us  [the longest x2 11.8 us: summed_rows(): lax.all_to_all(block.reshape(ctx_count, rows, columns), 'ctx', split_axis...]
  transfers between devices with their start and end apart: 50 -> 30, of which waited for: 38 -> 22; matrix products, arithmetic and copies ran while one was open for 18% -> 20% of each run, Pallas kernels for 0% -> 12%
where the time goes in v1:
time: 873 us; the launch traced here: 859 us
  waiting for transfers between devices  401 us (46%)
  matrix products  115 us (13%)
  Pallas kernels  102 us (12%)
  starting transfers between devices  98.9 us (11%)
  other arithmetic  46 us (5%)
  local copies, waits for them, and re-layouts  40.4 us (5%)
  blocking collectives  38.7 us (4%)
  between operations  16.4 us (2%)
    ppermute x16, waiting for transfers between devices, passed_along(): lax.ppermute(value, axis, [(source, source + steps) for source in range(f...  103 us
    all_gather x1, waiting for transfers between devices, local(): front_full = lax.all_gather(front_rows, BOTH_AXES, axis=0, tiled=True)  80.6 us
    all_to_all x1, waiting for transfers between devices, local(): lax.all_to_all(back_columns, 'ctx', split_axis=0, concat_axis=0, tiled=True)  79.5 us
    ppermute x16, starting transfers between devices, passed_along(): lax.ppermute(value, axis, [(source, source + steps) for source in range(f...  51.6 us
    all_to_all x1, blocking collectives, local(): lax.all_to_all(outgoing, 'ctx', split_axis=0, concat_axis=0, tiled=True)  38.7 us
    pallas_call x1, Pallas kernels, run_backward(): per_head(backward_kernel, [columns_of(rows, rows), matrix_of(DK, DV), nar...  37.8 us
    dot_general x6, matrix products, times_transposed(): lax.dot_general(left, right, (((1,), (1,)), ((), ())), preferred_element_...  37.8 us
    all_to_all x1, waiting for transfers between devices, local(): lax.all_to_all(swap_columns(grad_front_low, ctx_count), 'ctx', split_axis...  33.9 us
  transfers between devices with their start and end apart: 30, of which 22 were waited for; matrix products, arithmetic and copies ran while one was open for 20% of the time, Pallas kernels for 12%

profile of v1, /device:TPU:8, one launch (start us, length us, event | category | flops | bytes accessed | tf_op | source)
XLA Modules:
  0.0 859.2 jit_solution(16070230675159105077)
XLA Ops:
  13.9 80.6 %all-gather.6.cloned.1.call-done = bf16[1024,4608]{1,0:T(8,128)(2,1)} async-done(((bf16[32,4608]{1,0:T(8,128)(2,1)}), bf16[1024,4608]{1,0:T(8,128)(2,1)}) %all-gather.6.cloned.1.call-update) | async-done | bytes 9437200 | tf_op jit(solution)/shard_map/all_gather | solution.py:658
  110.3 27.8 %shard_map.427 = (f32[128,768]{1,0:T(8,128)}, f32[128,2304]{1,0:T(8,128)}, f32[6,128,384]{2,1,0:T(8,128)}) custom-call(f32[128,3072]{1,0:T(8,128)} %get-tuple-element.94.query_ref.key_ref.value_ref, f32[128,3072]{1,0:T(8,128)} %get-tuple-element.94.query_ref.key_ref.value_ref, f32[128,3072]{1,0:T(8,128)} %get-tuple-element.94.query_ref.key_ref.value_ref, ...), custom_call_target="tpu_custom_call" | custom-call | tf_op jit(solution)/shard_map/pallas_call | solution.py:415
  147.8 12.9 %collective-permute-done.1 = bf16[6,128,256]{2,1,0:T(8,128)(2,1)S(1)} collective-permute-done((bf16[6,128,256]{2,1,0:T(8,128)(2,1)S(1)}, bf16[6,128,256]{2,1,0:T(8,128)(2,1)S(1)}, u32[]{:S(2)}, u32[]{:S(2)}) %collective-permute-start.1) | collective-permute-done | bytes 393248 | tf_op jit(solution)/shard_map/ppermute | solution.py:38
  176.3 6.0 collective-permute-start.4
  191.2 36.7 %collective-permute-done.6 = bf16[6,128,128]{2,1,0:T(8,128)(2,1)} collective-permute-done((bf16[6,128,128]{2,1,0:T(8,128)(2,1)}, bf16[6,128,128]{2,1,0:T(8,128)(2,1)}, u32[]{:S(2)}, u32[]{:S(2)}) %collective-permute-start.6) | collective-permute-done | bytes 196640 | tf_op jit(solution)/shard_map/ppermute | solution.py:38
  230.4 14.3 %shard_map.428 = bf16[128,1536]{1,0:T(8,128)(2,1)} custom-call(f32[128,3072]{1,0:T(8,128)} %get-tuple-element.94.query_ref.key_ref.value_ref, f32[128,3072]{1,0:T(8,128)} %get-tuple-element.94.query_ref.key_ref.value_ref, f32[128,12]{1,0:T(8,128)} %pad_maximum_fusion.9.rates_ref, f32[128,2304]{1,0:T(8,128)} %get-tuple-element.43.both_ref, ...), custom_call_target="tpu_custom_call" | custom-call | tf_op jit(solution)/shard_map/pallas_call | solution.py:446
  244.6 15.6 %all-gather.8.cloned.1.call-done = bf16[1024,9984]{1,0:T(8,128)(2,1)} async-done(((bf16[32,9984]{1,0:T(8,128)(2,1)}), bf16[1024,9984]{1,0:T(8,128)(2,1)}) %all-gather.8.cloned.1.call-update) | async-done | bytes 20447248 | tf_op jit(solution)/shard_map/all_gather | solution.py:660
  277.5 7.9 multiply_reduce_fusion.4
  290.6 22.3 %shard_map.429 = f32[6,128,256]{2,1,0:T(8,128)} custom-call(f32[128,3072]{1,0:T(8,128)} %get-tuple-element.94.query_ref.key_ref.value_ref, f32[128,3072]{1,0:T(8,128)} %get-tuple-element.94.query_ref.key_ref.value_ref, f32[128,12]{1,0:T(8,128)} %pad_maximum_fusion.9.rates_ref, f32[128,2304]{1,0:T(8,128)} %get-tuple-element.43.both_ref, f32[128,4608]{1,0:T(8,128)} %copy-done, ...), custom_call_target="tpu_custom_call" | custom-call | tf_op jit(solution)/shard_map/pallas_call | solution.py:456
  320.9 12.0 %collective-permute-done.8 = bf16[6,128,256]{2,1,0:T(8,128)(2,1)S(1)} collective-permute-done((bf16[6,128,256]{2,1,0:T(8,128)(2,1)S(1)}, bf16[6,128,256]{2,1,0:T(8,128)(2,1)S(1)}, u32[]{:S(2)}, u32[]{:S(2)}) %collective-permute-start.8) | collective-permute-done | bytes 393248 | tf_op jit(solution)/shard_map/ppermute | solution.py:38
  336.8 8.6 %collective-permute-done.9 = bf16[6,128,128]{1,2,0:T(8,128)(2,1)S(1)} collective-permute-done((bf16[6,128,128]{1,2,0:T(8,128)(2,1)S(1)}, bf16[6,128,128]{1,2,0:T(8,128)(2,1)S(1)}, u32[]{:S(2)}, u32[]{:S(2)}) %collective-permute-start.9) | collective-permute-done | bytes 196640 | tf_op jit(solution)/shard_map/ppermute | solution.py:38
  348.8 7.8 collective-permute-done.10
  365.0 17.7 %collective-permute-done.13 = bf16[6,128,128]{2,1,0:T(8,128)(2,1)S(1)} collective-permute-done((bf16[6,128,128]{2,1,0:T(8,128)(2,1)S(1)}, bf16[6,128,128]{2,1,0:T(8,128)(2,1)S(1)}, u32[]{:S(2)}, u32[]{:S(2)}) %collective-permute-start.13) | collective-permute-done | bytes 196640 | tf_op jit(solution)/shard_map/ppermute | solution.py:38
  383.9 37.8 %shard_map.430 = (f32[128,768]{1,0:T(8,128)}, f32[128,768]{1,0:T(8,128)}, f32[128,1536]{1,0:T(8,128)}, f32[128,12]{1,0:T(8,128)}, bf16[128,1536]{1,0:T(8,128)(2,1)}, /*index=5*/f32[6,1,256]{2,1,0:T(1,128)}) custom-call(f32[128,768]{1,0:T(8,128)} %get-tuple-element.46.inverse_ref, f32[6,128,256]{2,1,0:T(8,128)} %convert_add_fusion.1.state_ref, ...), custom_call_target="tpu_custom_call" | custom-call | tf_op jit(solution)/shard_map/pallas_call | solution.py:467
  438.2 5.4 all-to-all-start
  451.2 33.9 %all-to-all-done = bf16[8,128,576]{1,2,0:T(8,128)(2,1)} async-done(((bf16[8,128,576]{1,2,0:T(8,128)(2,1)}), bf16[8,128,576]{1,2,0:T(8,128)(2,1)}, u32[]{:S(2)}, u32[]{:S(2)}) %all-to-all-start) | async-done | bytes 1179680 | tf_op jit(solution)/shard_map/all_to_all | solution.py:734
  485.1 7.3 all-to-all-start.3
  496.8 79.5 %all-to-all-done.3 = bf16[8,128,1248]{1,2,0:T(8,128)(2,1)} async-done(((bf16[8,128,1248]{1,2,0:T(8,128)(2,1)}), bf16[8,128,1248]{1,2,0:T(8,128)(2,1)}, u32[]{:S(2)}, u32[]{:S(2)}) %all-to-all-start.3) | async-done | bytes 2555936 | tf_op jit(solution)/shard_map/all_to_all | solution.py:718
  588.0 5.4 fusion.39
  597.0 7.2 all-to-all-start.2
  620.8 27.6 %all-to-all-done.4 = bf16[4,256,1248]{1,2,0:T(8,128)(2,1)} async-done(((bf16[4,256,1248]{1,2,0:T(8,128)(2,1)}), bf16[4,256,1248]{1,2,0:T(8,128)(2,1)}, u32[]{:S(2)}, u32[]{:S(2)}) %all-to-all-start.4) | async-done | bytes 2555936 | tf_op jit(solution)/shard_map/all_to_all | solution.py:545
  661.4 10.9 %all-to-all-done.5 = bf16[8,32,1248]{2,1,0:T(8,128)(2,1)S(1)} async-done(((bf16[8,32,1248]{2,1,0:T(8,128)(2,1)}), bf16[8,32,1248]{2,1,0:T(8,128)(2,1)S(1)}, u32[]{:S(2)}, u32[]{:S(2)}) %all-to-all-start.5) | async-done | bytes 639008 | tf_op jit(solution)/shard_map/all_to_all | solution.py:550
  681.5 38.7 %all_to_all.55 = bf16[8,32,2816]{2,1,0:T(8,128)(2,1)} all-to-all(bf16[8,32,2816]{2,1,0:T(8,128)(2,1)S(1)} %bitcast_dynamic-update-slice_fusion), channel_id=1, replica_groups=mesh['dp'=4,'ctx'=8] {'ctx'}, dimensions={0} | all-to-all | bytes 2883584 | tf_op jit(solution)/shard_map/all_to_all | solution.py:799
  722.0 7.0 fusion.145
  738.9 6.7 all-to-all-done.8
  750.7 14.1 %all-gather.14.cloned.1.call-done = bf16[1024,2816]{1,0:T(8,128)(2,1)} async-done(((bf16[256,2816]{1,0:T(8,128)(2,1)}), bf16[1024,2816]{1,0:T(8,128)(2,1)}) %all-gather.14.cloned.1.call-update) | async-done | bytes 5767184 | tf_op jit(solution)/shard_map/all_gather | solution.py:576
  764.8 13.0 %select_reduce_fusion = (f32[]{:T(128)}, f32[1024,1024]{1,0:T(8,128)}) fusion(bf16[1024,2816]{1,0:T(8,128)(2,1)} %all-gather.14.cloned.1.call-done), kind=kOutput, calls=%fused_computation.14 | convolution fusion | flops 5908725760 | bytes 9961476 | tf_op jit(solution)/shard_map/dot_general | solution.py:50
  778.5 7.3 add_convert_fusion.1
  802.4 7.0 fusion.9
  809.4 6.2 all-to-all-start.7
  815.6 5.5 fusion.66
  825.0 22.7 %all-to-all-done.7 = bf16[8,32,2816]{2,1,0:T(8,128)(2,1)S(1)} async-done(((bf16[8,32,2816]{2,1,0:T(8,128)(2,1)}), bf16[8,32,2816]{2,1,0:T(8,128)(2,1)S(1)}, u32[]{:S(2)}, u32[]{:S(2)}) %all-to-all-start.7) | async-done | bytes 1441824 | tf_op jit(solution)/shard_map/all_to_all | solution.py:801
  (328 shorter events, 229.5 us)
Async XLA Ops:
  7.2 87.2 %all-gather.6.cloned.1.call-start = ((), (), s32[]{:S(2)}) async-start(), calls=%async_computation.10 | async-start | bytes 9732096 | tf_op jit(solution)/shard_map/all_gather | solution.py:658
  11.8 82.8 %copy-start.45 = (f32[26892]{0:T(1024)S(1)}, f32[26892]{0:T(1024)}, u32[]{:S(2)}) copy-start(f32[26892]{0:T(1024)} %param.38) | copy-start | bytes 322708
  11.8 83.4 %copy-start.4 = (bf16[1,128,1024]{2,1,0:T(8,128)(2,1)S(1)}, bf16[1,128,1024]{2,1,0:T(8,128)(2,1)}, u32[]{:S(2)}) copy-start(bf16[1,128,1024]{2,1,0:T(8,128)(2,1)} %param.20) | copy-start | bytes 786436
  11.8 248.4 %all-gather.8.cloned.1.call-start = ((), (), s32[]{:S(2)}) async-start(), calls=%async_computation.11 | async-start | bytes 21086208 | tf_op jit(solution)/shard_map/all_gather | solution.py:660
  94.5 397.8 %all-gather.10.cloned.1.call-start = ((), (), s32[]{:S(2)}) async-start(), calls=%async_computation.12 | async-start | bytes 4718592 | tf_op jit(solution)/shard_map/all_gather | solution.py:708
  101.4 6.7 collective-permute-start
  139.3 21.4 %collective-permute-start.1 = (bf16[6,128,256]{2,1,0:T(8,128)(2,1)S(1)}, bf16[6,128,256]{2,1,0:T(8,128)(2,1)S(1)}, u32[]{:S(2)}, u32[]{:S(2)}) collective-permute-start(bf16[6,128,256]{2,1,0:T(8,128)(2,1)S(1)} %slice.416), channel_id=1, source_target_pairs={{0,1},{1,2},{2,3},{3,4},{4,5},{5,6},{6,7},{8,9},{9,10},{10,11},{11... | collective-permute-start | bytes 1179656 | tf_op jit(solution)/shard_map/ppermute | solution.py:38
  144.3 24.9 %collective-permute-start.2 = (bf16[6,128,128]{2,1,0:T(8,128)(2,1)S(1)}, bf16[6,128,128]{2,1,0:T(8,128)(2,1)S(1)}, u32[]{:S(2)}, u32[]{:S(2)}) collective-permute-start(bf16[6,128,128]{2,1,0:T(8,128)(2,1)S(1)} %slice.417), channel_id=1, source_target_pairs={{0,1},{1,2},{2,3},{3,4},{4,5},{5,6},{6,7},{8,9},{9,10},{10,11},{11... | collective-permute-start | bytes 589832 | tf_op jit(solution)/shard_map/ppermute | solution.py:38
  162.5 12.6 %collective-permute-start.3 = (bf16[6,128,256]{2,1,0:T(8,128)(2,1)S(1)}, bf16[6,128,256]{2,1,0:T(8,128)(2,1)S(1)}, u32[]{:S(2)}, u32[]{:S(2)}) collective-permute-start(bf16[6,128,256]{2,1,0:T(8,128)(2,1)S(1)} %get-tuple-element.134), channel_id=1, source_target_pairs={{0,2},{1,3},{2,4},{3,5},{4,6},{5,7},{8,10},{9,11},{10,12},{11,13},... | collective-permute-start | bytes 1179656 | tf_op jit(solution)/shard_map/ppermute | solution.py:38
  170.5 15.4 %collective-permute-start.5 = (bf16[6,128,128]{2,1,0:T(8,128)(2,1)S(1)}, bf16[6,128,128]{2,1,0:T(8,128)(2,1)S(1)}, u32[]{:S(2)}, u32[]{:S(2)}) collective-permute-start(bf16[6,128,128]{2,1,0:T(8,128)(2,1)S(1)} %get-tuple-element.132), channel_id=1, source_target_pairs={{0,2},{1,3},{2,4},{3,5},{4,6},{5,7},{8,10},{9,11},{10,12},{11,13},... | collective-permute-start | bytes 589832 | tf_op jit(solution)/shard_map/ppermute | solution.py:38
  176.3 51.6 %collective-permute-start.4 = (bf16[6,128,256]{2,1,0:T(8,128)(2,1)}, bf16[6,128,256]{2,1,0:T(8,128)(2,1)}, u32[]{:S(2)}, u32[]{:S(2)}) collective-permute-start(bf16[6,128,256]{2,1,0:T(8,128)(2,1)} %fusion.55), channel_id=1, source_target_pairs={{0,1},{1,2},{2,3},{3,4},{4,5},{5,6},{6,7},{8,9},{9,10},{10,11},{11... | collective-permute-start | bytes 1179656 | tf_op jit(solution)/shard_map/ppermute | solution.py:38
  182.3 45.7 %collective-permute-start.7 = (bf16[6,128,256]{2,1,0:T(8,128)(2,1)}, bf16[6,128,256]{2,1,0:T(8,128)(2,1)}, u32[]{:S(2)}, u32[]{:S(2)}) collective-permute-start(bf16[6,128,256]{2,1,0:T(8,128)(2,1)} %fusion.55), channel_id=1, source_target_pairs={{0,5},{1,6},{2,7},{8,13},{9,14},{10,15},{16,21},{17,22},{18,23},{2... | collective-permute-start | bytes 1179656 | tf_op jit(solution)/shard_map/ppermute | solution.py:38
  186.9 41.0 %collective-permute-start.6 = (bf16[6,128,128]{2,1,0:T(8,128)(2,1)}, bf16[6,128,128]{2,1,0:T(8,128)(2,1)}, u32[]{:S(2)}, u32[]{:S(2)}) collective-permute-start(bf16[6,128,128]{2,1,0:T(8,128)(2,1)} %convolution_convert_fusion.1), channel_id=1, source_target_pairs={{0,1},{1,2},{2,3},{3,4},{4,5},{5,6},{6,7},{8,9},{9,10},{10,11},{11... | collective-permute-start | bytes 589832 | tf_op jit(solution)/shard_map/ppermute | solution.py:38
  265.2 322.8 %all-gather.12.cloned.1.call-start = ((), (), s32[]{:S(2)}) async-start(), calls=%async_computation.13 | async-start | bytes 4718592 | tf_op jit(solution)/shard_map/all_gather | solution.py:709
  314.2 18.7 %collective-permute-start.8 = (bf16[6,128,256]{2,1,0:T(8,128)(2,1)S(1)}, bf16[6,128,256]{2,1,0:T(8,128)(2,1)S(1)}, u32[]{:S(2)}, u32[]{:S(2)}) collective-permute-start(bf16[6,128,256]{2,1,0:T(8,128)(2,1)S(1)} %convert_element_type.328), channel_id=1, source_target_pairs={{1,0},{2,1},{3,2},{4,3},{5,4},{6,5},{7,6},{9,8},{10,9},{11,10},{12... | collective-permute-start | bytes 1179656 | tf_op jit(solution)/shard_map/ppermute | solution.py:38
  319.0 26.4 %collective-permute-start.9 = (bf16[6,128,128]{1,2,0:T(8,128)(2,1)S(1)}, bf16[6,128,128]{1,2,0:T(8,128)(2,1)S(1)}, u32[]{:S(2)}, u32[]{:S(2)}) collective-permute-start(bf16[6,128,128]{1,2,0:T(8,128)(2,1)S(1)} %slice_bitcast_fusion), channel_id=1, source_target_pairs={{1,0},{2,1},{3,2},{4,3},{5,4},{6,5},{7,6},{9,8},{10,9},{11,10},{12... | collective-permute-start | bytes 589832 | tf_op jit(solution)/shard_map/ppermute | solution.py:38
  334.4 22.2 %collective-permute-start.10 = (bf16[6,128,256]{2,1,0:T(8,128)(2,1)S(1)}, bf16[6,128,256]{2,1,0:T(8,128)(2,1)S(1)}, u32[]{:S(2)}, u32[]{:S(2)}) collective-permute-start(bf16[6,128,256]{2,1,0:T(8,128)(2,1)S(1)} %get-tuple-element.141), channel_id=1, source_target_pairs={{2,0},{3,1},{4,2},{5,3},{6,4},{7,5},{10,8},{11,9},{12,10},{13,11},... | collective-permute-start | bytes 1179656 | tf_op jit(solution)/shard_map/ppermute | solution.py:38
  346.9 13.9 %collective-permute-start.12 = (bf16[6,128,128]{2,1,0:T(8,128)(2,1)S(1)}, bf16[6,128,128]{2,1,0:T(8,128)(2,1)S(1)}, u32[]{:S(2)}, u32[]{:S(2)}) collective-permute-start(bf16[6,128,128]{2,1,0:T(8,128)(2,1)S(1)} %get-tuple-element.139), channel_id=1, source_target_pairs={{2,0},{3,1},{4,2},{5,3},{6,4},{7,5},{10,8},{11,9},{12,10},{13,11},... | collective-permute-start | bytes 589832 | tf_op jit(solution)/shard_map/ppermute | solution.py:38
  357.1 25.6 %collective-permute-start.11 = (bf16[6,128,256]{2,1,0:T(8,128)(2,1)S(1)}, bf16[6,128,256]{2,1,0:T(8,128)(2,1)S(1)}, u32[]{:S(2)}, u32[]{:S(2)}) collective-permute-start(bf16[6,128,256]{2,1,0:T(8,128)(2,1)S(1)} %fusion.56), channel_id=1, source_target_pairs={{1,0},{2,1},{3,2},{4,3},{5,4},{6,5},{7,6},{9,8},{10,9},{11,10},{12... | collective-permute-start | bytes 1179656 | tf_op jit(solution)/shard_map/ppermute | solution.py:38
  359.0 23.7 %collective-permute-start.14 = (bf16[6,128,256]{2,1,0:T(8,128)(2,1)S(1)}, bf16[6,128,256]{2,1,0:T(8,128)(2,1)S(1)}, u32[]{:S(2)}, u32[]{:S(2)}) collective-permute-start(bf16[6,128,256]{2,1,0:T(8,128)(2,1)S(1)} %fusion.56), channel_id=1, source_target_pairs={{5,0},{6,1},{7,2},{13,8},{14,9},{15,10},{21,16},{22,17},{23,18},{2... | collective-permute-start | bytes 1179656 | tf_op jit(solution)/shard_map/ppermute | solution.py:38
  361.1 21.6 %collective-permute-start.13 = (bf16[6,128,128]{2,1,0:T(8,128)(2,1)S(1)}, bf16[6,128,128]{2,1,0:T(8,128)(2,1)S(1)}, u32[]{:S(2)}, u32[]{:S(2)}) collective-permute-start(bf16[6,128,128]{2,1,0:T(8,128)(2,1)S(1)} %convolution_convert_fusion), channel_id=1, source_target_pairs={{1,0},{2,1},{3,2},{4,3},{5,4},{6,5},{7,6},{9,8},{10,9},{11,10},{12... | collective-permute-start | bytes 589832 | tf_op jit(solution)/shard_map/ppermute | solution.py:38
  429.9 5.9 collective-permute-start.15
  438.2 46.8 %all-to-all-start = ((bf16[8,128,576]{1,2,0:T(8,128)(2,1)}), bf16[8,128,576]{1,2,0:T(8,128)(2,1)}, u32[]{:S(2)}, u32[]{:S(2)}) async-start(bf16[8,128,576]{1,2,0:T(8,128)(2,1)} %bitcast.9), calls=%async_computation | async-start | bytes 2359296 | tf_op jit(solution)/shard_map/all_to_all | solution.py:734
  485.1 91.2 %all-to-all-start.3 = ((bf16[8,128,1248]{1,2,0:T(8,128)(2,1)}), bf16[8,128,1248]{1,2,0:T(8,128)(2,1)}, u32[]{:S(2)}, u32[]{:S(2)}) async-start(bf16[8,128,1248]{1,2,0:T(8,128)(2,1)} %pad_maximum_fusion), calls=%async_computation.3 | async-start | bytes 5111808 | tf_op jit(solution)/shard_map/all_to_all | solution.py:718
  576.3 19.5 %all-to-all-start.1 = ((bf16[4,256,576]{1,2,0:T(8,128)(2,1)}), bf16[4,256,576]{1,2,0:T(8,128)(2,1)S(1)}, u32[]{:S(2)}, u32[]{:S(2)}) async-start(bf16[4,256,576]{1,2,0:T(8,128)(2,1)} %bitcast.173), calls=%async_computation.1 | async-start | bytes 2359296 | tf_op jit(solution)/shard_map/all_to_all | solution.py:545
  597.0 16.2 %all-to-all-start.2 = ((bf16[8,32,576]{2,1,0:T(8,128)(2,1)}), bf16[8,32,576]{2,1,0:T(8,128)(2,1)S(1)}, u32[]{:S(2)}, u32[]{:S(2)}) async-start(bf16[8,32,576]{2,1,0:T(8,128)(2,1)} %bitcast.10), calls=%async_computation.2 | async-start | bytes 655360 | tf_op jit(solution)/shard_map/all_to_all | solution.py:550
  613.2 35.2 %all-to-all-start.4 = ((bf16[4,256,1248]{1,2,0:T(8,128)(2,1)}), bf16[4,256,1248]{1,2,0:T(8,128)(2,1)}, u32[]{:S(2)}, u32[]{:S(2)}) async-start(bf16[4,256,1248]{1,2,0:T(8,128)(2,1)} %bitcast.174), calls=%async_computation.4 | async-start | bytes 5111808 | tf_op jit(solution)/shard_map/all_to_all | solution.py:545
  652.0 20.3 %all-to-all-start.5 = ((bf16[8,32,1248]{2,1,0:T(8,128)(2,1)}), bf16[8,32,1248]{2,1,0:T(8,128)(2,1)S(1)}, u32[]{:S(2)}, u32[]{:S(2)}) async-start(bf16[8,32,1248]{2,1,0:T(8,128)(2,1)} %bitcast.19), calls=%async_computation.5 | async-start | bytes 1310720 | tf_op jit(solution)/shard_map/all_to_all | solution.py:550
  656.6 108.2 %all-gather.14.cloned.1.call-start = ((), (), s32[]{:S(2)}) async-start(), calls=%async_computation.14 | async-start | bytes 7208960 | tf_op jit(solution)/shard_map/all_gather | solution.py:576
  735.2 10.4 %all-to-all-start.8 = ((f32[32,1,896]{2,1,0:T(1,128)}), f32[32,1,896]{2,1,0:T(1,128)S(1)}, u32[]{:S(2)}, u32[]{:S(2)}) async-start(f32[32,1,896]{2,1,0:T(1,128)} %bitcast.53), calls=%async_computation.8 | async-start | bytes 229376 | tf_op jit(solution)/shard_map/all_to_all | solution.py:564
  746.4 62.9 %all-to-all-start.9 = ((f32[32,1,896]{2,1,0:T(1,128)}), f32[32,1,896]{2,1,0:T(1,128)}, u32[]{:S(2)}, u32[]{:S(2)}) async-start(f32[32,1,896]{2,1,0:T(1,128)} %broadcast_in_dim.41), calls=%async_computation.9 | async-start | bytes 229376 | tf_op jit(solution)/shard_map/all_to_all | solution.py:566
  809.4 38.3 %all-to-all-start.7 = ((bf16[8,32,2816]{2,1,0:T(8,128)(2,1)}), bf16[8,32,2816]{2,1,0:T(8,128)(2,1)S(1)}, u32[]{:S(2)}, u32[]{:S(2)}) async-start(bf16[8,32,2816]{2,1,0:T(8,128)(2,1)} %bitcast.184), calls=%async_computation.7 | async-start | bytes 2883584 | tf_op jit(solution)/shard_map/all_to_all | solution.py:801
  (72 other events, 882.6 us)
Sparse Core Ops, SparseCore 0:
  11.9 82.4 all-gather.5
  97.5 162.7 all-gather.7
  265.3 89.7 all-gather.9
  434.1 129.7 all-gather.11
  720.4 44.3 all-gather.13

commit v2 on v1

--- a/solution.py
+++ b/solution.py
@@ -4,7 +4,7 @@
 import jax.numpy as jnp
 from jax import lax
 from jax.experimental import pallas as pl
-from jax.sharding import PartitionSpec as P
+from jax.sharding import Mesh, PartitionSpec as P
 
 D = 1024
 H = 6
@@ -17,7 +17,11 @@
 VD = 1536
 QKV = 3072
 FF = 2816
-BOTH_AXES = ("dp", "ctx")
+DP_AXES = ("y", "core")
+CTX_AXES = ("z", "x")
+ALL_AXES = ("y", "core", "z", "x")
+NEAR_AXES = ("core", "y", "x")
+CHIP_AXES = ("y", "x")
 
 
 highest_precision = lax.Precision.HIGHEST
@@ -60,10 +64,6 @@
 
 def root_norm(values, gain):
     return values * lax.rsqrt(jnp.mean(values * values, axis=-1, keepdims=True) + eps_norm) * gain
-
-
-def unit_rows(values):
-    return values * lax.rsqrt(jnp.sum(values * values, axis=-1, keepdims=True) + eps_unit)
 
 
 def unpack_small(packed):
@@ -97,13 +97,24 @@
     return jax.nn.silu(summed)
 
 
+def split_low(value):
+    high = value.astype(jnp.bfloat16)
+    return high, (value - high.astype(jnp.float32)).astype(jnp.bfloat16)
+
+
 def raw_dot(left, right, left_dim, right_dim):
-    return lax.dot_general(
-        left,
-        right,
-        (((left_dim,), (right_dim,)), ((), ())),
-        precision=highest_precision,
-        preferred_element_type=jnp.float32,
+    def product(first, second):
+        return lax.dot_general(
+            first,
+            second,
+            (((left_dim,), (right_dim,)), ((), ())),
+            preferred_element_type=jnp.float32,
+        )
+
+    left_high, left_rest = split_low(left)
+    right_high, right_rest = split_low(right)
+    return product(left_high, right_high) + (
+        product(left_high, right_rest) + product(left_rest, right_high)
     )
 
 
@@ -196,7 +207,7 @@
 def decay_parts(log_wide):
     rows = log_wide.shape[0]
     at, source = position_pair(rows, rows)
-    same, inclusive, strictly = head_masks(rows)
+    same, inclusive, _ = head_masks(rows)
     growth = jnp.exp(mm(inclusive.astype(jnp.float32), log_wide))
     tail = jnp.exp(mm((same & ~inclusive).astype(jnp.float32), log_wide))
     differ = mm(inclusive.astype(jnp.float32), jnp.where(at > source, log_wide, 0.0))
@@ -216,7 +227,7 @@
 
 
 def lower_system(keys, beta_wide, within):
-    unused_same, unused_inclusive, strictly = head_masks(keys.shape[0])
+    _, _, strictly = head_masks(keys.shape[0])
     return jnp.where(strictly, beta_wide * within * mm_nt(keys, keys), 0.0)
 
 
@@ -226,7 +237,7 @@
     )
 
 
-def head_terms(queries, keys, values, beta_wide, log_wide):
+def head_terms(keys, values, beta_wide, log_wide):
     growth, tail, within = decay_parts(log_wide)
     lower = lower_system(keys, beta_wide, within)
     inverse = unit_inverse(lower)
@@ -273,7 +284,7 @@
 
 
 def head_whole(inverse, state, queries, keys, values, beta_wide, log_wide, gate_pre, head_gain):
-    growth, tail, within = decay_parts(log_wide)
+    growth, _, within = decay_parts(log_wide)
     lower = lower_system(keys, beta_wide, within)
     both = solved(lower, solve_targets(keys, values, beta_wide, growth), inverse)
     return head_outputs(queries, keys, log_wide, both, gate_pre, head_gain, state)
@@ -299,10 +310,10 @@
 
 
 def terms_kernel(query_ref, key_ref, value_ref, rates_ref, inverse_ref, both_ref, map_ref):
-    queries, keys, beta_wide, log_wide = head_inputs(
+    _, keys, beta_wide, log_wide = head_inputs(
         query_ref[...], key_ref[...], rates_ref[...], pl.program_id(0)
     )
-    inverse, both, state = head_terms(queries, keys, value_ref[...], beta_wide, log_wide)
+    inverse, both, state = head_terms(keys, value_ref[...], beta_wide, log_wide)
     inverse_ref[...] = inverse
     both_ref[...] = both
     map_ref[0] = state
@@ -311,10 +322,10 @@
 def outputs_kernel(
     query_ref, key_ref, rates_ref, both_ref, gate_ref, gain_ref, state_ref, mixed_ref
 ):
-    queries, keys, beta_wide, log_wide = head_inputs(
+    queries, keys, _, log_wide = head_inputs(
         query_ref[...], key_ref[...], rates_ref[...], pl.program_id(0)
     )
-    mixed, unused = head_outputs(
+    mixed, _ = head_outputs(
         queries, keys, log_wide, both_ref[...], gate_ref[...], gain_ref[...], state_ref[0]
     )
     mixed_ref[...] = mixed.astype(mixed_ref.dtype)
@@ -323,7 +334,7 @@
 def state_kernel(
     query_ref, key_ref, rates_ref, both_ref, gate_ref, gain_ref, state_ref, grad_ref, out_ref
 ):
-    queries, keys, beta_wide, log_wide = head_inputs(
+    queries, keys, _, log_wide = head_inputs(
         query_ref[...], key_ref[...], rates_ref[...], pl.program_id(0)
     )
 
@@ -332,7 +343,7 @@
             queries, keys, log_wide, both_ref[...], gate_ref[...], gain_ref[...], state
         )[0]
 
-    unused, back = jax.vjp(from_state, state_ref[0])
+    _, back = jax.vjp(from_state, state_ref[0])
     out_ref[0] = back(grad_ref[...])[0]
 
 
@@ -363,7 +374,7 @@
             inverse, state, queries, keys, values, beta_wide, log_wide, gate_pre, gain
         )
 
-    unused, back = jax.vjp(
+    _, back = jax.vjp(
         whole,
         query_ref[...],
         key_ref[...],
@@ -512,11 +523,11 @@
 
 
 def sent_low(value, steps):
-    return passed_along(value.astype(jnp.bfloat16), "ctx", steps).astype(jnp.float32)
+    return passed_along(value.astype(jnp.bfloat16), CTX_AXES, steps).astype(jnp.float32)
 
 
 def window_maps(trans, direction):
-    count = lax.axis_size("ctx")
+    count = lax.axis_size(CTX_AXES)
     levels = [trans]
     window = 1
     while 2 * window < count:
@@ -528,7 +539,8 @@
 def carried_state(levels, near_trans, offset, direction):
     window = 1
     for trans in levels[:-1]:
-        offset = offset + map_times(trans, sent_low(offset, direction * window))
+        before = sent_low(offset, direction * window)
+        offset = offset + map_times(trans, before)
         window = 2 * window
     near = sent_low(offset, direction)
     far = sent_low(offset, direction * (window + 1))
@@ -540,15 +552,43 @@
     return jnp.transpose(split, (1, 0, 2))
 
 
+def gathered_near(rows):
+    chips = lax.axis_size(CHIP_AXES)
+    own = lax.all_to_all(
+        jnp.broadcast_to(rows[None], (chips,) + rows.shape),
+        CHIP_AXES,
+        split_axis=0,
+        concat_axis=0,
+        tiled=True,
+    )
+    own = own.reshape(-1, rows.shape[1])
+    other = lax.ppermute(own, "core", [(0, 1), (1, 0)])
+    first = lax.axis_index("core") == 0
+    return jnp.concatenate([jnp.where(first, own, other), jnp.where(first, other, own)], axis=0)
+
+
 def summed_rows(terms, columns):
-    dp_count, ctx_count = lax.axis_size("dp"), lax.axis_size("ctx")
-    parts = lax.all_to_all(
-        terms.reshape(dp_count, D // dp_count, columns), "dp", split_axis=0, concat_axis=0, tiled=True
-    )
-    block = jnp.sum(parts.astype(jnp.float32), axis=0).astype(jnp.bfloat16)
-    rows = D // (dp_count * ctx_count)
+    y_count, core_count, far_count, x_count = (lax.axis_size(axis) for axis in ALL_AXES)
+    near_count = lax.axis_size(NEAR_AXES)
+    rows = D // far_count
+    split = terms.reshape(
+        y_count, core_count, far_count, x_count, rows // near_count, columns
+    )
+    split = jnp.transpose(split, (2, 1, 0, 3, 4, 5)).reshape(far_count, rows, columns)
+    mine = lax.axis_index("z")
+    total = lax.dynamic_index_in_dim(split, mine, 0, keepdims=False).astype(jnp.float32)
+    for step in range(1, far_count):
+        pairs = [(source, (source + step) % far_count) for source in range(far_count)]
+        leaving = lax.dynamic_index_in_dim(split, (mine + step) % far_count, 0, keepdims=False)
+        arrived = lax.ppermute(leaving, "z", pairs)
+        total = total + arrived.astype(jnp.float32)
+    block = total.astype(jnp.bfloat16)
     return lax.all_to_all(
-        block.reshape(ctx_count, rows, columns), "ctx", split_axis=0, concat_axis=0, tiled=True
+        block.reshape(near_count, rows // near_count, columns),
+        NEAR_AXES,
+        split_axis=0,
+        concat_axis=0,
+        tiled=True,
     )
 
 
@@ -558,12 +598,12 @@
 
 
 def summed_everywhere(vector):
-    count = lax.axis_size("dp") * lax.axis_size("ctx")
+    count = lax.axis_size(ALL_AXES)
     chunk = -(-vector.shape[0] // (count * 128)) * 128
     padded = jnp.pad(vector, (0, count * chunk - vector.shape[0])).reshape(count, chunk)
-    parts = lax.all_to_all(padded, BOTH_AXES, split_axis=0, concat_axis=0, tiled=True)
+    parts = lax.all_to_all(padded, ALL_AXES, split_axis=0, concat_axis=0, tiled=True)
     total = jnp.broadcast_to(jnp.sum(parts, axis=0)[None], (count, chunk))
-    whole = lax.all_to_all(total, BOTH_AXES, split_axis=0, concat_axis=0, tiled=True)
+    whole = lax.all_to_all(total, ALL_AXES, split_axis=0, concat_axis=0, tiled=True)
     return whole.reshape(-1)[: vector.shape[0]]
 
 
@@ -573,7 +613,7 @@
 
 def orthogonal_rows(raw_rows):
     low = jnp.bfloat16
-    raw = lax.all_gather(raw_rows, "dp", axis=0, tiled=True)
+    raw = lax.all_gather(raw_rows, DP_AXES, axis=0, tiled=True)
     gram_raw = times_transposed(raw, raw)
     norm = jnp.sqrt(jnp.trace(gram_raw))
     scale = 1.0 / (norm + eps_muon)
@@ -587,7 +627,7 @@
             turned = poly_one * gram + square_times(factor, gram_low)
             gram = poly_one * turned + square_times(turned.astype(low), factor)
     rows = raw_rows.shape[0]
-    start = lax.axis_index("dp") * rows
+    start = lax.axis_index(DP_AXES) * rows
     last = factors[-1]
     at = lax.broadcasted_iota(jnp.int32, (rows, D), 0) + start
     own = at == lax.broadcasted_iota(jnp.int32, (rows, D), 1)
@@ -647,7 +687,8 @@
         swiglu_down_moment,
     )
     low = jnp.bfloat16
-    ctx_count = lax.axis_size("ctx")
+    ctx_count = lax.axis_size(CTX_AXES)
+    near_count = lax.axis_size(NEAR_AXES)
     gain_one, gain_two, head_gain, conv_taps, decay_log, decay_bias, route_weight = unpack_small(
         small_params
     )
@@ -655,9 +696,9 @@
     rim_rows = CONV - 1
     front_rows = jnp.concatenate([member.astype(low) for member in weights_in[:4]], axis=1)
     back_rows = jnp.concatenate([member.astype(low) for member in weights_in[4:]], axis=1)
-    front_full = lax.all_gather(front_rows, BOTH_AXES, axis=0, tiled=True)
+    front_full = lax.all_gather(front_rows, ALL_AXES, axis=0, tiled=True)
     front_full, back_rows = lax.optimization_barrier((front_full, back_rows))
-    back_full = lax.all_gather(back_rows, BOTH_AXES, axis=0, tiled=True)
+    back_full = lax.all_gather(back_rows, ALL_AXES, axis=0, tiled=True)
     output_full = back_full[:, :VD]
     gate_up_full = back_full[:, VD : VD + 2 * FF]
     down_full = back_full[:, VD + 2 * FF :]
@@ -665,11 +706,14 @@
     inputs_full = tokens_in[0].astype(jnp.float32)
     normed_one, norm_one_back = jax.vjp(root_norm, inputs_full, gain_one)
     normed_one_low = normed_one.astype(low)
+    upstream_full = upstream[0]
+    upstream_low = upstream_full.astype(low)
+    early_left = gathered_near(jnp.concatenate([normed_one_low, upstream_low], axis=1))
     projected = matmul(normed_one_low, front_full)
     pre_proj = projected[:, :QKV]
     route_pre = matmul(normed_one_low, route_low)
     prior_rim = passed_along(
-        pre_proj[pre_proj.shape[0] - rim_rows :].astype(low), "ctx", 1
+        pre_proj[pre_proj.shape[0] - rim_rows :].astype(low), CTX_AXES, 1
     ).astype(jnp.float32)
     extended = jnp.concatenate([prior_rim, pre_proj], axis=0)
     conv_out, conv_back = jax.vjp(conv_silu, extended, conv_taps)
@@ -691,8 +735,6 @@
     middle = (gate_act * sigma * up_act).astype(low)
     block_out = residual_one + times_transposed(middle, down_full)
 
-    upstream_full = upstream[0]
-    upstream_low = upstream_full.astype(low)
     grad_middle = matmul(upstream_low, down_full)
     grad_gate = (grad_middle * up_act * sigma * (1.0 + gate_act * (1.0 - sigma))).astype(low)
     grad_up = (grad_middle * gate_act * sigma).astype(low)
@@ -703,28 +745,22 @@
     grad_residual_low = grad_residual.astype(low)
     grad_mixed = matmul(grad_residual_low, output_full)
 
-    early_left = jnp.concatenate([normed_one_low, upstream_low], axis=1)
-    early_left, unused_full = lax.optimization_barrier((early_left, back_full))
-    early_left = lax.all_gather(early_left, "ctx", axis=0, tiled=True)
-    late_left = lax.all_gather(
-        jnp.concatenate([normed_two_low, grad_residual_low], axis=1), "ctx", axis=0, tiled=True
-    )
-
+    late_left = gathered_near(jnp.concatenate([normed_two_low, grad_residual_low], axis=1))
+    back_columns = jnp.concatenate(
+        [swap_columns(member, near_count) for member in (mixed_low, grad_gate_up, middle)], axis=2
+    )
+    back_columns = lax.all_to_all(back_columns, NEAR_AXES, split_axis=0, concat_axis=0, tiled=True)
     state_grad = run_state(conv_out, rates, both, projected, gain_row, state_in, grad_mixed)
     state_out_grad = carried_state(back_levels, back_near, state_grad, -1)
-    back_columns = jnp.concatenate(
-        [swap_columns(member, ctx_count) for member in (mixed_low, grad_gate_up, middle)], axis=2
-    )
-    back_columns = lax.all_to_all(back_columns, "ctx", split_axis=0, concat_axis=0, tiled=True)
-
-    query_grad, key_grad, value_grad, rates_grad, grad_gate_pre_low, gain_grads = run_backward(
+
+    (query_grad, key_grad, value_grad, rates_grad, grad_gate_pre_low, gain_grads) = run_backward(
         inverse, state_in, conv_out, rates, projected, gain_row, grad_mixed, state_out_grad
     )
     grad_conv = jnp.concatenate([query_grad, key_grad, value_grad], axis=1)
     grad_extended, grad_conv_taps = conv_back(grad_conv)
     grad_route_pre, grad_decay_log, grad_decay_bias = rates_back(rates_grad)
     grad_head_gain = jnp.sum(gain_grads, axis=(0, 1))
-    back_rim = passed_along(shortened(grad_extended[:rim_rows]), "ctx", -1)
+    back_rim = passed_along(shortened(grad_extended[:rim_rows]), CTX_AXES, -1)
     grad_pre = grad_extended[rim_rows:]
     split_row = grad_pre.shape[0] - rim_rows
     grad_pre = jnp.concatenate([grad_pre[:split_row], grad_pre[split_row:] + back_rim], axis=0)
@@ -732,10 +768,14 @@
     grad_route_low = grad_route_pre.astype(low)
 
     front_columns = lax.all_to_all(
-        swap_columns(grad_front_low, ctx_count), "ctx", split_axis=0, concat_axis=0, tiled=True
-    )
-    count_rows = ctx_count * grad_front_low.shape[0]
-    widths = (VD // ctx_count, 2 * FF // ctx_count, FF // ctx_count)
+        swap_columns(grad_front_low, near_count),
+        NEAR_AXES,
+        split_axis=0,
+        concat_axis=0,
+        tiled=True,
+    )
+    count_rows = near_count * grad_front_low.shape[0]
+    widths = (VD // near_count, 2 * FF // near_count, FF // near_count)
     back_columns = back_columns.reshape(count_rows, sum(widths))
     piece_out = back_columns[:, : widths[0]]
     piece_gate_up = back_columns[:, widths[0] : widths[0] + widths[1]]
@@ -749,7 +789,7 @@
         axis=1,
     )
     back_blocks = summed_rows(back_terms, sum(widths))
-    front_width = grad_front_low.shape[1] // ctx_count
+    front_width = grad_front_low.shape[1] // near_count
     front_terms = transposed_times(
         early_left[:, :D], front_columns.reshape(count_rows, front_width)
     ).astype(low)
@@ -796,10 +836,10 @@
             for owner in range(ctx_count)
         ]
     )
-    received = lax.all_to_all(outgoing, "ctx", split_axis=0, concat_axis=0, tiled=True)
+    received = lax.all_to_all(outgoing, CTX_AXES, split_axis=0, concat_axis=0, tiled=True)
     ortho = orthogonal_rows(received.reshape(-1, FF))
     returned = lax.all_to_all(
-        ortho.reshape(received.shape), "ctx", split_axis=0, concat_axis=0, tiled=True
+        ortho.reshape(received.shape), CTX_AXES, split_axis=0, concat_axis=0, tiled=True
     )
     weights_new = []
     for index in range(8):
@@ -828,58 +868,12 @@
 
 
 def solution(mesh):
-    in_specs = (
-        P("dp", "ctx", None),
-        P("dp", "ctx", None),
-        P(("dp", "ctx"), None),
-        P(("dp", "ctx"), None),
-        P(("dp", "ctx"), None),
-        P(("dp", "ctx"), None),
-        P(("dp", "ctx"), None),
-        P(("dp", "ctx"), None),
-        P(("dp", "ctx"), None),
-        P(("dp", "ctx"), None),
-        P(("dp", "ctx"), None),
-        P(("dp", "ctx"), None),
-        P(("dp", "ctx"), None),
-        P(("dp", "ctx"), None),
-        P(("dp", "ctx"), None),
-        P(("dp", "ctx"), None),
-        P(("dp", "ctx"), None),
-        P(("dp", "ctx"), None),
-        P(),
-        P(),
-    )
-    out_specs = (
-        P("dp", "ctx", None),
-        P("dp", "ctx", None),
-        P(("dp", "ctx"), None),
-        P(("dp", "ctx"), None),
-        P(("dp", "ctx"), None),
-        P(("dp", "ctx"), None),
-        P(("dp", "ctx"), None),
-        P(("dp", "ctx"), None),
-        P(("dp", "ctx"), None),
-        P(("dp", "ctx"), None),
-        P(("dp", "ctx"), None),
-        P(("dp", "ctx"), None),
-        P(("dp", "ctx"), None),
-        P(("dp", "ctx"), None),
-        P(("dp", "ctx"), None),
-        P(("dp", "ctx"), None),
-        P(("dp", "ctx"), None),
-        P(("dp", "ctx"), None),
-        P(("dp", "ctx"), None),
-        P(("dp", "ctx"), None),
-        P(("dp", "ctx"), None),
-        P(("dp", "ctx"), None),
-        P(("dp", "ctx"), None),
-        P(("dp", "ctx"), None),
-        P(("dp", "ctx"), None),
-        P(("dp", "ctx"), None),
-        P(),
-        P(),
-        P(),
-        P(),
-    )
-    return jax.shard_map(local, mesh=mesh, in_specs=in_specs, out_specs=out_specs, check_vma=False)
+    dp_count, ctx_count = mesh.shape["dp"], mesh.shape["ctx"]
+    split_mesh = Mesh(mesh.devices.reshape(dp_count // 2, 2, ctx_count // 2, 2), ALL_AXES)
+    tokens, rows, copied = P(DP_AXES, CTX_AXES, None), P(ALL_AXES, None), P()
+    in_specs = (tokens,) * 2 + (rows,) * 16 + (copied,) * 2
+    out_specs = (tokens,) * 2 + (rows,) * 24 + (copied,) * 4
+
+    return jax.shard_map(
+        local, mesh=split_mesh, in_specs=in_specs, out_specs=out_specs, check_vma=False
+    )

time: 873 us -> 832 us (0.953)
  waiting for transfers between devices: 401 us -> 348 us
  Pallas kernels: 102 us -> 72.6 us
  local copies, waits for them, and re-layouts: 40.4 us -> 69 us
  other arithmetic: 46 us -> 63.8 us
    all_to_all x9, waiting for transfers between devices: 188 us -> 63.7 us  [the longest x1 22.7 us: local(): lax.all_to_all(ortho.reshape(received.shape), CTX_AXES, split_axis=0, con...]
    ppermute x0 -> x8, waiting for transfers between devices: none -> 56 us  [the longest x6 56 us: summed_rows(): arrived = lax.ppermute(leaving, 'z', pairs)]
    pallas_call x1, Pallas kernels: 37.8 us -> 24.7 us  [run_backward(): per_head(backward_kernel, [columns_of(rows, rows), matrix_of(DK, DV), nar...]
    all_gather x5 -> x3, waiting for transfers between devices: 110 us -> 120 us  [the longest x1 80.6 us: local(): front_full = lax.all_gather(front_rows, ALL_AXES, axis=0, tiled=True)]
  transfers between devices with their start and end apart: 30 -> 36, of which waited for: 22 -> 23; matrix products, arithmetic and copies ran while one was open for 20% -> 21% of each run, Pallas kernels for 12% -> 7%
where the time goes in v2:
time: 832 us; the launch traced here: 820 us
  waiting for transfers between devices  348 us (42%)
  matrix products  109 us (13%)
  starting transfers between devices  101 us (12%)
  Pallas kernels  72.6 us (9%)
  local copies, waits for them, and re-layouts  69 us (8%)
  other arithmetic  63.8 us (8%)
  blocking collectives  39.5 us (5%)
  between operations  16.4 us (2%)
    ppermute x16, waiting for transfers between devices, passed_along(): lax.ppermute(value, axis, [(source, source + steps) for source in range(f...  108 us
    all_gather x1, waiting for transfers between devices, local(): front_full = lax.all_gather(front_rows, ALL_AXES, axis=0, tiled=True)  80.6 us
    ppermute x6, waiting for transfers between devices, summed_rows(): arrived = lax.ppermute(leaving, 'z', pairs)  56 us
    ppermute x16, starting transfers between devices, passed_along(): lax.ppermute(value, axis, [(source, source + steps) for source in range(f...  53.7 us
    all_to_all x1, blocking collectives, local(): lax.all_to_all(outgoing, CTX_AXES, split_axis=0, concat_axis=0, tiled=True)  39.5 us
    dot_general x6, matrix products, times_transposed(): lax.dot_general(left, right, (((1,), (1,)), ((), ())), preferred_element_...  37.1 us
    dot_general x9, matrix products, square_times(): return jnp.dot(left, right, preferred_element_type=jnp.float32)  30.3 us
    all_gather x1, waiting for transfers between devices, local(): back_full = lax.all_gather(back_rows, ALL_AXES, axis=0, tiled=True)  25.4 us
  transfers between devices with their start and end apart: 36, of which 23 were waited for; matrix products, arithmetic and copies ran while one was open for 21% of the time, Pallas kernels for 7%

profile of v2, /device:TPU:8, one launch (start us, length us, event | category | flops | bytes accessed | tf_op | source)
XLA Modules:
  0.0 819.5 jit_solution(13052715554781852119)
XLA Ops:
  13.9 80.6 %all-gather.4.cloned.1.call-done = bf16[1024,4608]{1,0:T(8,128)(2,1)} async-done(((bf16[32,4608]{1,0:T(8,128)(2,1)}), bf16[1024,4608]{1,0:T(8,128)(2,1)}) %all-gather.4.cloned.1.call-update) | async-done | bytes 9437200 | tf_op jit(solution)/shard_map/all_gather | solution.py:699
  96.7 5.1 fusion.152.gate_ref
  110.9 21.8 %shard_map.427 = (f32[128,768]{1,0:T(8,128)}, f32[128,2304]{1,0:T(8,128)}, f32[6,128,384]{2,1,0:T(8,128)}) custom-call(f32[128,3072]{1,0:T(8,128)} %get-tuple-element.92.query_ref.key_ref.value_ref, f32[128,3072]{1,0:T(8,128)} %get-tuple-element.92.query_ref.key_ref.value_ref, f32[128,3072]{1,0:T(8,128)} %get-tuple-element.92.query_ref.key_ref.value_ref, ...), custom_call_target="tpu_custom_call" | custom-call | tf_op jit(solution)/shard_map/pallas_call | solution.py:426
  140.9 15.9 %collective-permute-done.1 = bf16[6,128,256]{2,1,0:T(8,128)(2,1)S(1)} collective-permute-done((bf16[6,128,256]{2,1,0:T(8,128)(2,1)S(1)}, bf16[6,128,256]{2,1,0:T(8,128)(2,1)S(1)}, u32[]{:S(2)}, u32[]{:S(2)}) %collective-permute-start.1) | collective-permute-done | bytes 393248 | tf_op jit(solution)/shard_map/ppermute | solution.py:42
  171.8 9.7 %collective-permute-start.4 = (bf16[6,128,256]{2,1,0:T(8,128)(2,1)S(1)}, bf16[6,128,256]{2,1,0:T(8,128)(2,1)S(1)}, u32[]{:S(2)}, u32[]{:S(2)}) collective-permute-start(bf16[6,128,256]{2,1,0:T(8,128)(2,1)S(1)} %fusion.59), channel_id=1, source_target_pairs={{0,1},{1,2},{2,3},{3,4},{4,5},{5,6},{6,7},{8,9},{9,10},{10,11},{11... | collective-permute-start | bytes 1179656 | tf_op jit(solution)/shard_map/ppermute | solution.py:42
  187.7 35.2 %collective-permute-done.6 = bf16[6,128,128]{2,1,0:T(8,128)(2,1)S(1)} collective-permute-done((bf16[6,128,128]{2,1,0:T(8,128)(2,1)S(1)}, bf16[6,128,128]{2,1,0:T(8,128)(2,1)S(1)}, u32[]{:S(2)}, u32[]{:S(2)}) %collective-permute-start.6) | collective-permute-done | bytes 196640 | tf_op jit(solution)/shard_map/ppermute | solution.py:42
  227.5 10.4 %shard_map.428 = bf16[128,1536]{1,0:T(8,128)(2,1)} custom-call(f32[128,3072]{1,0:T(8,128)} %get-tuple-element.92.query_ref.key_ref.value_ref, f32[128,3072]{1,0:T(8,128)} %get-tuple-element.92.query_ref.key_ref.value_ref, f32[128,12]{1,0:T(8,128)} %pad_maximum_fusion.17.rates_ref, f32[128,2304]{1,0:T(8,128)} %get-tuple-element.42.both_ref, ...), custom_call_target="tpu_custom_call" | custom-call | tf_op jit(solution)/shard_map/pallas_call | solution.py:457
  237.8 25.4 %all-gather.6.cloned.1.call-done = bf16[1024,9984]{1,0:T(8,128)(2,1)} async-done(((bf16[32,9984]{1,0:T(8,128)(2,1)}), bf16[1024,9984]{1,0:T(8,128)(2,1)}) %all-gather.6.cloned.1.call-update) | async-done | bytes 20447248 | tf_op jit(solution)/shard_map/all_gather | solution.py:701
  266.6 5.4 fusion.2
  277.1 7.9 multiply_reduce_fusion.4
  290.0 15.7 %shard_map.429 = f32[6,128,256]{2,1,0:T(8,128)} custom-call(f32[128,3072]{1,0:T(8,128)} %get-tuple-element.92.query_ref.key_ref.value_ref, f32[128,3072]{1,0:T(8,128)} %get-tuple-element.92.query_ref.key_ref.value_ref, f32[128,12]{1,0:T(8,128)} %pad_maximum_fusion.17.rates_ref, f32[128,2304]{1,0:T(8,128)} %get-tuple-element.42.both_ref, ...), custom_call_target="tpu_custom_call" | custom-call | tf_op jit(solution)/shard_map/pallas_call | solution.py:467
  315.1 5.9 collective-permute-done.8
  347.6 30.9 %collective-permute-done.13 = bf16[6,128,128]{2,1,0:T(8,128)(2,1)S(1)} collective-permute-done((bf16[6,128,128]{2,1,0:T(8,128)(2,1)S(1)}, bf16[6,128,128]{2,1,0:T(8,128)(2,1)S(1)}, u32[]{:S(2)}, u32[]{:S(2)}) %collective-permute-start.13) | collective-permute-done | bytes 196640 | tf_op jit(solution)/shard_map/ppermute | solution.py:42
  379.7 24.7 %shard_map.430 = (f32[128,768]{1,0:T(8,128)}, f32[128,768]{1,0:T(8,128)}, f32[128,1536]{1,0:T(8,128)}, f32[128,12]{1,0:T(8,128)}, bf16[128,1536]{1,0:T(8,128)(2,1)}, /*index=5*/f32[6,1,256]{2,1,0:T(1,128)}) custom-call(f32[128,768]{1,0:T(8,128)} %get-tuple-element.45.inverse_ref, f32[6,128,256]{2,1,0:T(8,128)} %convert_add_fusion.2.state_ref, ...), custom_call_target="tpu_custom_call" | custom-call | tf_op jit(solution)/shard_map/pallas_call | solution.py:478
  430.1 11.5 %collective-permute-done.15 = bf16[3,3072]{1,0:T(4,128)(2,1)S(1)} collective-permute-done((bf16[3,3072]{1,0:T(4,128)(2,1)S(1)}, bf16[3,3072]{1,0:T(4,128)(2,1)S(1)}, u32[]{:S(2)}, u32[]{:S(2)}) %collective-permute-start.15) | collective-permute-done | bytes 18464 | tf_op jit(solution)/shard_map/ppermute | solution.py:42
  457.6 7.9 all-to-all-done.1
  486.1 14.7 %all-to-all-done.4 = bf16[8,128,1248]{1,2,0:T(8,128)(2,1)} async-done(((bf16[8,128,1248]{1,2,0:T(8,128)(2,1)}), bf16[8,128,1248]{1,2,0:T(8,128)(2,1)}, u32[]{:S(2)}, u32[]{:S(2)}) %all-to-all-start.4) | async-done | bytes 2555936 | tf_op jit(solution)/shard_map/all_to_all | solution.py:752
  564.1 10.6 %collective-permute-done.23 = bf16[256,1248]{0,1:T(8,128)(2,1)S(1)} collective-permute-done((bf16[256,1248]{0,1:T(8,128)(2,1)}, bf16[256,1248]{0,1:T(8,128)(2,1)S(1)}, u32[]{:S(2)}, u32[]{:S(2)}) %collective-permute-start.23) | collective-permute-done | bytes 639008 | tf_op jit(solution)/shard_map/ppermute | solution.py:583
  575.0 25.7 %collective-permute-done.22 = bf16[256,1248]{0,1:T(8,128)(2,1)} collective-permute-done((bf16[256,1248]{0,1:T(8,128)(2,1)}, bf16[256,1248]{0,1:T(8,128)(2,1)}, u32[]{:S(2)}, u32[]{:S(2)}) %collective-permute-start.22) | collective-permute-done | bytes 639008 | tf_op jit(solution)/shard_map/ppermute | solution.py:583
  602.0 12.3 %collective-permute-done.21 = bf16[256,1248]{0,1:T(8,128)(2,1)} collective-permute-done((bf16[256,1248]{0,1:T(8,128)(2,1)}, bf16[256,1248]{0,1:T(8,128)(2,1)}, u32[]{:S(2)}, u32[]{:S(2)}) %collective-permute-start.21) | collective-permute-done | bytes 639008 | tf_op jit(solution)/shard_map/ppermute | solution.py:583
  623.8 8.2 all-to-all-done.5
  641.2 39.5 %all_to_all.55 = bf16[8,32,2816]{2,1,0:T(8,128)(2,1)} all-to-all(bf16[8,32,2816]{2,1,0:T(8,128)(2,1)S(1)} %bitcast_dynamic-update-slice_fusion), channel_id=1, replica_groups=mesh['y'=2,'core'=2,'z'=4,'x'=2] {'z','x'}, dimensions={0} | all-to-all | bytes 2883584 | tf_op jit(solution)/shard_map/all_to_all | solution.py:839
  682.6 7.1 fusion.153
  690.1 5.3 concatenate.60
  699.8 6.7 all-to-all-done.8
  711.5 13.6 %all-gather.8.cloned.1.call-done = bf16[1024,2816]{1,0:T(8,128)(2,1)} async-done(((bf16[256,2816]{1,0:T(8,128)(2,1)}), bf16[1024,2816]{1,0:T(8,128)(2,1)}) %all-gather.8.cloned.1.call-update) | async-done | bytes 5767184 | tf_op jit(solution)/shard_map/all_gather | solution.py:616
  725.1 13.0 %select_reduce_fusion = (f32[]{:T(128)}, f32[1024,1024]{1,0:T(8,128)}) fusion(bf16[1024,2816]{1,0:T(8,128)(2,1)} %all-gather.8.cloned.1.call-done), kind=kOutput, calls=%fused_computation.18 | convolution fusion | flops 5908725760 | bytes 9961476 | tf_op jit(solution)/shard_map/dot_general | solution.py:54
  738.9 7.3 add_convert_fusion.1
  762.7 7.0 fusion.9
  769.7 6.2 all-to-all-start.7
  776.0 5.4 fusion.67
  785.3 22.7 %all-to-all-done.7 = bf16[8,32,2816]{2,1,0:T(8,128)(2,1)S(1)} async-done(((bf16[8,32,2816]{2,1,0:T(8,128)(2,1)}), bf16[8,32,2816]{2,1,0:T(8,128)(2,1)S(1)}, u32[]{:S(2)}, u32[]{:S(2)}) %all-to-all-start.7) | async-done | bytes 1441824 | tf_op jit(solution)/shard_map/all_to_all | solution.py:841
  (342 shorter events, 283.9 us)
Async XLA Ops:
  7.2 87.2 %all-gather.4.cloned.1.call-start = ((), (), s32[]{:S(2)}) async-start(), calls=%async_computation.10 | async-start | bytes 9732096 | tf_op jit(solution)/shard_map/all_gather | solution.py:699
  11.8 251.4 %all-gather.6.cloned.1.call-start = ((), (), s32[]{:S(2)}) async-start(), calls=%async_computation.11 | async-start | bytes 21086208 | tf_op jit(solution)/shard_map/all_gather | solution.py:701
  133.9 23.0 %collective-permute-start.1 = (bf16[6,128,256]{2,1,0:T(8,128)(2,1)S(1)}, bf16[6,128,256]{2,1,0:T(8,128)(2,1)S(1)}, u32[]{:S(2)}, u32[]{:S(2)}) collective-permute-start(bf16[6,128,256]{2,1,0:T(8,128)(2,1)S(1)} %slice.424), channel_id=1, source_target_pairs={{0,1},{1,2},{2,3},{3,4},{4,5},{5,6},{6,7},{8,9},{9,10},{10,11},{11... | collective-permute-start | bytes 1179656 | tf_op jit(solution)/shard_map/ppermute | solution.py:42
  137.3 26.4 %collective-permute-start.2 = (bf16[6,128,128]{2,1,0:T(8,128)(2,1)S(1)}, bf16[6,128,128]{2,1,0:T(8,128)(2,1)S(1)}, u32[]{:S(2)}, u32[]{:S(2)}) collective-permute-start(bf16[6,128,128]{2,1,0:T(8,128)(2,1)S(1)} %slice.425), channel_id=1, source_target_pairs={{0,1},{1,2},{2,3},{3,4},{4,5},{5,6},{6,7},{8,9},{9,10},{10,11},{11... | collective-permute-start | bytes 589832 | tf_op jit(solution)/shard_map/ppermute | solution.py:42
  158.6 12.7 %collective-permute-start.3 = (bf16[6,128,256]{2,1,0:T(8,128)(2,1)S(1)}, bf16[6,128,256]{2,1,0:T(8,128)(2,1)S(1)}, u32[]{:S(2)}, u32[]{:S(2)}) collective-permute-start(bf16[6,128,256]{2,1,0:T(8,128)(2,1)S(1)} %get-tuple-element.142), channel_id=1, source_target_pairs={{0,2},{1,3},{2,4},{3,5},{4,6},{5,7},{8,10},{9,11},{10,12},{11,13},... | collective-permute-start | bytes 1179656 | tf_op jit(solution)/shard_map/ppermute | solution.py:42
  164.9 19.5 %collective-permute-start.5 = (bf16[6,128,128]{2,1,0:T(8,128)(2,1)S(1)}, bf16[6,128,128]{2,1,0:T(8,128)(2,1)S(1)}, u32[]{:S(2)}, u32[]{:S(2)}) collective-permute-start(bf16[6,128,128]{2,1,0:T(8,128)(2,1)S(1)} %get-tuple-element.140), channel_id=1, source_target_pairs={{0,2},{1,3},{2,4},{3,5},{4,6},{5,7},{8,10},{9,11},{10,12},{11,13},... | collective-permute-start | bytes 589832 | tf_op jit(solution)/shard_map/ppermute | solution.py:42
  171.8 51.1 %collective-permute-start.4 = (bf16[6,128,256]{2,1,0:T(8,128)(2,1)S(1)}, bf16[6,128,256]{2,1,0:T(8,128)(2,1)S(1)}, u32[]{:S(2)}, u32[]{:S(2)}) collective-permute-start(bf16[6,128,256]{2,1,0:T(8,128)(2,1)S(1)} %fusion.59), channel_id=1, source_target_pairs={{0,1},{1,2},{2,3},{3,4},{4,5},{5,6},{6,7},{8,9},{9,10},{10,11},{11... | collective-permute-start | bytes 1179656 | tf_op jit(solution)/shard_map/ppermute | solution.py:42
  181.5 44.7 %collective-permute-start.7 = (bf16[6,128,256]{2,1,0:T(8,128)(2,1)S(1)}, bf16[6,128,256]{2,1,0:T(8,128)(2,1)S(1)}, u32[]{:S(2)}, u32[]{:S(2)}) collective-permute-start(bf16[6,128,256]{2,1,0:T(8,128)(2,1)S(1)} %fusion.59), channel_id=1, source_target_pairs={{0,5},{1,6},{2,7},{8,13},{9,14},{10,15},{16,21},{17,22},{18,23},{2... | collective-permute-start | bytes 1179656 | tf_op jit(solution)/shard_map/ppermute | solution.py:42
  184.8 38.1 %collective-permute-start.6 = (bf16[6,128,128]{2,1,0:T(8,128)(2,1)S(1)}, bf16[6,128,128]{2,1,0:T(8,128)(2,1)S(1)}, u32[]{:S(2)}, u32[]{:S(2)}) collective-permute-start(bf16[6,128,128]{2,1,0:T(8,128)(2,1)S(1)} %convolution_convert_fusion.1), channel_id=1, source_target_pairs={{0,1},{1,2},{2,3},{3,4},{4,5},{5,6},{6,7},{8,9},{9,10},{10,11},{11... | collective-permute-start | bytes 589832 | tf_op jit(solution)/shard_map/ppermute | solution.py:42
  307.0 13.9 %collective-permute-start.8 = (bf16[6,128,256]{2,1,0:T(8,128)(2,1)S(1)}, bf16[6,128,256]{2,1,0:T(8,128)(2,1)S(1)}, u32[]{:S(2)}, u32[]{:S(2)}) collective-permute-start(bf16[6,128,256]{2,1,0:T(8,128)(2,1)S(1)} %convert_element_type.360), channel_id=1, source_target_pairs={{1,0},{2,1},{3,2},{4,3},{5,4},{6,5},{7,6},{9,8},{10,9},{11,10},{12... | collective-permute-start | bytes 1179656 | tf_op jit(solution)/shard_map/ppermute | solution.py:42
  313.2 19.9 %collective-permute-start.9 = (bf16[6,128,128]{1,2,0:T(8,128)(2,1)}, bf16[6,128,128]{1,2,0:T(8,128)(2,1)}, u32[]{:S(2)}, u32[]{:S(2)}) collective-permute-start(bf16[6,128,128]{1,2,0:T(8,128)(2,1)} %slice_bitcast_fusion), channel_id=1, source_target_pairs={{1,0},{2,1},{3,2},{4,3},{5,4},{6,5},{7,6},{9,8},{10,9},{11,10},{12... | collective-permute-start | bytes 589832 | tf_op jit(solution)/shard_map/ppermute | solution.py:42
  323.5 13.2 %collective-permute-start.10 = (bf16[6,128,256]{2,1,0:T(8,128)(2,1)}, bf16[6,128,256]{2,1,0:T(8,128)(2,1)}, u32[]{:S(2)}, u32[]{:S(2)}) collective-permute-start(bf16[6,128,256]{2,1,0:T(8,128)(2,1)} %get-tuple-element.149), channel_id=1, source_target_pairs={{2,0},{3,1},{4,2},{5,3},{6,4},{7,5},{10,8},{11,9},{12,10},{13,11},... | collective-permute-start | bytes 1179656 | tf_op jit(solution)/shard_map/ppermute | solution.py:42
  328.1 84.7 %all-to-all-start = ((bf16[4,128,2048]{2,1,0:T(8,128)(2,1)}), bf16[4,128,2048]{2,1,0:T(8,128)(2,1)}, u32[]{:S(2)}, u32[]{:S(2)}) async-start(bf16[4,128,2048]{2,1,0:T(8,128)(2,1)} %broadcast_in_dim.25), calls=%async_computation | async-start | bytes 4194304 | tf_op jit(solution)/shard_map/all_to_all | solution.py:557
  338.4 40.1 %collective-permute-start.11 = (bf16[6,128,256]{2,1,0:T(8,128)(2,1)S(1)}, bf16[6,128,256]{2,1,0:T(8,128)(2,1)S(1)}, u32[]{:S(2)}, u32[]{:S(2)}) collective-permute-start(bf16[6,128,256]{2,1,0:T(8,128)(2,1)S(1)} %fusion.60), channel_id=1, source_target_pairs={{1,0},{2,1},{3,2},{4,3},{5,4},{6,5},{7,6},{9,8},{10,9},{11,10},{12... | collective-permute-start | bytes 1179656 | tf_op jit(solution)/shard_map/ppermute | solution.py:42
  342.4 36.1 %collective-permute-start.14 = (bf16[6,128,256]{2,1,0:T(8,128)(2,1)S(1)}, bf16[6,128,256]{2,1,0:T(8,128)(2,1)S(1)}, u32[]{:S(2)}, u32[]{:S(2)}) collective-permute-start(bf16[6,128,256]{2,1,0:T(8,128)(2,1)S(1)} %fusion.60), channel_id=1, source_target_pairs={{5,0},{6,1},{7,2},{13,8},{14,9},{15,10},{21,16},{22,17},{23,18},{2... | collective-permute-start | bytes 1179656 | tf_op jit(solution)/shard_map/ppermute | solution.py:42
  344.1 34.4 %collective-permute-start.13 = (bf16[6,128,128]{2,1,0:T(8,128)(2,1)S(1)}, bf16[6,128,128]{2,1,0:T(8,128)(2,1)S(1)}, u32[]{:S(2)}, u32[]{:S(2)}) collective-permute-start(bf16[6,128,128]{2,1,0:T(8,128)(2,1)S(1)} %convolution_convert_fusion), channel_id=1, source_target_pairs={{1,0},{2,1},{3,2},{4,3},{5,4},{6,5},{7,6},{9,8},{10,9},{11,10},{12... | collective-permute-start | bytes 589832 | tf_op jit(solution)/shard_map/ppermute | solution.py:42
  414.3 30.7 %all-to-all-start.3 = ((bf16[4,128,2048]{2,1,0:T(8,128)(2,1)}), bf16[4,128,2048]{2,1,0:T(8,128)(2,1)S(1)}, u32[]{:S(2)}, u32[]{:S(2)}) async-start(bf16[4,128,2048]{2,1,0:T(8,128)(2,1)} %broadcast_in_dim.26), calls=%async_computation.3 | async-start | bytes 4194304 | tf_op jit(solution)/shard_map/all_to_all | solution.py:557
  422.7 18.9 %collective-permute-start.15 = (bf16[3,3072]{1,0:T(4,128)(2,1)S(1)}, bf16[3,3072]{1,0:T(4,128)(2,1)S(1)}, u32[]{:S(2)}, u32[]{:S(2)}) collective-permute-start(bf16[3,3072]{1,0:T(4,128)(2,1)S(1)} %slice.260), channel_id=1, source_target_pairs={{1,0},{2,1},{3,2},{4,3},{5,4},{6,5},{7,6},{9,8},{10,9},{11,10},{12... | collective-permute-start | bytes 55304 | tf_op jit(solution)/shard_map/ppermute | solution.py:42
  425.7 44.3 %collective-permute-start.16 = (bf16[512,2048]{1,0:T(8,128)(2,1)}, bf16[512,2048]{1,0:T(8,128)(2,1)}, u32[]{:S(2)}, u32[]{:S(2)}) collective-permute-start(bf16[512,2048]{1,0:T(8,128)(2,1)} %bitcast.8), channel_id=1, source_target_pairs={{0,8},{8,0},{1,9},{9,1},{2,10},{10,2},{3,11},{11,3},{4,12},{12,4},... | collective-permute-start | bytes 6291464 | tf_op jit(solution)/shard_map/ppermute | solution.py:565
  445.0 20.5 %all-to-all-start.1 = ((bf16[8,128,576]{1,2,0:T(8,128)(2,1)}), bf16[8,128,576]{1,2,0:T(8,128)(2,1)}, u32[]{:S(2)}, u32[]{:S(2)}) async-start(bf16[8,128,576]{1,2,0:T(8,128)(2,1)} %bitcast.205), calls=%async_computation.1 | async-start | bytes 2359296 | tf_op jit(solution)/shard_map/all_to_all | solution.py:770
  465.5 35.4 %all-to-all-start.4 = ((bf16[8,128,1248]{1,2,0:T(8,128)(2,1)}), bf16[8,128,1248]{1,2,0:T(8,128)(2,1)}, u32[]{:S(2)}, u32[]{:S(2)}) async-start(bf16[8,128,1248]{1,2,0:T(8,128)(2,1)} %pad_maximum_fusion), calls=%async_computation.4 | async-start | bytes 5111808 | tf_op jit(solution)/shard_map/all_to_all | solution.py:752
  472.5 65.9 %collective-permute-start.20 = (bf16[512,2048]{1,0:T(8,128)(2,1)S(1)}, bf16[512,2048]{1,0:T(8,128)(2,1)}, u32[]{:S(2)}, u32[]{:S(2)}) collective-permute-start(bf16[512,2048]{1,0:T(8,128)(2,1)S(1)} %bitcast.198), channel_id=1, source_target_pairs={{0,8},{8,0},{1,9},{9,1},{2,10},{10,2},{3,11},{11,3},{4,12},{12,4},... | collective-permute-start | bytes 6291464 | tf_op jit(solution)/shard_map/ppermute | solution.py:565
  484.1 24.9 %collective-permute-start.19 = (bf16[256,576]{1,0:T(8,128)(2,1)}, bf16[256,576]{1,0:T(8,128)(2,1)}, u32[]{:S(2)}, u32[]{:S(2)}) collective-permute-start(bf16[256,576]{1,0:T(8,128)(2,1)} %get-tuple-element.117), channel_id=1, source_target_pairs={{0,6},{2,0},{4,2},{6,4},{1,7},{3,1},{5,3},{7,5},{8,14},{10,8},{12,... | collective-permute-start | bytes 884744 | tf_op jit(solution)/shard_map/ppermute | solution.py:583
  484.1 24.9 %collective-permute-start.18 = (bf16[256,576]{1,0:T(8,128)(2,1)}, bf16[256,576]{1,0:T(8,128)(2,1)}, u32[]{:S(2)}, u32[]{:S(2)}) collective-permute-start(bf16[256,576]{1,0:T(8,128)(2,1)} %get-tuple-element.118), channel_id=1, source_target_pairs={{0,4},{2,6},{4,0},{6,2},{1,5},{3,7},{5,1},{7,3},{8,12},{10,14},{12... | collective-permute-start | bytes 884744 | tf_op jit(solution)/shard_map/ppermute | solution.py:583
  484.1 28.6 %collective-permute-start.17 = (bf16[256,576]{1,0:T(8,128)(2,1)}, bf16[256,576]{1,0:T(8,128)(2,1)}, u32[]{:S(2)}, u32[]{:S(2)}) collective-permute-start(bf16[256,576]{1,0:T(8,128)(2,1)} %get-tuple-element.116), channel_id=1, source_target_pairs={{0,2},{2,4},{4,6},{6,0},{1,3},{3,5},{5,7},{7,1},{8,10},{10,12},{12... | collective-permute-start | bytes 884744 | tf_op jit(solution)/shard_map/ppermute | solution.py:583
  554.9 19.9 %collective-permute-start.23 = (bf16[256,1248]{0,1:T(8,128)(2,1)}, bf16[256,1248]{0,1:T(8,128)(2,1)S(1)}, u32[]{:S(2)}, u32[]{:S(2)}) collective-permute-start(bf16[256,1248]{0,1:T(8,128)(2,1)} %bitcast.213), channel_id=1, source_target_pairs={{0,6},{2,0},{4,2},{6,4},{1,7},{3,1},{5,3},{7,5},{8,14},{10,8},{12,... | collective-permute-start | bytes 1916936 | tf_op jit(solution)/shard_map/ppermute | solution.py:583
  560.2 40.5 %collective-permute-start.22 = (bf16[256,1248]{0,1:T(8,128)(2,1)}, bf16[256,1248]{0,1:T(8,128)(2,1)}, u32[]{:S(2)}, u32[]{:S(2)}) collective-permute-start(bf16[256,1248]{0,1:T(8,128)(2,1)} %bitcast.214), channel_id=1, source_target_pairs={{0,4},{2,6},{4,0},{6,2},{1,5},{3,7},{5,1},{7,3},{8,12},{10,14},{12... | collective-permute-start | bytes 1916936 | tf_op jit(solution)/shard_map/ppermute | solution.py:583
  561.3 53.0 %collective-permute-start.21 = (bf16[256,1248]{0,1:T(8,128)(2,1)}, bf16[256,1248]{0,1:T(8,128)(2,1)}, u32[]{:S(2)}, u32[]{:S(2)}) collective-permute-start(bf16[256,1248]{0,1:T(8,128)(2,1)} %bitcast.32), channel_id=1, source_target_pairs={{0,2},{2,4},{4,6},{6,0},{1,3},{3,5},{5,7},{7,1},{8,10},{10,12},{12... | collective-permute-start | bytes 1916936 | tf_op jit(solution)/shard_map/ppermute | solution.py:583
  617.9 14.1 %all-to-all-start.5 = ((bf16[8,32,1248]{2,1,0:T(8,128)(2,1)}), bf16[8,32,1248]{2,1,0:T(8,128)(2,1)S(1)}, u32[]{:S(2)}, u32[]{:S(2)}) async-start(bf16[8,32,1248]{2,1,0:T(8,128)(2,1)} %bitcast.35), calls=%async_computation.5 | async-start | bytes 1310720 | tf_op jit(solution)/shard_map/all_to_all | solution.py:586
  621.5 103.6 %all-gather.8.cloned.1.call-start = ((), (), s32[]{:S(2)}) async-start(), calls=%async_computation.12 | async-start | bytes 7208960 | tf_op jit(solution)/shard_map/all_gather | solution.py:616
  707.2 62.5 %all-to-all-start.9 = ((f32[32,1,896]{2,1,0:T(1,128)}), f32[32,1,896]{2,1,0:T(1,128)}, u32[]{:S(2)}, u32[]{:S(2)}) async-start(f32[32,1,896]{2,1,0:T(1,128)} %broadcast_in_dim.28), calls=%async_computation.9 | async-start | bytes 229376 | tf_op jit(solution)/shard_map/all_to_all | solution.py:606
  769.7 38.3 %all-to-all-start.7 = ((bf16[8,32,2816]{2,1,0:T(8,128)(2,1)}), bf16[8,32,2816]{2,1,0:T(8,128)(2,1)S(1)}, u32[]{:S(2)}, u32[]{:S(2)}) async-start(bf16[8,32,2816]{2,1,0:T(8,128)(2,1)} %bitcast.211), calls=%async_computation.7 | async-start | bytes 2883584 | tf_op jit(solution)/shard_map/all_to_all | solution.py:841
  (74 other events, 1036.0 us)
Sparse Core Ops, SparseCore 0:
  11.9 82.4 all-gather.3
  97.5 165.6 all-gather.5
  680.9 44.1 all-gather.7

commit v3 on v2

--- a/solution.py
+++ b/solution.py
@@ -614,7 +614,7 @@
 def orthogonal_rows(raw_rows):
     low = jnp.bfloat16
     raw = lax.all_gather(raw_rows, DP_AXES, axis=0, tiled=True)
-    gram_raw = times_transposed(raw, raw)
+    gram_raw = lax.optimization_barrier(times_transposed(raw, raw))
     norm = jnp.sqrt(jnp.trace(gram_raw))
     scale = 1.0 / (norm + eps_muon)
     gram = gram_raw * (scale * scale)
@@ -709,6 +709,16 @@
     upstream_full = upstream[0]
     upstream_low = upstream_full.astype(low)
     early_left = gathered_near(jnp.concatenate([normed_one_low, upstream_low], axis=1))
+    rim_pad = 16 - rim_rows
+    prior_normed = passed_along(normed_one_low[normed_one_low.shape[0] - rim_rows :], CTX_AXES, 1)
+    rim_left = gathered_near(jnp.pad(prior_normed, ((0, rim_pad), (0, 0))))
+    front_left = jnp.concatenate(
+        [
+            early_left[:, :D].reshape(near_count, -1, D),
+            rim_left.reshape(near_count, rim_rows + rim_pad, D),
+        ],
+        axis=1,
+    ).reshape(-1, D)
     projected = matmul(normed_one_low, front_full)
     pre_proj = projected[:, :QKV]
     route_pre = matmul(normed_one_low, route_low)
@@ -766,9 +776,23 @@
     grad_pre = jnp.concatenate([grad_pre[:split_row], grad_pre[split_row:] + back_rim], axis=0)
     grad_front_low = jnp.concatenate([grad_pre.astype(low), grad_gate_pre_low], axis=1)
     grad_route_low = grad_route_pre.astype(low)
+    front_parts = jnp.concatenate(
+        [
+            jnp.concatenate(
+                [
+                    grad_extended[rim_rows:],
+                    grad_extended[:rim_rows],
+                    jnp.zeros((rim_pad, QKV), jnp.float32),
+                ],
+                axis=0,
+            ).astype(low),
+            jnp.pad(grad_gate_pre_low, ((0, rim_rows + rim_pad), (0, 0))),
+        ],
+        axis=1,
+    )
 
     front_columns = lax.all_to_all(
-        swap_columns(grad_front_low, near_count),
+        swap_columns(front_parts, near_count),
         NEAR_AXES,
         split_axis=0,
         concat_axis=0,
@@ -791,7 +815,7 @@
     back_blocks = summed_rows(back_terms, sum(widths))
     front_width = grad_front_low.shape[1] // near_count
     front_terms = transposed_times(
-        early_left[:, :D], front_columns.reshape(count_rows, front_width)
+        front_left, front_columns.reshape(front_left.shape[0], front_width)
     ).astype(low)
     front_blocks = summed_rows(front_terms, front_width)
     front_grads = joined_columns(front_blocks)

time: 832 us -> 816 us (0.981)
  waiting for transfers between devices: 348 us -> 332 us
    ppermute x16 -> x17, waiting for transfers between devices: 108 us -> 106 us  [passed_along(): lax.ppermute(value, axis, [(source, source + steps) for source in range(f...]
    ppermute x16 -> x17, starting transfers between devices: 53.7 us -> 51.9 us  [passed_along(): lax.ppermute(value, axis, [(source, source + steps) for source in range(f...]
  transfers between devices with their start and end apart: 36 -> 39, of which waited for: 23 -> 21; matrix products, arithmetic and copies ran while one was open for 21% -> 25% of each run, Pallas kernels for 7% -> 9%
where the time goes in v3:
time: 816 us; the launch traced here: 803 us
  waiting for transfers between devices  332 us (41%)
  matrix products  109 us (13%)
  starting transfers between devices  103 us (13%)
  Pallas kernels  72.7 us (9%)
  local copies, waits for them, and re-layouts  69.7 us (9%)
  other arithmetic  58 us (7%)
  blocking collectives  41.5 us (5%)
  between operations  16.3 us (2%)
    ppermute x17, waiting for transfers between devices, passed_along(): lax.ppermute(value, axis, [(source, source + steps) for source in range(f...  106 us
    all_gather x1, waiting for transfers between devices, local(): front_full = lax.all_gather(front_rows, ALL_AXES, axis=0, tiled=True)  80.6 us
    ppermute x6, waiting for transfers between devices, summed_rows(): arrived = lax.ppermute(leaving, 'z', pairs)  54.7 us
    ppermute x17, starting transfers between devices, passed_along(): lax.ppermute(value, axis, [(source, source + steps) for source in range(f...  51.9 us
    all_to_all x1, blocking collectives, local(): lax.all_to_all(outgoing, CTX_AXES, split_axis=0, concat_axis=0, tiled=True)  41.5 us
    dot_general x6, matrix products, times_transposed(): lax.dot_general(left, right, (((1,), (1,)), ((), ())), preferred_element_...  35.8 us
    dot_general x9, matrix products, square_times(): return jnp.dot(left, right, preferred_element_type=jnp.float32)  30.2 us
    pallas_call x1, Pallas kernels, run_backward(): per_head(backward_kernel, [columns_of(rows, rows), matrix_of(DK, DV), nar...  24.8 us
  transfers between devices with their start and end apart: 39, of which 21 were waited for; matrix products, arithmetic and copies ran while one was open for 25% of the time, Pallas kernels for 9%

profile of v3, /device:TPU:8, one launch (start us, length us, event | category | flops | bytes accessed | tf_op | source)
XLA Modules:
  0.0 802.9 jit_solution(13687418757435951419)
XLA Ops:
  13.9 80.6 %all-gather.4.cloned.1.call-done = bf16[1024,4608]{1,0:T(8,128)(2,1)} async-done(((bf16[32,4608]{1,0:T(8,128)(2,1)}), bf16[1024,4608]{1,0:T(8,128)(2,1)}) %all-gather.4.cloned.1.call-update) | async-done | bytes 9437200 | tf_op jit(solution)/shard_map/all_gather | solution.py:699
  96.7 5.2 fusion.160.gate_ref
  111.7 21.8 %shard_map.427 = (f32[128,768]{1,0:T(8,128)}, f32[128,2304]{1,0:T(8,128)}, f32[6,128,384]{2,1,0:T(8,128)}) custom-call(f32[128,3072]{1,0:T(8,128)} %get-tuple-element.92.query_ref.key_ref.value_ref, f32[128,3072]{1,0:T(8,128)} %get-tuple-element.92.query_ref.key_ref.value_ref, f32[128,3072]{1,0:T(8,128)} %get-tuple-element.92.query_ref.key_ref.value_ref, ...), custom_call_target="tpu_custom_call" | custom-call | tf_op jit(solution)/shard_map/pallas_call | solution.py:426
  141.5 15.0 %collective-permute-done.17 = bf16[3,1024]{1,0:T(4,128)(2,1)S(1)} collective-permute-done((bf16[3,1024]{1,0:T(4,128)(2,1)S(1)}, bf16[3,1024]{1,0:T(4,128)(2,1)S(1)}, u32[]{:S(2)}, u32[]{:S(2)}) %collective-permute-start.17) | collective-permute-done | bytes 6176 | tf_op jit(solution)/shard_map/ppermute | solution.py:42
  181.4 8.4 %collective-permute-done.3 = bf16[6,128,256]{2,1,0:T(8,128)(2,1)} collective-permute-done((bf16[6,128,256]{2,1,0:T(8,128)(2,1)}, bf16[6,128,256]{2,1,0:T(8,128)(2,1)}, u32[]{:S(2)}, u32[]{:S(2)}) %collective-permute-start.3) | collective-permute-done | bytes 393248 | tf_op jit(solution)/shard_map/ppermute | solution.py:42
  198.9 15.8 %collective-permute-done.5 = bf16[6,128,128]{2,1,0:T(8,128)(2,1)S(1)} collective-permute-done((bf16[6,128,128]{2,1,0:T(8,128)(2,1)S(1)}, bf16[6,128,128]{2,1,0:T(8,128)(2,1)S(1)}, u32[]{:S(2)}, u32[]{:S(2)}) %collective-permute-start.5) | collective-permute-done | bytes 196640 | tf_op jit(solution)/shard_map/ppermute | solution.py:42
  217.6 5.1 collective-permute-start.9
  222.7 26.4 %collective-permute-done.6 = bf16[6,128,128]{2,1,0:T(8,128)(2,1)S(1)} collective-permute-done((bf16[6,128,128]{2,1,0:T(8,128)(2,1)S(1)}, bf16[6,128,128]{2,1,0:T(8,128)(2,1)S(1)}, u32[]{:S(2)}, u32[]{:S(2)}) %collective-permute-start.6) | collective-permute-done | bytes 196640 | tf_op jit(solution)/shard_map/ppermute | solution.py:42
  250.3 10.4 %shard_map.428 = bf16[128,1536]{1,0:T(8,128)(2,1)} custom-call(f32[128,3072]{1,0:T(8,128)} %get-tuple-element.92.query_ref.key_ref.value_ref, f32[128,3072]{1,0:T(8,128)} %get-tuple-element.92.query_ref.key_ref.value_ref, f32[128,12]{1,0:T(8,128)} %pad_maximum_fusion.17.rates_ref, f32[128,2304]{1,0:T(8,128)} %get-tuple-element.42.both_ref, ...), custom_call_target="tpu_custom_call" | custom-call | tf_op jit(solution)/shard_map/pallas_call | solution.py:457
  260.7 22.2 %all-gather.6.cloned.1.call-done = bf16[1024,9984]{1,0:T(8,128)(2,1)} async-done(((bf16[32,9984]{1,0:T(8,128)(2,1)}), bf16[1024,9984]{1,0:T(8,128)(2,1)}) %all-gather.6.cloned.1.call-update) | async-done | bytes 20447248 | tf_op jit(solution)/shard_map/all_gather | solution.py:701
  286.3 5.4 fusion.2
  296.7 7.9 multiply_reduce_fusion.4
  309.7 15.7 %shard_map.429 = f32[6,128,256]{2,1,0:T(8,128)} custom-call(f32[128,3072]{1,0:T(8,128)} %get-tuple-element.92.query_ref.key_ref.value_ref, f32[128,3072]{1,0:T(8,128)} %get-tuple-element.92.query_ref.key_ref.value_ref, f32[128,12]{1,0:T(8,128)} %pad_maximum_fusion.17.rates_ref, f32[128,2304]{1,0:T(8,128)} %get-tuple-element.42.both_ref, ...), custom_call_target="tpu_custom_call" | custom-call | tf_op jit(solution)/shard_map/pallas_call | solution.py:467
  332.9 7.0 collective-permute-done.8
  366.7 30.4 %collective-permute-done.11 = bf16[6,128,256]{2,1,0:T(8,128)(2,1)} collective-permute-done((bf16[6,128,256]{2,1,0:T(8,128)(2,1)}, bf16[6,128,256]{2,1,0:T(8,128)(2,1)}, u32[]{:S(2)}, u32[]{:S(2)}) %collective-permute-start.11) | collective-permute-done | bytes 393248 | tf_op jit(solution)/shard_map/ppermute | solution.py:42
  399.5 24.8 %shard_map.430 = (f32[128,768]{1,0:T(8,128)}, f32[128,768]{1,0:T(8,128)}, f32[128,1536]{1,0:T(8,128)}, f32[128,12]{1,0:T(8,128)}, bf16[128,1536]{1,0:T(8,128)(2,1)}, /*index=5*/f32[6,1,256]{2,1,0:T(1,128)}) custom-call(f32[128,768]{1,0:T(8,128)} %get-tuple-element.45.inverse_ref, f32[6,128,256]{2,1,0:T(8,128)} %convert_add_fusion.2.state_ref, ...), custom_call_target="tpu_custom_call" | custom-call | tf_op jit(solution)/shard_map/pallas_call | solution.py:478
  446.7 17.8 %all-to-all-done.5 = bf16[8,128,1248]{1,2,0:T(8,128)(2,1)} async-done(((bf16[8,128,1248]{1,2,0:T(8,128)(2,1)}), bf16[8,128,1248]{1,2,0:T(8,128)(2,1)}, u32[]{:S(2)}, u32[]{:S(2)}) %all-to-all-start.5) | async-done | bytes 2555936 | tf_op jit(solution)/shard_map/all_to_all | solution.py:762
  500.9 18.0 %collective-permute-done.21 = bf16[256,576]{1,0:T(8,128)(2,1)} collective-permute-done((bf16[256,576]{1,0:T(8,128)(2,1)}, bf16[256,576]{1,0:T(8,128)(2,1)}, u32[]{:S(2)}, u32[]{:S(2)}) %collective-permute-start.21) | collective-permute-done | bytes 294944 | tf_op jit(solution)/shard_map/ppermute | solution.py:583
  556.6 21.6 %collective-permute-done.24 = bf16[256,1248]{0,1:T(8,128)(2,1)} collective-permute-done((bf16[256,1248]{0,1:T(8,128)(2,1)}, bf16[256,1248]{0,1:T(8,128)(2,1)}, u32[]{:S(2)}, u32[]{:S(2)}) %collective-permute-start.24) | collective-permute-done | bytes 639008 | tf_op jit(solution)/shard_map/ppermute | solution.py:583
  580.4 11.5 %collective-permute-done.23 = bf16[256,1248]{0,1:T(8,128)(2,1)} collective-permute-done((bf16[256,1248]{0,1:T(8,128)(2,1)}, bf16[256,1248]{0,1:T(8,128)(2,1)}, u32[]{:S(2)}, u32[]{:S(2)}) %collective-permute-start.23) | collective-permute-done | bytes 639008 | tf_op jit(solution)/shard_map/ppermute | solution.py:583
  603.0 8.0 all-to-all-done.6
  622.2 41.5 %all_to_all.60 = bf16[8,32,2816]{2,1,0:T(8,128)(2,1)} all-to-all(bf16[8,32,2816]{2,1,0:T(8,128)(2,1)} %bitcast_dynamic-update-slice_fusion), channel_id=1, replica_groups=mesh['y'=2,'core'=2,'z'=4,'x'=2] {'z','x'}, dimensions={0} | all-to-all | bytes 2883584 | tf_op jit(solution)/shard_map/all_to_all | solution.py:863
  670.6 7.9 fusion.73
  678.9 5.0 concatenate.77
  687.7 6.7 all-to-all-done.9
  699.4 8.6 %all-gather.8.cloned.1.call-done = bf16[1024,2816]{1,0:T(8,128)(2,1)} async-done(((bf16[256,2816]{1,0:T(8,128)(2,1)}), bf16[1024,2816]{1,0:T(8,128)(2,1)}) %all-gather.8.cloned.1.call-update) | async-done | bytes 5767184 | tf_op jit(solution)/shard_map/all_gather | solution.py:616
  708.0 11.0 %fusion.161 = f32[1024,1024]{1,0:T(8,128)S(1)} fusion(bf16[1024,2816]{1,0:T(8,128)(2,1)} %all-gather.8.cloned.1.call-done), kind=kOutput, calls=%fused_computation.288 | convolution fusion | flops 5905580032 | bytes 9961472 | tf_op jit(solution)/shard_map/dot_general | solution.py:54
  722.6 7.3 add_convert_fusion.1
  746.4 6.9 fusion.9
  753.3 6.2 all-to-all-start.8
  759.6 5.5 fusion.70
  768.9 22.7 %all-to-all-done.8 = bf16[8,32,2816]{2,1,0:T(8,128)(2,1)S(1)} async-done(((bf16[8,32,2816]{2,1,0:T(8,128)(2,1)}), bf16[8,32,2816]{2,1,0:T(8,128)(2,1)S(1)}, u32[]{:S(2)}, u32[]{:S(2)}) %all-to-all-start.8) | async-done | bytes 1441824 | tf_op jit(solution)/shard_map/all_to_all | solution.py:865
  (400 shorter events, 278.4 us)
Async XLA Ops:
  7.2 87.2 %all-gather.4.cloned.1.call-start = ((), (), s32[]{:S(2)}) async-start(), calls=%async_computation.11 | async-start | bytes 9732096 | tf_op jit(solution)/shard_map/all_gather | solution.py:699
  11.8 271.1 %all-gather.6.cloned.1.call-start = ((), (), s32[]{:S(2)}) async-start(), calls=%async_computation.12 | async-start | bytes 21086208 | tf_op jit(solution)/shard_map/all_gather | solution.py:701
  134.8 30.3 %collective-permute-start.1 = (bf16[6,128,256]{2,1,0:T(8,128)(2,1)S(1)}, bf16[6,128,256]{2,1,0:T(8,128)(2,1)S(1)}, u32[]{:S(2)}, u32[]{:S(2)}) collective-permute-start(bf16[6,128,256]{2,1,0:T(8,128)(2,1)S(1)} %slice.430), channel_id=1, source_target_pairs={{0,1},{1,2},{2,3},{3,4},{4,5},{5,6},{6,7},{8,9},{9,10},{10,11},{11... | collective-permute-start | bytes 1179656 | tf_op jit(solution)/shard_map/ppermute | solution.py:42
  137.2 19.4 %collective-permute-start.17 = (bf16[3,1024]{1,0:T(4,128)(2,1)S(1)}, bf16[3,1024]{1,0:T(4,128)(2,1)S(1)}, u32[]{:S(2)}, u32[]{:S(2)}) collective-permute-start(bf16[3,1024]{1,0:T(4,128)(2,1)S(1)} %slice.272), channel_id=1, source_target_pairs={{0,1},{1,2},{2,3},{3,4},{4,5},{5,6},{6,7},{8,9},{9,10},{10,11},{11... | collective-permute-start | bytes 18440 | tf_op jit(solution)/shard_map/ppermute | solution.py:42
  161.2 15.5 %collective-permute-start.2 = (bf16[6,128,128]{2,1,0:T(8,128)(2,1)}, bf16[6,128,128]{2,1,0:T(8,128)(2,1)}, u32[]{:S(2)}, u32[]{:S(2)}) collective-permute-start(bf16[6,128,128]{2,1,0:T(8,128)(2,1)} %slice.431), channel_id=1, source_target_pairs={{0,1},{1,2},{2,3},{3,4},{4,5},{5,6},{6,7},{8,9},{9,10},{10,11},{11... | collective-permute-start | bytes 589832 | tf_op jit(solution)/shard_map/ppermute | solution.py:42
  166.3 23.4 %collective-permute-start.3 = (bf16[6,128,256]{2,1,0:T(8,128)(2,1)}, bf16[6,128,256]{2,1,0:T(8,128)(2,1)}, u32[]{:S(2)}, u32[]{:S(2)}) collective-permute-start(bf16[6,128,256]{2,1,0:T(8,128)(2,1)} %get-tuple-element.144), channel_id=1, source_target_pairs={{0,2},{1,3},{2,4},{3,5},{4,6},{5,7},{8,10},{9,11},{10,12},{11,13},... | collective-permute-start | bytes 1179656 | tf_op jit(solution)/shard_map/ppermute | solution.py:42
  172.0 157.4 %all-to-all-start = ((bf16[4,128,2048]{2,1,0:T(8,128)(2,1)}), bf16[4,128,2048]{2,1,0:T(8,128)(2,1)}, u32[]{:S(2)}, u32[]{:S(2)}) async-start(bf16[4,128,2048]{2,1,0:T(8,128)(2,1)} %broadcast_in_dim.29), calls=%async_computation | async-start | bytes 4194304 | tf_op jit(solution)/shard_map/all_to_all | solution.py:557
  176.6 152.0 %collective-permute-start.18 = (bf16[64,1024]{1,0:T(8,128)(2,1)S(1)}, bf16[64,1024]{1,0:T(8,128)(2,1)S(1)}, u32[]{:S(2)}, u32[]{:S(2)}) collective-permute-start(bf16[64,1024]{1,0:T(8,128)(2,1)S(1)} %bitcast.216), channel_id=1, source_target_pairs={{0,8},{8,0},{1,9},{9,1},{2,10},{10,2},{3,11},{11,3},{4,12},{12,4},... | collective-permute-start | bytes 393224 | tf_op jit(solution)/shard_map/ppermute | solution.py:565
  177.9 36.7 %collective-permute-start.5 = (bf16[6,128,128]{2,1,0:T(8,128)(2,1)S(1)}, bf16[6,128,128]{2,1,0:T(8,128)(2,1)S(1)}, u32[]{:S(2)}, u32[]{:S(2)}) collective-permute-start(bf16[6,128,128]{2,1,0:T(8,128)(2,1)S(1)} %get-tuple-element.142), channel_id=1, source_target_pairs={{0,2},{1,3},{2,4},{3,5},{4,6},{5,7},{8,10},{9,11},{10,12},{11,13},... | collective-permute-start | bytes 589832 | tf_op jit(solution)/shard_map/ppermute | solution.py:42
  191.2 57.9 %collective-permute-start.4 = (bf16[6,128,256]{2,1,0:T(8,128)(2,1)S(1)}, bf16[6,128,256]{2,1,0:T(8,128)(2,1)S(1)}, u32[]{:S(2)}, u32[]{:S(2)}) collective-permute-start(bf16[6,128,256]{2,1,0:T(8,128)(2,1)S(1)} %fusion.62), channel_id=1, source_target_pairs={{0,1},{1,2},{2,3},{3,4},{4,5},{5,6},{6,7},{8,9},{9,10},{10,11},{11... | collective-permute-start | bytes 1179656 | tf_op jit(solution)/shard_map/ppermute | solution.py:42
  193.9 55.2 %collective-permute-start.7 = (bf16[6,128,256]{2,1,0:T(8,128)(2,1)S(1)}, bf16[6,128,256]{2,1,0:T(8,128)(2,1)S(1)}, u32[]{:S(2)}, u32[]{:S(2)}) collective-permute-start(bf16[6,128,256]{2,1,0:T(8,128)(2,1)S(1)} %fusion.62), channel_id=1, source_target_pairs={{0,5},{1,6},{2,7},{8,13},{9,14},{10,15},{16,21},{17,22},{18,23},{2... | collective-permute-start | bytes 1179656 | tf_op jit(solution)/shard_map/ppermute | solution.py:42
  215.0 34.2 %collective-permute-start.6 = (bf16[6,128,128]{2,1,0:T(8,128)(2,1)S(1)}, bf16[6,128,128]{2,1,0:T(8,128)(2,1)S(1)}, u32[]{:S(2)}, u32[]{:S(2)}) collective-permute-start(bf16[6,128,128]{2,1,0:T(8,128)(2,1)S(1)} %convolution_convert_fusion.1), channel_id=1, source_target_pairs={{0,1},{1,2},{2,3},{3,4},{4,5},{5,6},{6,7},{8,9},{9,10},{10,11},{11... | collective-permute-start | bytes 589832 | tf_op jit(solution)/shard_map/ppermute | solution.py:42
  217.6 112.0 %collective-permute-start.9 = (bf16[6,128,128]{1,2,0:T(8,128)(2,1)}, bf16[6,128,128]{1,2,0:T(8,128)(2,1)}, u32[]{:S(2)}, u32[]{:S(2)}) collective-permute-start(bf16[6,128,128]{1,2,0:T(8,128)(2,1)} %slice_bitcast_fusion), channel_id=1, source_target_pairs={{1,0},{2,1},{3,2},{4,3},{5,4},{6,5},{7,6},{9,8},{10,9},{11,10},{12... | collective-permute-start | bytes 589832 | tf_op jit(solution)/shard_map/ppermute | solution.py:42
  329.3 142.5 %collective-permute-start.16 = (bf16[512,2048]{1,0:T(8,128)(2,1)}, bf16[512,2048]{1,0:T(8,128)(2,1)}, u32[]{:S(2)}, u32[]{:S(2)}) collective-permute-start(bf16[512,2048]{1,0:T(8,128)(2,1)} %bitcast.8), channel_id=1, source_target_pairs={{0,8},{8,0},{1,9},{9,1},{2,10},{10,2},{3,11},{11,3},{4,12},{12,4},... | collective-permute-start | bytes 6291464 | tf_op jit(solution)/shard_map/ppermute | solution.py:565
  345.1 21.6 %collective-permute-start.13 = (bf16[6,128,128]{2,1,0:T(8,128)(2,1)}, bf16[6,128,128]{2,1,0:T(8,128)(2,1)}, u32[]{:S(2)}, u32[]{:S(2)}) collective-permute-start(bf16[6,128,128]{2,1,0:T(8,128)(2,1)} %convolution_convert_fusion), channel_id=1, source_target_pairs={{1,0},{2,1},{3,2},{4,3},{5,4},{6,5},{7,6},{9,8},{10,9},{11,10},{12... | collective-permute-start | bytes 589832 | tf_op jit(solution)/shard_map/ppermute | solution.py:42
  351.6 77.4 %all-to-all-start.4 = ((bf16[4,128,2048]{2,1,0:T(8,128)(2,1)}), bf16[4,128,2048]{2,1,0:T(8,128)(2,1)}, u32[]{:S(2)}, u32[]{:S(2)}) async-start(bf16[4,128,2048]{2,1,0:T(8,128)(2,1)} %broadcast_in_dim.32), calls=%async_computation.4 | async-start | bytes 4194304 | tf_op jit(solution)/shard_map/all_to_all | solution.py:557
  357.5 39.7 %collective-permute-start.11 = (bf16[6,128,256]{2,1,0:T(8,128)(2,1)}, bf16[6,128,256]{2,1,0:T(8,128)(2,1)}, u32[]{:S(2)}, u32[]{:S(2)}) collective-permute-start(bf16[6,128,256]{2,1,0:T(8,128)(2,1)} %fusion.63), channel_id=1, source_target_pairs={{1,0},{2,1},{3,2},{4,3},{5,4},{6,5},{7,6},{9,8},{10,9},{11,10},{12... | collective-permute-start | bytes 1179656 | tf_op jit(solution)/shard_map/ppermute | solution.py:42
  360.0 37.2 %collective-permute-start.14 = (bf16[6,128,256]{2,1,0:T(8,128)(2,1)}, bf16[6,128,256]{2,1,0:T(8,128)(2,1)}, u32[]{:S(2)}, u32[]{:S(2)}) collective-permute-start(bf16[6,128,256]{2,1,0:T(8,128)(2,1)} %fusion.63), channel_id=1, source_target_pairs={{5,0},{6,1},{7,2},{13,8},{14,9},{15,10},{21,16},{22,17},{23,18},{2... | collective-permute-start | bytes 1179656 | tf_op jit(solution)/shard_map/ppermute | solution.py:42
  429.0 35.5 %all-to-all-start.5 = ((bf16[8,128,1248]{1,2,0:T(8,128)(2,1)}), bf16[8,128,1248]{1,2,0:T(8,128)(2,1)}, u32[]{:S(2)}, u32[]{:S(2)}) async-start(bf16[8,128,1248]{1,2,0:T(8,128)(2,1)} %pad_maximum_fusion), calls=%async_computation.5 | async-start | bytes 5111808 | tf_op jit(solution)/shard_map/all_to_all | solution.py:762
  433.5 38.4 %collective-permute-start.22 = (bf16[512,2048]{1,0:T(8,128)(2,1)}, bf16[512,2048]{1,0:T(8,128)(2,1)}, u32[]{:S(2)}, u32[]{:S(2)}) collective-permute-start(bf16[512,2048]{1,0:T(8,128)(2,1)} %bitcast.23), channel_id=1, source_target_pairs={{0,8},{8,0},{1,9},{9,1},{2,10},{10,2},{3,11},{11,3},{4,12},{12,4},... | collective-permute-start | bytes 6291464 | tf_op jit(solution)/shard_map/ppermute | solution.py:565
  464.4 23.8 %all-to-all-start.2 = ((bf16[8,144,576]{2,1,0:T(8,128)(2,1)}), bf16[8,144,576]{2,1,0:T(8,128)(2,1)}, u32[]{:S(2)}, u32[]{:S(2)}) async-start(bf16[8,144,576]{2,1,0:T(8,128)(2,1)} %bitcast.194), calls=%async_computation.2 | async-start | bytes 2949120 | tf_op jit(solution)/shard_map/all_to_all | solution.py:794
  493.9 24.9 %collective-permute-start.21 = (bf16[256,576]{1,0:T(8,128)(2,1)}, bf16[256,576]{1,0:T(8,128)(2,1)}, u32[]{:S(2)}, u32[]{:S(2)}) collective-permute-start(bf16[256,576]{1,0:T(8,128)(2,1)} %get-tuple-element.117), channel_id=1, source_target_pairs={{0,6},{2,0},{4,2},{6,4},{1,7},{3,1},{5,3},{7,5},{8,14},{10,8},{12,... | collective-permute-start | bytes 884744 | tf_op jit(solution)/shard_map/ppermute | solution.py:583
  493.9 24.9 %collective-permute-start.20 = (bf16[256,576]{1,0:T(8,128)(2,1)}, bf16[256,576]{1,0:T(8,128)(2,1)}, u32[]{:S(2)}, u32[]{:S(2)}) collective-permute-start(bf16[256,576]{1,0:T(8,128)(2,1)} %get-tuple-element.118), channel_id=1, source_target_pairs={{0,4},{2,6},{4,0},{6,2},{1,5},{3,7},{5,1},{7,3},{8,12},{10,14},{12... | collective-permute-start | bytes 884744 | tf_op jit(solution)/shard_map/ppermute | solution.py:583
  494.3 28.2 %collective-permute-start.19 = (bf16[256,576]{1,0:T(8,128)(2,1)}, bf16[256,576]{1,0:T(8,128)(2,1)}, u32[]{:S(2)}, u32[]{:S(2)}) collective-permute-start(bf16[256,576]{1,0:T(8,128)(2,1)} %get-tuple-element.116), channel_id=1, source_target_pairs={{0,2},{2,4},{4,6},{6,0},{1,3},{3,5},{5,7},{7,1},{8,10},{10,12},{12... | collective-permute-start | bytes 884744 | tf_op jit(solution)/shard_map/ppermute | solution.py:583
  524.7 17.6 %all-to-all-start.3 = ((bf16[8,32,576]{2,1,0:T(8,128)(2,1)}), bf16[8,32,576]{2,1,0:T(8,128)(2,1)}, u32[]{:S(2)}, u32[]{:S(2)}) async-start(bf16[8,32,576]{2,1,0:T(8,128)(2,1)} %bitcast.212), calls=%async_computation.3 | async-start | bytes 655360 | tf_op jit(solution)/shard_map/all_to_all | solution.py:586
  532.3 22.2 %collective-permute-start.25 = (bf16[256,1248]{0,1:T(8,128)(2,1)}, bf16[256,1248]{0,1:T(8,128)(2,1)}, u32[]{:S(2)}, u32[]{:S(2)}) collective-permute-start(bf16[256,1248]{0,1:T(8,128)(2,1)} %bitcast.213), channel_id=1, source_target_pairs={{0,6},{2,0},{4,2},{6,4},{1,7},{3,1},{5,3},{7,5},{8,14},{10,8},{12,... | collective-permute-start | bytes 1916936 | tf_op jit(solution)/shard_map/ppermute | solution.py:583
  538.7 39.5 %collective-permute-start.24 = (bf16[256,1248]{0,1:T(8,128)(2,1)}, bf16[256,1248]{0,1:T(8,128)(2,1)}, u32[]{:S(2)}, u32[]{:S(2)}) collective-permute-start(bf16[256,1248]{0,1:T(8,128)(2,1)} %bitcast.214), channel_id=1, source_target_pairs={{0,4},{2,6},{4,0},{6,2},{1,5},{3,7},{5,1},{7,3},{8,12},{10,14},{12... | collective-permute-start | bytes 1916936 | tf_op jit(solution)/shard_map/ppermute | solution.py:583
  540.8 51.0 %collective-permute-start.23 = (bf16[256,1248]{0,1:T(8,128)(2,1)}, bf16[256,1248]{0,1:T(8,128)(2,1)}, u32[]{:S(2)}, u32[]{:S(2)}) collective-permute-start(bf16[256,1248]{0,1:T(8,128)(2,1)} %bitcast.215), channel_id=1, source_target_pairs={{0,2},{2,4},{4,6},{6,0},{1,3},{3,5},{5,7},{7,1},{8,10},{10,12},{12... | collective-permute-start | bytes 1916936 | tf_op jit(solution)/shard_map/ppermute | solution.py:583
  596.7 14.4 %all-to-all-start.6 = ((bf16[8,32,1248]{2,1,0:T(8,128)(2,1)}), bf16[8,32,1248]{2,1,0:T(8,128)(2,1)S(1)}, u32[]{:S(2)}, u32[]{:S(2)}) async-start(bf16[8,32,1248]{2,1,0:T(8,128)(2,1)} %bitcast.208), calls=%async_computation.6 | async-start | bytes 1310720 | tf_op jit(solution)/shard_map/all_to_all | solution.py:586
  600.5 107.5 %all-gather.8.cloned.1.call-start = ((), (), s32[]{:S(2)}) async-start(), calls=%async_computation.13 | async-start | bytes 7208960 | tf_op jit(solution)/shard_map/all_gather | solution.py:616
  695.2 58.1 %all-to-all-start.10 = ((f32[32,1,896]{2,1,0:T(1,128)}), f32[32,1,896]{2,1,0:T(1,128)}, u32[]{:S(2)}, u32[]{:S(2)}) async-start(f32[32,1,896]{2,1,0:T(1,128)} %broadcast_in_dim.66), calls=%async_computation.10 | async-start | bytes 229376 | tf_op jit(solution)/shard_map/all_to_all | solution.py:606
  753.3 38.3 %all-to-all-start.8 = ((bf16[8,32,2816]{2,1,0:T(8,128)(2,1)}), bf16[8,32,2816]{2,1,0:T(8,128)(2,1)S(1)}, u32[]{:S(2)}, u32[]{:S(2)}) async-start(bf16[8,32,2816]{2,1,0:T(8,128)(2,1)} %bitcast.211), calls=%async_computation.8 | async-start | bytes 2883584 | tf_op jit(solution)/shard_map/all_to_all | solution.py:865
  (98 other events, 1233.4 us)
Sparse Core Ops, SparseCore 0:
  11.9 82.4 all-gather.3
  97.5 185.3 all-gather.5
  663.8 44.1 all-gather.7
